TPU v7x, 128 devices: a whole 4x4x4 slice. The times are simulated.
128 devices in a mesh: tm: 32 (over y, z, core), tmpl: 4 (over x).
Axes of the slice: x: 4, y: 4, z: 4, core: 2. Of those that a mesh axis runs over, the one named last changes fastest.
Arguments:
- waveforms: bfloat16 [2000, 131072], P(None, 'tm'), may hold values from -6 to 6
- templates: bfloat16 [64, 96, 512], P('tm', 'tmpl'), may hold values from -6 to 6
- channel_lists: int32 [64, 96], P(None, 'tmpl'), may hold values from 0 to 1999, as said below
- channel_counts: int32 [64], replicated, may hold values from 32 to 96, as said below
- owner_rounds: int32 [4], replicated, may hold values from 0 to 31
Outputs:
- detection: float32 [8, 131072], P(None, ('tm', 'tmpl'))
Inputs may be any that keep to these rules, and one draw needn't show every extreme that they name: `channel_lists`: the 96 channels of one template are distinct. `channel_counts`: slots at or past a template's count are padding; at least one template uses all 96 slots.
All inputs are finite; a program needn't handle non-finite values.
Results may differ from a plain program's by a relative error of at most 0.0003.
Values may be sent and summed in bfloat16 or wider, within the bound.
No kernel may reach another device: no remote copies, remote signals or barrier semaphores. Data moves between devices by JAX's collectives and lax.ppermute only.
A program may use at most 128 MiB of HBM per device.

v0:
```python
import math

import jax
import jax.numpy as jnp
import numpy as np
from jax import lax
from jax.sharding import PartitionSpec as P

stability_floor = 1e-06


def passed_along(array, axis, by):
    size = lax.axis_size(axis)
    pairs = [(i, i + by) for i in range(size) if 0 <= i + by < size]
    return lax.ppermute(array, axis, pairs)


def from_root(array, axis, root):
    mine = lax.axis_index(axis) == root
    return lax.psum(jnp.where(mine, array, jnp.zeros_like(array)), axis)


def shards(waveforms, templates, channel_lists, channel_counts, owner_rounds):
    shard_len = waveforms.shape[1]
    batch_size, slot_dev, tap_count = templates.shape
    stacked = batch_size * slot_dev
    round_count = owner_rounds.shape[0]
    block_len = math.gcd(math.gcd(128, tap_count), shard_len)
    block_count = shard_len // block_len
    tap_blocks = tap_count // block_len
    shift_count = tap_blocks + 1
    kernel_len = shift_count * block_len
    padded_len = tap_count + 2 * block_len
    groups = lax.axis_size("tmpl")
    group_id = lax.axis_index("tmpl")
    slot_ids = group_id * slot_dev + jnp.arange(slot_dev, dtype=jnp.int32)
    lower_triangle_table = jnp.asarray(
        np.arange(block_len)[:, None] < np.arange(block_len)[None, :], jnp.float32
    )
    heads = waveforms[:, :tap_count]
    tail_all = passed_along(heads, "tm", -1)

    def correlate(waveset, picked, tail_rows, usable):
        extended = jnp.concatenate([picked, tail_rows], axis=1)
        blocks = extended.reshape(stacked, block_count + tap_blocks, block_len)
        shifted = jnp.concatenate(
            [blocks[:, shift_id : shift_id + block_count, :] for shift_id in range(shift_count)],
            axis=2,
        )
        waves = waveset.reshape(stacked, tap_count)
        padded = jnp.pad(waves, ((0, 0), (block_len, block_len)))
        tiled = jnp.tile(padded, (1, block_len))[:, block_len:]
        toeplitz = tiled.reshape(stacked, block_len, padded_len - 1)[:, :, :kernel_len]
        correl = jnp.einsum(
            "sbk,sck->sbc", shifted, toeplitz, preferred_element_type=jnp.float32
        ).reshape(stacked, shard_len)
        squared_block_values = jnp.square(blocks.astype(jnp.float32))
        prefix = jnp.einsum(
            "naw,wc->nac",
            squared_block_values,
            lower_triangle_table,
            precision=lax.Precision.HIGHEST,
        )
        totals = jnp.sum(squared_block_values, axis=2)
        window_total = totals[:, 0:block_count]
        for offset in range(1, tap_blocks):
            window_total = window_total + totals[:, offset : offset + block_count]
        energy = (
            window_total[:, :, None]
            - prefix[:, :block_count, :]
            + prefix[:, tap_blocks : tap_blocks + block_count, :]
        )
        energy = energy.reshape(stacked, shard_len)
        wave_f = waves.astype(jnp.float32)
        template_power = jnp.sum(wave_f * wave_f, axis=1)
        normed = correl / (
            jnp.sqrt(jnp.maximum(energy, tap_count / 4.0))
            * jnp.sqrt(template_power + stability_floor)[:, None]
        )
        normed = jnp.where(usable.reshape(stacked, 1), normed, 0.0)
        return jnp.sum(normed.reshape(batch_size, slot_dev, shard_len), axis=1)

    def round_step(round_index, result_rows):
        owner_id = owner_rounds[round_index]
        first_row = owner_id * batch_size
        waveset = from_root(templates, "tm", owner_id)
        chosen = lax.dynamic_slice_in_dim(channel_lists, first_row, batch_size, 0)
        count_rows = lax.dynamic_slice_in_dim(channel_counts, first_row, batch_size, 0)
        chosen_flat = chosen.reshape(stacked)
        picked = jnp.take(waveforms, chosen_flat, axis=0)
        tail_rows = jnp.take(tail_all, chosen_flat, axis=0)
        usable = slot_ids[None, :] < count_rows[:, None]
        local_sum = correlate(waveset, picked, tail_rows, usable)
        share = lax.psum_scatter(local_sum, "tmpl", scatter_dimension=1, tiled=True)
        return lax.dynamic_update_slice_in_dim(result_rows, share, round_index * batch_size, 0)

    result_rows = jnp.zeros((round_count * batch_size, shard_len // groups), jnp.float32)
    return lax.fori_loop(0, round_count, round_step, result_rows)


def solution(mesh):
    in_specs = (P(None, "tm"), P("tm", "tmpl", None), P(None, "tmpl"), P(), P())
    out_specs = P(None, ("tm", "tmpl"))
    return jax.shard_map(shards, mesh=mesh, in_specs=in_specs, out_specs=out_specs, check_vma=False)
```

profile of v0, /device:TPU:0, one launch (start us, length us, event | category | flops | bytes accessed | tf_op | source)
XLA Modules:
  0.0 970.3 jit_solution(954034108740233425)
XLA Ops:
  6.5 1.7 slice.133
  8.3 1.3 collective-permute-start
  9.7 4.7 collective-permute-done
  14.4 948.7 %while.17 = (s32[]{:T(128)}, f32[8,1024]{1,0:T(8,128)S(1)}, s32[4]{0:T(128)S(1)}, s32[64]{0:T(128)S(1)}, s32[64,24]{1,0:T(8,128)S(1)}, /*index=5*/bf16[2000,4096...) while((s32[]{:T(128)}, f32[8,1024]{1,0:T(8,128)S(1)}, ...), condition=%wide.region_6.7_spmd.clone.clone, body=%wide.region_0.6_spmd.sunk.clone.clone.sunk | while | flops 594661696 | bytes 99252792 | solution.py:98
  16.1 8.9 gather_fusion.1
  25.0 2.5 gather_fusion
  29.2 1.0 slice_dynamic-update-slice_fusion.11
  30.1 0.9 slice_dynamic-update-slice_fusion.12
  31.0 0.9 slice_dynamic-update-slice_fusion.13
  31.9 0.9 slice_dynamic-update-slice_fusion.14
  33.5 145.6 %psum.18 = bf16[2,24,512]{2,1,0:T(8,128)(2,1)S(1)} all-reduce(bf16[2,24,512]{2,1,0:T(8,128)(2,1)S(1)} %broadcast_select_fusion.8), channel_id=1, replica_groups=mesh['tm'=32,'tmpl'=4] {'tm'}, use_global_device_ids=true, to_apply=%region_1.1 | all-reduce | flops 24576 | bytes 98304 | tf_op jit(solution)/shard_map/while/body/eval_jaxpr/psum | solution.py:20
  179.3 4.3 tile.31
  183.6 12.9 %copy.28 = bf16[6,8,128,768]{3,1,2,0:T(8,128)(2,1)} copy(bf16[6,8,128,768]{3,2,1,0:T(8,128)(2,1)} %bitcast.29) | data formatting | bytes 18874368 | tf_op jit(solution)/shard_map/while
  196.5 7.9 slice.242
  204.4 23.0 %reshape.222 = bf16[48,128,767]{2,1,0:T(8,128)(2,1)} reshape(bf16[48,98176]{1,0:T(8,128)(2,1)} %slice.242) | data formatting | bytes 18849792 | tf_op jit(solution)/shard_map/while/body/eval_jaxpr/reshape | solution.py:53
  227.4 6.6 fusion.26
  236.4 2.0 copy.31
  238.5 26.1 %reduce-scatter.6.cloned.1.call-done = f32[1024,2]{1,0:T(8,128)} async-done(((f32[4096,2]{1,0:T(8,128)}), f32[1024,2]{1,0:T(8,128)}) %reduce-scatter.6.cloned.1.call-update) | async-done | bytes 8208 | tf_op jit(solution)/shard_map/while
  264.6 1.2 copy.32
  267.4 8.9 gather_fusion.1
  276.4 2.5 gather_fusion
  280.5 1.0 slice_dynamic-update-slice_fusion.11
  281.5 0.9 slice_dynamic-update-slice_fusion.12
  282.4 0.9 slice_dynamic-update-slice_fusion.13
  283.3 0.9 slice_dynamic-update-slice_fusion.14
  284.9 128.3 %psum.18 = bf16[2,24,512]{2,1,0:T(8,128)(2,1)S(1)} all-reduce(bf16[2,24,512]{2,1,0:T(8,128)(2,1)S(1)} %broadcast_select_fusion.8), channel_id=1, replica_groups=mesh['tm'=32,'tmpl'=4] {'tm'}, use_global_device_ids=true, to_apply=%region_1.1 | all-reduce | flops 24576 | bytes 98304 | tf_op jit(solution)/shard_map/while/body/eval_jaxpr/psum | solution.py:20
  413.3 4.3 tile.31
  417.6 12.9 %copy.28 = bf16[6,8,128,768]{3,1,2,0:T(8,128)(2,1)} copy(bf16[6,8,128,768]{3,2,1,0:T(8,128)(2,1)} %bitcast.29) | data formatting | bytes 18874368 | tf_op jit(solution)/shard_map/while
  430.5 7.9 slice.242
  438.4 23.0 %reshape.222 = bf16[48,128,767]{2,1,0:T(8,128)(2,1)} reshape(bf16[48,98176]{1,0:T(8,128)(2,1)} %slice.242) | data formatting | bytes 18849792 | tf_op jit(solution)/shard_map/while/body/eval_jaxpr/reshape | solution.py:53
  461.4 6.6 fusion.26
  470.4 2.0 copy.31
  472.5 24.5 %reduce-scatter.6.cloned.1.call-done = f32[1024,2]{1,0:T(8,128)} async-done(((f32[4096,2]{1,0:T(8,128)}), f32[1024,2]{1,0:T(8,128)}) %reduce-scatter.6.cloned.1.call-update) | async-done | bytes 8208 | tf_op jit(solution)/shard_map/while
  497.0 1.2 copy.32
  499.9 8.9 gather_fusion.1
  508.8 2.5 gather_fusion
  512.9 1.0 slice_dynamic-update-slice_fusion.11
  513.9 0.9 slice_dynamic-update-slice_fusion.12
  514.8 0.9 slice_dynamic-update-slice_fusion.13
  515.7 0.9 slice_dynamic-update-slice_fusion.14
  517.3 128.3 %psum.18 = bf16[2,24,512]{2,1,0:T(8,128)(2,1)S(1)} all-reduce(bf16[2,24,512]{2,1,0:T(8,128)(2,1)S(1)} %broadcast_select_fusion.8), channel_id=1, replica_groups=mesh['tm'=32,'tmpl'=4] {'tm'}, use_global_device_ids=true, to_apply=%region_1.1 | all-reduce | flops 24576 | bytes 98304 | tf_op jit(solution)/shard_map/while/body/eval_jaxpr/psum | solution.py:20
  645.7 4.3 tile.31
  650.0 12.9 %copy.28 = bf16[6,8,128,768]{3,1,2,0:T(8,128)(2,1)} copy(bf16[6,8,128,768]{3,2,1,0:T(8,128)(2,1)} %bitcast.29) | data formatting | bytes 18874368 | tf_op jit(solution)/shard_map/while
  662.9 7.9 slice.242
  670.9 23.0 %reshape.222 = bf16[48,128,767]{2,1,0:T(8,128)(2,1)} reshape(bf16[48,98176]{1,0:T(8,128)(2,1)} %slice.242) | data formatting | bytes 18849792 | tf_op jit(solution)/shard_map/while/body/eval_jaxpr/reshape | solution.py:53
  693.9 6.6 fusion.26
  702.9 2.0 copy.31
  704.9 24.5 %reduce-scatter.6.cloned.1.call-done = f32[1024,2]{1,0:T(8,128)} async-done(((f32[4096,2]{1,0:T(8,128)}), f32[1024,2]{1,0:T(8,128)}) %reduce-scatter.6.cloned.1.call-update) | async-done | bytes 8208 | tf_op jit(solution)/shard_map/while
  729.5 1.2 copy.32
  732.3 8.9 gather_fusion.1
  741.3 2.5 gather_fusion
  745.4 1.0 slice_dynamic-update-slice_fusion.11
  746.4 0.9 slice_dynamic-update-slice_fusion.12
  747.3 0.9 slice_dynamic-update-slice_fusion.13
  748.2 0.9 slice_dynamic-update-slice_fusion.14
  749.8 128.3 %psum.18 = bf16[2,24,512]{2,1,0:T(8,128)(2,1)S(1)} all-reduce(bf16[2,24,512]{2,1,0:T(8,128)(2,1)S(1)} %broadcast_select_fusion.8), channel_id=1, replica_groups=mesh['tm'=32,'tmpl'=4] {'tm'}, use_global_device_ids=true, to_apply=%region_1.1 | all-reduce | flops 24576 | bytes 98304 | tf_op jit(solution)/shard_map/while/body/eval_jaxpr/psum | solution.py:20
  878.2 4.3 tile.31
  882.5 12.9 %copy.28 = bf16[6,8,128,768]{3,1,2,0:T(8,128)(2,1)} copy(bf16[6,8,128,768]{3,2,1,0:T(8,128)(2,1)} %bitcast.29) | data formatting | bytes 18874368 | tf_op jit(solution)/shard_map/while
  895.4 7.9 slice.242
  903.3 23.0 %reshape.222 = bf16[48,128,767]{2,1,0:T(8,128)(2,1)} reshape(bf16[48,98176]{1,0:T(8,128)(2,1)} %slice.242) | data formatting | bytes 18849792 | tf_op jit(solution)/shard_map/while/body/eval_jaxpr/reshape | solution.py:53
  926.3 6.6 fusion.26
  935.3 2.0 copy.31
  937.4 24.5 %reduce-scatter.6.cloned.1.call-done = f32[1024,2]{1,0:T(8,128)} async-done(((f32[4096,2]{1,0:T(8,128)}), f32[1024,2]{1,0:T(8,128)}) %reduce-scatter.6.cloned.1.call-update) | async-done | bytes 8208 | tf_op jit(solution)/shard_map/while
  961.9 1.2 copy.32
  (138 shorter events, 20.6 us)
Async XLA Ops:
  6.5 7.9 copy-start
  6.5 3.1 copy-start.3
  6.5 7.9 copy-start.5
  6.5 7.9 copy-start.4
  6.5 7.9 copy-start.1
  8.3 6.1 collective-permute-start
  14.5 250.1 %reduce-scatter.6.cloned.1.call-start = ((), (), s32[]{:S(2)}) async-start(), calls=%async_computation.1 | async-start | bytes 2621440 | tf_op jit(solution)/shard_map/while
  265.8 231.2 %reduce-scatter.6.cloned.1.call-start = ((), (), s32[]{:S(2)}) async-start(), calls=%async_computation.1 | async-start | bytes 2621440 | tf_op jit(solution)/shard_map/while
  498.3 231.2 %reduce-scatter.6.cloned.1.call-start = ((), (), s32[]{:S(2)}) async-start(), calls=%async_computation.1 | async-start | bytes 2621440 | tf_op jit(solution)/shard_map/while
  730.7 231.2 %reduce-scatter.6.cloned.1.call-start = ((), (), s32[]{:S(2)}) async-start(), calls=%async_computation.1 | async-start | bytes 2621440 | tf_op jit(solution)/shard_map/while
  963.1 0.6 copy-start.2
Sparse Core Ops, SparseCore 0:
  238.6 25.9 reduce-scatter.5
  472.6 24.3 reduce-scatter.5
  705.0 24.3 reduce-scatter.5
  937.5 24.3 reduce-scatter.5
where the time goes:
time: 972 us; the launch traced here: 970 us
  blocking collectives  531 us (55%)
  local copies, waits for them, and re-layouts  279 us (29%)
  waiting for transfers between devices  104 us (11%)
  matrix products  29.9 us (3%)
  between operations  13.1 us (1%)
    psum x4, blocking collectives, from_root(): return lax.psum(jnp.where(mine, array, jnp.zeros_like(array)), axis)  531 us
    while x8, waiting for transfers between devices  99.7 us
    reshape x4, local copies, waits for them, and re-layouts, correlate(): tiled.reshape(stacked, block_len, padded_len - 1)[:, :, :kernel_len]  92.1 us
    while x28, local copies, waits for them, and re-layouts  78.9 us
    gather x4, local copies, waits for them, and re-layouts, round_step(): picked = jnp.take(waveforms, chosen_flat, axis=0)  35.7 us
    slice x4, local copies, waits for them, and re-layouts, correlate(): tiled = jnp.tile(padded, (1, block_len))[:, block_len:]  31.7 us
    dot_general x4, matrix products, correlate(): jnp.einsum('sbk,sck->sbc', shifted, toeplitz, preferred_element_type=jnp....  26.5 us
  transfers between devices with their start and end apart: 5, of which 5 were waited for; matrix products, arithmetic and copies ran while one was open for 0% of the time, Pallas kernels for 0%

commit v1 on v0

v1 whole, which is shorter than its diff:
```python
import functools

import jax
import jax.numpy as jnp
from jax import lax
from jax.experimental import pallas as pl
from jax.experimental.pallas import tpu as pltpu
from jax.sharding import PartitionSpec as P

bf=jnp.bfloat16; f32=jnp.float32
NB=32; YB=40
def head_kernel(slots, owner, cl, wf, o, buf, scr, sem):
    n=buf.shape[0]
    def ch(i):
        j=i//slots
        return cl[owner[j//2]*2+j%2, i%slots]
    def cp(i,c):
        r=pl.multiple_of(((c%8)//2)*2,2)
        return pltpu.make_async_copy(wf.at[c//8,pl.ds(0,4),pl.ds(r,2),:], buf.at[i], sem.at[0])
    def start(i,_): cp(i,ch(i)).start(); return 0
    def wait(i,_): cp(i,0).wait(); return 0
    lax.fori_loop(0,n,start,0,unroll=8)
    lax.fori_loop(0,n,wait,0,unroll=8)
    G=8
    def body(g,_):
        scr[...]=buf[pl.ds(g*G,G)].reshape(G*8,128).astype(f32)
        for k in range(G):
            i=g*G+k
            o[pl.ds(i*4,4),:]=scr[pl.ds(k*8+ch(i)%2,4,stride=2),:]
        return 0
    lax.fori_loop(0,n//G,body,0)
def corr_kernel(slots, w_ref, y_ref, rn_ref, cnt_ref, o_ref, w32, sc):
    n=w_ref.shape[0]; nt=n//slots
    w=w_ref[...].astype(f32)
    for j in range(4): w32[j]=w[:,128*j:128*(j+1)]
    q=w*w
    hi=q.astype(bf); lo=(q-hi.astype(f32)).astype(bf)
    ones=jnp.ones((512,128),bf)
    te=jnp.dot(hi,ones,preferred_element_type=f32)+jnp.dot(lo,ones,preferred_element_type=f32)
    sc[...]=cnt_ref[...]*lax.rsqrt(te+1e-6)
    lane=lax.broadcasted_iota(jnp.int32,(128,128),1); row=lax.broadcasted_iota(jnp.int32,(128,128),0)
    up=lane>=row
    zero=jnp.zeros((128,128),f32)
    def one(i):
        R=[]
        for j in range(4):
            b=w32[j,pl.ds(i,8,stride=0),:]
            b=jnp.concatenate([b]*16,axis=0)
            R.append(pltpu.roll(b,0,axis=1,stride=1,stride_axis=0))
        R=[zero]+R+[zero]
        T=jnp.concatenate([jnp.where(up,R[j+1],R[j]).astype(bf) for j in range(5)],axis=1)
        X=jnp.concatenate([y_ref[i,j:j+32,:].astype(bf) for j in range(5)],axis=1)
        out=lax.dot_general(X,T,(((1,),(1,)),((),())),preferred_element_type=f32)
        s=sc[pl.ds(i,8,stride=0),:]
        return out*rn_ref[i]*jnp.concatenate([s]*4,axis=0)
    for t in range(nt):
        def body(k,acc):
            return acc+one(t*slots+k)
        o_ref[t]=lax.fori_loop(0,slots,body,jnp.zeros((32,128),f32),unroll=UN)
UN=2
def corr(w,y,rn,cnt,slots=24):
    n=w.shape[0]
    return pl.pallas_call(functools.partial(corr_kernel,slots),
      out_shape=jax.ShapeDtypeStruct((n//slots,32,128),f32),
      scratch_shapes=[pltpu.VMEM((4,n,128),f32),pltpu.VMEM((n,128),f32)],
      compiler_params=pltpu.CompilerParams(vmem_limit_bytes=60*1024*1024))(w,y,rn,cnt)
def heads(owner,cl,wf4,slots=24,n=192):
    return pl.pallas_call(functools.partial(head_kernel,slots),
      out_shape=jax.ShapeDtypeStruct((n*4,128),f32),
      grid_spec=pltpu.PrefetchScalarGridSpec(num_scalar_prefetch=2,grid=(),in_specs=[pl.BlockSpec(memory_space=pl.ANY)],
        out_specs=pl.BlockSpec(memory_space=pltpu.VMEM),
        scratch_shapes=[pltpu.VMEM((n,4,2,128),bf),pltpu.VMEM((64,128),f32),pltpu.SemaphoreType.DMA((1,))]))(owner,cl,wf4)
def energy_kernel(slots, owner, cl, wf, hd, y, rn, buf, scr, pt, sem):
    n=buf.shape[0]
    def ch(i):
        j=i//slots
        return cl[owner[j//2]*2+j%2, i%slots]
    def cp(i,c):
        r=pl.multiple_of(((c%8)//2)*2,2)
        return pltpu.make_async_copy(wf.at[c//8,:,pl.ds(r,2),:], buf.at[i], sem.at[i])
    def start(i,_): cp(i,ch(i)).start(); return 0
    lax.fori_loop(0,n,start,0,unroll=8)
    r0=lax.broadcasted_iota(jnp.int32,(256,256),0)%128; c0=lax.broadcasted_iota(jnp.int32,(256,256),1)
    U=jnp.where((c0>=128)|(r0<c0),1.0,0.0).astype(bf)
    G=EG
    def body(g,_):
        for k in range(G):
            i=g*G+k
            cp(i,0).wait()
            scr[k]=buf[i].reshape(64,128).astype(f32)
        sqs=[]
        for k in range(G):
            i=g*G+k
            a=scr[k,pl.ds(ch(i)%2,32,stride=2),:]
            y[i,0:32,:]=a
            y[i,32:36,:]=hd[pl.ds(i*4,4),:]
            y[i,36:40,:]=jnp.zeros((4,128),f32)
            a=y[i]
            sqs.append(a*a)
        q=jnp.concatenate(sqs,axis=0)
        hi=q.astype(bf); lo=(q-hi.astype(f32)).astype(bf)
        pt[...]=jnp.dot(jnp.concatenate([hi,lo],axis=1),U,preferred_element_type=f32)
        for k in range(G):
            o=k*YB
            tot=[pt[o+d:o+d+32,128:256] for d in range(4)]
            e=(tot[0]+tot[1])+(tot[2]+tot[3])+(pt[o+4:o+36,0:128]-pt[o:o+32,0:128])
            rn[g*G+k]=lax.rsqrt(jnp.maximum(e,128.0))
        return 0
    lax.fori_loop(0,n//G,body,0)
EG=8
def energy(owner,cl,wf4,hd,slots=24,n=192):
    return pl.pallas_call(functools.partial(energy_kernel,slots),
      out_shape=(jax.ShapeDtypeStruct((n,YB,128),f32),jax.ShapeDtypeStruct((n,32,128),f32)),
      grid_spec=pltpu.PrefetchScalarGridSpec(num_scalar_prefetch=2,grid=(),in_specs=[pl.BlockSpec(memory_space=pl.ANY),pl.BlockSpec(memory_space=pltpu.VMEM)],
        out_specs=(pl.BlockSpec(memory_space=pltpu.VMEM),pl.BlockSpec(memory_space=pltpu.VMEM)),
        scratch_shapes=[pltpu.VMEM((n,32,2,128),bf),pltpu.VMEM((EG,64,128),f32),pltpu.VMEM((EG*YB,256),f32),pltpu.SemaphoreType.DMA((n,))]),
      compiler_params=pltpu.CompilerParams(vmem_limit_bytes=60*1024*1024))(owner,cl,wf4,hd)


def permuted(x, axis, to):
    return lax.ppermute(x, axis, [(i, to(i)) for i in range(lax.axis_size(axis))])


def shards(waveforms, templates, channel_lists, channel_counts, owner_rounds):
    c, shard_len = waveforms.shape
    tpb, slots, taps = templates.shape
    rounds = owner_rounds.shape[0]
    nt = rounds * tpb
    n = nt * slots
    me = lax.axis_index("tm")
    group = lax.axis_index("tmpl")
    wf4 = waveforms.reshape(c // 8, 8, shard_len // 128, 128).transpose(0, 2, 1, 3)
    mine = (owner_rounds == me)[:, None, None, None]
    waves = jnp.where(mine, templates[None], jnp.zeros((), templates.dtype)).reshape(n, taps)
    for s in (1, 2, 4, 8, 16):
        waves = waves + permuted(waves, "tm", lambda i, s=s: i ^ s)
    hd = heads(owner_rounds, channel_lists, wf4, slots, n).astype(jnp.bfloat16)
    hd = lax.ppermute(hd, "tm", [(i, i - 1) for i in range(1, lax.axis_size("tm"))]).astype(jnp.float32)
    y, rn = energy(owner_rounds, channel_lists, wf4, hd, slots, n)
    ids = (owner_rounds[:, None] * tpb + jnp.arange(tpb, dtype=jnp.int32)[None, :]).reshape(-1)
    counts = jnp.take(channel_counts, ids, axis=0)
    slot_ids = group * slots + jnp.arange(slots, dtype=jnp.int32)
    mask = jnp.broadcast_to((slot_ids[None, :] < counts[:, None]).astype(jnp.float32).reshape(n, 1), (n, 128))
    local = corr(waves, y, rn, mask, slots)
    groups = lax.axis_size("tmpl")
    local = local.reshape(nt, groups, shard_len // groups)
    pick = lambda k: lax.dynamic_index_in_dim(local, (group + k) % groups, 1, keepdims=False)
    out = pick(0)
    for k in range(1, groups):
        out = out + lax.ppermute(pick(k), "tmpl", [(i, (i + k) % groups) for i in range(groups)])
    return out


def solution(mesh):
    in_specs = (P(None, "tm"), P("tm", "tmpl", None), P(None, "tmpl"), P(), P())
    return jax.shard_map(shards, mesh=mesh, in_specs=in_specs, out_specs=P(None, ("tm", "tmpl")), check_vma=False)
```

time: 972 us -> 116 us (0.12)
  blocking collectives: 531 us -> 0 us
  local copies, waits for them, and re-layouts: 279 us -> 4.3 us
  waiting for transfers between devices: 104 us -> 18.4 us
  Pallas kernels: 0 us -> 67.6 us
  matrix products: 29.9 us -> 0 us
  starting transfers between devices: 1.46 us -> 20 us
  between operations: 13.1 us -> 0.13 us
    psum x4 -> x0, blocking collectives: 531 us -> none  [from_root(): return lax.psum(jnp.where(mine, array, jnp.zeros_like(array)), axis)]
    while x8 -> x0, waiting for transfers between devices: 99.7 us -> none
    reshape x20 -> x1, local copies, waits for them, and re-layouts: 94.5 us -> 0.95 us  [shards(): local = local.reshape(nt, groups, shard_len // groups)]
    while x28 -> x0, local copies, waits for them, and re-layouts: 78.9 us -> none
    pallas_call x0 -> x3, Pallas kernels: none -> 67.6 us  [the longest x1 34 us: corr(): pl.pallas_call(functools.partial(corr_kernel, slots), out_shape=jax.Shape...]
    gather x8 -> x1, local copies, waits for them, and re-layouts: 45.7 us -> 0.64 us  [shards(): counts = jnp.take(channel_counts, ids, axis=0)]
    slice x5 -> x0, local copies, waits for them, and re-layouts: 33.4 us -> none  [the longest x4 31.7 us: correlate(): tiled = jnp.tile(padded, (1, block_len))[:, block_len:]]
    dot_general x8 -> x0, matrix products: 29.9 us -> none  [the longest x4 26.5 us: correlate(): jnp.einsum('sbk,sck->sbc', shifted, toeplitz, preferred_element_type=jnp....]
  transfers between devices with their start and end apart: 5 -> 9, of which waited for: 5 -> 5; matrix products, arithmetic and copies ran while one was open for 0% -> 4% of each run, Pallas kernels for 0% -> 29%
where the time goes in v1:
time: 116 us; the launch traced here: 115 us
  Pallas kernels  67.6 us (58%)
  starting transfers between devices  20 us (17%)
  waiting for transfers between devices  18.4 us (16%)
  other arithmetic  5.16 us (4%)
  local copies, waits for them, and re-layouts  4.3 us (4%)
    pallas_call x1, Pallas kernels, corr(): pl.pallas_call(functools.partial(corr_kernel, slots), out_shape=jax.Shape...  34 us
    pallas_call x1, Pallas kernels, energy(): pl.pallas_call(functools.partial(energy_kernel, slots), out_shape=(jax.Sh...  21.9 us
    ppermute x5, waiting for transfers between devices, permuted(): lax.ppermute(x, axis, [(i, to(i)) for i in range(lax.axis_size(axis))])  14.1 us
    ppermute x5, starting transfers between devices, permuted(): lax.ppermute(x, axis, [(i, to(i)) for i in range(lax.axis_size(axis))])  14 us
    pallas_call x1, Pallas kernels, heads(): pl.pallas_call(functools.partial(head_kernel, slots), out_shape=jax.Shape...  11.7 us
    ppermute x3, starting transfers between devices, shards(): lax.ppermute(pick(k), 'tmpl', [(i, (i + k) % groups) for i in range(group...  4.65 us
    ppermute x3, waiting for transfers between devices, shards(): lax.ppermute(pick(k), 'tmpl', [(i, (i + k) % groups) for i in range(group...  4.24 us
  transfers between devices with their start and end apart: 9, of which 5 were waited for; matrix products, arithmetic and copies ran while one was open for 4% of the time, Pallas kernels for 29%

profile of v1, /device:TPU:0, one launch (start us, length us, event | category | flops | bytes accessed | tf_op | source)
XLA Modules:
  0.0 115.5 jit_solution(9988371089792316475)
XLA Ops:
  0.0 0.0 copy-start
  0.0 0.7 broadcast_compare_fusion
  0.7 0.1 broadcast_in_dim.39
  0.8 0.1 broadcast_in_dim.40
  0.8 0.9 bitcast_select_fusion
  1.7 0.1 collective-permute-start
  1.8 1.4 %copy.9.cl = s32[64,24]{1,0:T(8,128)} copy(s32[64,24]{0,1:T(8,128)} %param.7) | data formatting | bytes 12288 | tf_op args[2]
  3.2 0.0 copy-start.2
  3.2 0.0 copy-start.1
  3.3 11.7 %shard_map.55 = f32[768,128]{1,0:T(8,128)} custom-call(s32[4]{0:T(128)} %owner.3, s32[64,24]{1,0:T(8,128)} %copy.9.cl, bf16[250,32,8,128]{3,2,1,0:T(8,128)(2,1)} %bitcast.24), custom_call_target="tpu_custom_call" | custom-call | tf_op jit(solution)/shard_map/pallas_call | solution.py:68
  14.9 1.0 convert_element_type.16
  15.9 1.3 %collective-permute-start.5 = (bf16[768,128]{1,0:T(8,128)(2,1)S(1)}, bf16[768,128]{1,0:T(8,128)(2,1)S(1)}, u32[]{:S(2)}, u32[]{:S(2)}) collective-permute-start(bf16[768,128]{1,0:T(8,128)(2,1)S(1)} %convert_element_type.16), channel_id=1, source_target_pairs={{4,0},{8,4},{12,8},{16,12},{20,16},{24,20},{28,24},{32,28},{36,32}... | collective-permute-start | bytes 589832 | tf_op jit(solution)/shard_map/ppermute | solution.py:138
  17.2 0.0 copy-done.2
  17.3 0.1 iota_add_fusion
  17.3 0.1 add.131
  17.4 0.1 add.129
  17.5 0.0 collective-permute-done
  17.5 0.0 copy-done.1
  17.5 0.1 fusion.3
  17.6 2.8 %collective-permute-start.1 = (bf16[192,512]{1,0:T(8,128)(2,1)S(1)}, bf16[192,512]{1,0:T(8,128)(2,1)S(1)}, u32[]{:S(2)}, u32[]{:S(2)}) collective-permute-start(bf16[192,512]{1,0:T(8,128)(2,1)S(1)} %fusion.3), channel_id=1, source_target_pairs={{0,8},{4,12},{8,0},{12,4},{16,24},{20,28},{24,16},{28,20},{32,40},... | collective-permute-start | bytes 589832 | tf_op jit(solution)/shard_map/ppermute | solution.py:121
  20.4 7.4 %collective-permute-done.1 = bf16[192,512]{1,0:T(8,128)(2,1)S(1)} collective-permute-done((bf16[192,512]{1,0:T(8,128)(2,1)S(1)}, bf16[192,512]{1,0:T(8,128)(2,1)S(1)}, u32[]{:S(2)}, u32[]{:S(2)}) %collective-permute-start.1) | collective-permute-done | bytes 196640 | tf_op jit(solution)/shard_map/ppermute | solution.py:121
  27.8 0.1 add.120
  27.9 4.0 %collective-permute-start.2 = (bf16[192,512]{1,0:T(8,128)(2,1)S(1)}, bf16[192,512]{1,0:T(8,128)(2,1)S(1)}, u32[]{:S(2)}, u32[]{:S(2)}) collective-permute-start(bf16[192,512]{1,0:T(8,128)(2,1)S(1)} %add.120), channel_id=1, source_target_pairs={{0,16},{4,20},{8,24},{12,28},{16,0},{20,4},{24,8},{28,12},{32,48},... | collective-permute-start | bytes 589832 | tf_op jit(solution)/shard_map/ppermute | solution.py:121
  31.9 0.0 copy-done
  31.9 0.6 gather_fusion
  32.5 3.0 %collective-permute-done.2 = bf16[192,512]{1,0:T(8,128)(2,1)S(1)} collective-permute-done((bf16[192,512]{1,0:T(8,128)(2,1)S(1)}, bf16[192,512]{1,0:T(8,128)(2,1)S(1)}, u32[]{:S(2)}, u32[]{:S(2)}) %collective-permute-start.2) | collective-permute-done | bytes 196640 | tf_op jit(solution)/shard_map/ppermute | solution.py:121
  35.5 0.1 add.121
  35.6 2.0 %collective-permute-start.3 = (bf16[192,512]{1,0:T(8,128)(2,1)S(1)}, bf16[192,512]{1,0:T(8,128)(2,1)S(1)}, u32[]{:S(2)}, u32[]{:S(2)}) collective-permute-start(bf16[192,512]{1,0:T(8,128)(2,1)S(1)} %add.121), channel_id=1, source_target_pairs={{0,32},{4,36},{8,40},{12,44},{16,48},{20,52},{24,56},{28,60},{32,0... | collective-permute-start | bytes 589832 | tf_op jit(solution)/shard_map/ppermute | solution.py:121
  37.6 3.7 %collective-permute-done.3 = bf16[192,512]{1,0:T(8,128)(2,1)S(1)} collective-permute-done((bf16[192,512]{1,0:T(8,128)(2,1)S(1)}, bf16[192,512]{1,0:T(8,128)(2,1)S(1)}, u32[]{:S(2)}, u32[]{:S(2)}) %collective-permute-start.3) | collective-permute-done | bytes 196640 | tf_op jit(solution)/shard_map/ppermute | solution.py:121
  41.3 0.1 add.122
  41.4 5.1 %collective-permute-start.4 = (bf16[192,512]{1,0:T(8,128)(2,1)S(1)}, bf16[192,512]{1,0:T(8,128)(2,1)S(1)}, u32[]{:S(2)}, u32[]{:S(2)}) collective-permute-start(bf16[192,512]{1,0:T(8,128)(2,1)S(1)} %add.122), channel_id=1, source_target_pairs={{0,64},{4,68},{8,72},{12,76},{16,80},{20,84},{24,88},{28,92},{32,9... | collective-permute-start | bytes 589832 | tf_op jit(solution)/shard_map/ppermute | solution.py:121
  46.5 0.1 compare_convert_fusion
  46.6 0.1 reshape.88
  46.7 0.0 collective-permute-done.5
  46.7 0.8 convert_element_type.17.hd
  47.4 21.9 %shard_map.56 = (f32[192,40,128]{2,1,0:T(8,128)}, f32[192,32,128]{2,1,0:T(8,128)}) custom-call(s32[4]{0:T(128)} %owner.3, s32[64,24]{1,0:T(8,128)} %copy.9.cl, bf16[250,32,8,128]{3,2,1,0:T(8,128)(2,1)} %bitcast.25, f32[768,128]{1,0:T(8,128)} %convert_element_type.17.hd), custom_call_target="tpu_custom_call" | custom-call | tf_op jit(solution)/shard_map/pallas_call | solution.py:112
  69.3 0.0 collective-permute-done.4
  69.3 0.7 add.123.w_ref
  70.1 0.7 broadcast_in_dim.45.cnt_ref
  70.8 34.0 %shard_map.57 = f32[8,32,128]{2,1,0:T(8,128)} custom-call(bf16[192,512]{1,0:T(8,128)(2,1)} %add.123.w_ref, f32[192,40,128]{2,1,0:T(8,128)} %get-tuple-element.7.y_ref, f32[192,32,128]{2,1,0:T(8,128)} %get-tuple-element.8.rn_ref, f32[192,128]{1,0:T(8,128)} %broadcast_in_dim.45.cnt_ref), custom_call_target="tpu_custom_call" | custom-call | tf_op jit(solution)/shard_map/pallas_call | solution.py:63
  104.8 0.9 reshape.87
  105.8 0.1 constant_dynamic-slice_fusion.3
  105.9 2.8 %collective-permute-start.8 = (f32[8,1024]{1,0:T(8,128)S(1)}, f32[8,1024]{1,0:T(8,128)S(1)}, u32[]{:S(2)}, u32[]{:S(2)}) collective-permute-start(f32[8,1024]{1,0:T(8,128)S(1)} %bitcast.26), channel_id=1, source_target_pairs={{0,3},{1,0},{2,1},{3,2},{4,7},{5,4},{6,5},{7,6},{8,11},{9,8},{10,9... | collective-permute-start | bytes 98312 | tf_op jit(solution)/shard_map/ppermute | solution.py:150
  108.8 0.9 collective-permute-start.7
  109.7 1.0 collective-permute-start.6
  110.6 0.0 collective-permute-done.8
  110.6 3.7 %collective-permute-done.7 = f32[8,1024]{1,0:T(8,128)S(1)} collective-permute-done((f32[8,1024]{1,0:T(8,128)S(1)}, f32[8,1024]{1,0:T(8,128)S(1)}, u32[]{:S(2)}, u32[]{:S(2)}) %collective-permute-start.7) | collective-permute-done | bytes 32800 | tf_op jit(solution)/shard_map/ppermute | solution.py:150
  114.3 0.6 collective-permute-done.6
  114.8 0.6 fusion.1
  (8 shorter events, 0.0 us)
Async XLA Ops:
  0.0 31.9 %copy-start = (s32[64]{0:T(128)S(1)}, s32[64]{0:T(128)}, u32[]{:S(2)}) copy-start(s32[64]{0:T(128)} %param.8) | copy-start | bytes 772
  1.7 15.8 %collective-permute-start = (bf16[192,512]{1,0:T(8,128)(2,1)S(1)}, bf16[192,512]{1,0:T(8,128)(2,1)S(1)}, u32[]{:S(2)}, u32[]{:S(2)}) collective-permute-start(bf16[192,512]{1,0:T(8,128)(2,1)S(1)} %bitcast_select_fusion), channel_id=1, source_target_pairs={{0,4},{4,0},{8,12},{12,8},{16,20},{20,16},{24,28},{28,24},{32,36},... | collective-permute-start | bytes 589832 | tf_op jit(solution)/shard_map/ppermute | solution.py:121
  3.2 14.0 %copy-start.2 = (s32[4]{0:T(128)S(1)}, s32[4]{0:T(128)}, u32[]{:S(2)}) copy-start(s32[4]{0:T(128)} %owner.3) | copy-start | bytes 52
  3.2 14.3 %copy-start.1 = (bf16[2,24,512]{2,1,0:T(8,128)(2,1)S(1)}, bf16[2,24,512]{2,1,0:T(8,128)(2,1)}, u32[]{:S(2)}) copy-start(bf16[2,24,512]{2,1,0:T(8,128)(2,1)} %param.6) | copy-start | bytes 147460
  15.9 30.7 %collective-permute-start.5 = (bf16[768,128]{1,0:T(8,128)(2,1)S(1)}, bf16[768,128]{1,0:T(8,128)(2,1)S(1)}, u32[]{:S(2)}, u32[]{:S(2)}) collective-permute-start(bf16[768,128]{1,0:T(8,128)(2,1)S(1)} %convert_element_type.16), channel_id=1, source_target_pairs={{4,0},{8,4},{12,8},{16,12},{20,16},{24,20},{28,24},{32,28},{36,32}... | collective-permute-start | bytes 589832 | tf_op jit(solution)/shard_map/ppermute | solution.py:138
  17.6 10.2 %collective-permute-start.1 = (bf16[192,512]{1,0:T(8,128)(2,1)S(1)}, bf16[192,512]{1,0:T(8,128)(2,1)S(1)}, u32[]{:S(2)}, u32[]{:S(2)}) collective-permute-start(bf16[192,512]{1,0:T(8,128)(2,1)S(1)} %fusion.3), channel_id=1, source_target_pairs={{0,8},{4,12},{8,0},{12,4},{16,24},{20,28},{24,16},{28,20},{32,40},... | collective-permute-start | bytes 589832 | tf_op jit(solution)/shard_map/ppermute | solution.py:121
  27.9 7.6 %collective-permute-start.2 = (bf16[192,512]{1,0:T(8,128)(2,1)S(1)}, bf16[192,512]{1,0:T(8,128)(2,1)S(1)}, u32[]{:S(2)}, u32[]{:S(2)}) collective-permute-start(bf16[192,512]{1,0:T(8,128)(2,1)S(1)} %add.120), channel_id=1, source_target_pairs={{0,16},{4,20},{8,24},{12,28},{16,0},{20,4},{24,8},{28,12},{32,48},... | collective-permute-start | bytes 589832 | tf_op jit(solution)/shard_map/ppermute | solution.py:121
  35.6 5.7 %collective-permute-start.3 = (bf16[192,512]{1,0:T(8,128)(2,1)S(1)}, bf16[192,512]{1,0:T(8,128)(2,1)S(1)}, u32[]{:S(2)}, u32[]{:S(2)}) collective-permute-start(bf16[192,512]{1,0:T(8,128)(2,1)S(1)} %add.121), channel_id=1, source_target_pairs={{0,32},{4,36},{8,40},{12,44},{16,48},{20,52},{24,56},{28,60},{32,0... | collective-permute-start | bytes 589832 | tf_op jit(solution)/shard_map/ppermute | solution.py:121
  41.4 28.0 %collective-permute-start.4 = (bf16[192,512]{1,0:T(8,128)(2,1)S(1)}, bf16[192,512]{1,0:T(8,128)(2,1)S(1)}, u32[]{:S(2)}, u32[]{:S(2)}) collective-permute-start(bf16[192,512]{1,0:T(8,128)(2,1)S(1)} %add.122), channel_id=1, source_target_pairs={{0,64},{4,68},{8,72},{12,76},{16,80},{20,84},{24,88},{28,92},{32,9... | collective-permute-start | bytes 589832 | tf_op jit(solution)/shard_map/ppermute | solution.py:121
  105.9 4.7 %collective-permute-start.8 = (f32[8,1024]{1,0:T(8,128)S(1)}, f32[8,1024]{1,0:T(8,128)S(1)}, u32[]{:S(2)}, u32[]{:S(2)}) collective-permute-start(f32[8,1024]{1,0:T(8,128)S(1)} %bitcast.26), channel_id=1, source_target_pairs={{0,3},{1,0},{2,1},{3,2},{4,7},{5,4},{6,5},{7,6},{8,11},{9,8},{10,9... | collective-permute-start | bytes 98312 | tf_op jit(solution)/shard_map/ppermute | solution.py:150
  108.8 5.5 %collective-permute-start.7 = (f32[8,1024]{1,0:T(8,128)S(1)}, f32[8,1024]{1,0:T(8,128)S(1)}, u32[]{:S(2)}, u32[]{:S(2)}) collective-permute-start(f32[8,1024]{1,0:T(8,128)S(1)} %bitcast.27), channel_id=1, source_target_pairs={{0,2},{1,3},{2,0},{3,1},{4,6},{5,7},{6,4},{7,5},{8,10},{9,11},{10,... | collective-permute-start | bytes 98312 | tf_op jit(solution)/shard_map/ppermute | solution.py:150
  109.7 5.2 %collective-permute-start.6 = (f32[8,1024]{1,0:T(8,128)S(1)}, f32[8,1024]{1,0:T(8,128)S(1)}, u32[]{:S(2)}, u32[]{:S(2)}) collective-permute-start(f32[8,1024]{1,0:T(8,128)S(1)} %bitcast.28), channel_id=1, source_target_pairs={{0,1},{1,2},{2,3},{3,0},{4,5},{5,6},{6,7},{7,4},{8,9},{9,10},{10,1... | collective-permute-start | bytes 98312 | tf_op jit(solution)/shard_map/ppermute | solution.py:150

commit v2 on v0

v2 whole, which is shorter than its diff:
```python
import functools

import jax
import jax.numpy as jnp
from jax import lax
from jax.experimental import pallas as pl
from jax.experimental.pallas import tpu as pltpu
from jax.sharding import PartitionSpec as P

bf16, f32, i32 = jnp.bfloat16, jnp.float32, jnp.int32
LANES = 128
FLOOR = 1e-6
GROUP = 8
UNROLL = 12
VMEM_LIMIT = 24 * 1024 * 1024


def vmem_spec():
    return pl.BlockSpec(memory_space=pltpu.VMEM)


def smem_spec():
    return pl.BlockSpec(memory_space=pltpu.SMEM)


def exact_pair(x):
    hi = x.astype(bf16)
    return hi, (x - hi.astype(f32)).astype(bf16)


def gather_kernel(tpb, owner, lists, wf, y, heads, buf, scr, hs, sem):
    slots = lists.shape[0]
    n, blocks = y.shape[0], y.shape[1]
    hb = heads.shape[0] // n

    def template(t):
        return owner[t // tpb] * tpb + t % tpb

    def copy(i, c):
        pair = pl.multiple_of(((c % 8) // 2) * 2, 2)
        return pltpu.make_async_copy(wf.at[c // 8, :, pl.ds(pair, 2), :], buf.at[i], sem.at[i])

    for t in range(n // slots):
        tid = template(t)

        def start(s, _, t=t, tid=tid):
            copy(t * slots + s, lists[s, tid]).start()
            return 0

        lax.fori_loop(0, slots, start, 0, unroll=8)

    for t in range(n // slots):
        tid = template(t)

        def group(g, _, t=t, tid=tid):
            for k in range(GROUP):
                s = g * GROUP + k
                copy(t * slots + s, 0).wait()
            for k in range(GROUP):
                s = g * GROUP + k
                i = t * slots + s
                scr[k, 0 : 2 * blocks, :] = buf[i].reshape(2 * blocks, LANES).astype(f32)
                own = scr[k, pl.ds(lists[s, tid] % 2, blocks, stride=2), :]
                y[i] = own
                hs[pl.ds(i * hb, hb), :] = own[0:hb]
            return 0

        lax.fori_loop(0, slots // GROUP, group, 0)
    heads[...] = hs[...].astype(bf16)


def energy_kernel(taps, y, halo, rn, a, yg, pg, tg):
    n, blocks = y.shape[0], y.shape[1]
    tb = taps // LANES
    rows = yg.shape[1]
    half = blocks // 2
    wide = 2 * LANES
    r = lax.broadcasted_iota(i32, (wide, wide), 0) % LANES
    c = lax.broadcasted_iota(i32, (wide, wide), 1)
    sums = jnp.where((c >= LANES) | (r < c), 1.0, 0.0).astype(bf16)
    for k in range(GROUP):
        yg[k, blocks + tb :, :] = jnp.zeros((rows - blocks - tb, LANES), f32)

    def group(g, _):
        tails = halo[pl.ds(pl.multiple_of(g * GROUP * tb, GROUP * tb), GROUP * tb), :].astype(f32)
        for k in range(GROUP):
            yg[k, 0:blocks, :] = y[g * GROUP + k]
            yg[k, blocks : blocks + tb, :] = tails[tb * k : tb * (k + 1)]
        q = yg[...].reshape(GROUP * rows, LANES)
        parts = jnp.dot(jnp.concatenate(exact_pair(q * q), axis=1), sums, preferred_element_type=f32)
        pg[0 : GROUP * rows, :] = parts[:, 0:LANES]
        tg[0 : GROUP * rows, :] = parts[:, LANES:]
        for k in range(GROUP):
            i = g * GROUP + k
            o = k * rows
            tot = [tg[pl.ds(o + d, half, stride=2), :] for d in range(tb + 1)]
            pre = [pg[pl.ds(o + d, half, stride=2), :] for d in (0, 1, tb, tb + 1)]
            for v in range(2):
                e = pre[2 + v] - pre[v]
                for d in range(tb):
                    e = e + tot[v + d]
                rn[i, half * v : half * (v + 1), :] = lax.rsqrt(jnp.maximum(e, taps / 4.0))
            for v in range(tb + 2):
                a[i, half * v : half * (v + 1), :] = yg[k, pl.ds(v, half, stride=2), :].astype(bf16)
        return 0

    lax.fori_loop(0, n // GROUP, group, 0)


def correlate_kernel(tpb, slots, owner, counts, place, w, a, rn, *refs):
    outs, (wr, scale, acc) = refs[:-3], refs[-3:]
    n, taps = w.shape
    tb = taps // LANES
    nt = n // slots
    blocks = rn.shape[1]
    half = blocks // 2
    parts = len(outs)
    group = place[0]
    wf = w[...].astype(f32)
    hi, lo = exact_pair(wf * wf)
    ones = jnp.ones((taps, LANES), bf16)
    power = jnp.dot(hi, ones, preferred_element_type=f32) + jnp.dot(lo, ones, preferred_element_type=f32)
    norm = lax.rsqrt(power + FLOOR)
    slot_ids = lax.broadcasted_iota(i32, (slots, LANES), 0) + group * slots
    for t in range(nt):
        count = counts[owner[t // tpb] * tpb + t % tpb]
        scale[t * slots : (t + 1) * slots, :] = jnp.where(slot_ids < count, norm[t * slots : (t + 1) * slots], 0.0)
    row = lax.broadcasted_iota(i32, (LANES, LANES), 0)
    col = lax.broadcasted_iota(i32, (LANES, LANES), 1)
    flip = jnp.where(row + col == LANES - 1, 1.0, 0.0).astype(bf16)
    for j in range(tb):
        wr[j, 0:n, :] = jnp.dot(w[:, LANES * j : LANES * (j + 1)], flip, preferred_element_type=f32)
    own = row >= col
    zero = jnp.zeros((LANES, LANES), bf16)

    def one(i):
        d = [zero]
        for j in range(tb):
            b = jnp.concatenate([wr[j, pl.ds(i, 8, stride=0), :]] * (LANES // 8), axis=0)
            d.append(pltpu.roll(b, 1, axis=1, stride=1, stride_axis=0).astype(bf16))
        d.append(zero)
        band = jnp.concatenate([jnp.where(own, d[j + 1], d[j]) for j in range(tb + 1)], axis=0)
        x = jnp.concatenate([a[i, half * j : half * (j + 2), :] for j in range(tb + 1)], axis=1)
        out = jnp.dot(x, band, preferred_element_type=f32)
        s = scale[pl.ds(i, 8, stride=0), :]
        return out * rn[i] * jnp.concatenate([s] * (blocks // 8), axis=0)

    def template(t, _):
        r = lax.fori_loop(
            0, slots, lambda k, total: total + one(t * slots + k), jnp.zeros((blocks, LANES), f32), unroll=UNROLL
        )
        for v in range(2):
            acc[pl.ds(v * nt + t, half, stride=2 * nt), :] = r[half * v : half * (v + 1)]
        return 0

    lax.fori_loop(0, nt, template, 0)
    per = blocks // parts
    for k, o in enumerate(outs):
        to = (group + k) % parts
        for b in range(per):
            o[:, LANES * b : LANES * (b + 1)] = acc[pl.ds(pl.multiple_of((to * per + b) * nt, 8), nt), :]


def gather(owner, lists, wf4, tpb, tb):
    slots = lists.shape[0]
    n = owner.shape[0] * tpb * slots
    blocks = wf4.shape[1]
    return pl.pallas_call(
        functools.partial(gather_kernel, tpb),
        out_shape=(pltpu.VMEM((n, blocks, LANES), f32), jax.ShapeDtypeStruct((n * tb, LANES), bf16)),
        in_specs=[smem_spec(), smem_spec(), pl.BlockSpec(memory_space=pltpu.HBM)],
        out_specs=(vmem_spec(), vmem_spec()),
        scratch_shapes=[
            pltpu.VMEM((n, blocks, 2, LANES), bf16),
            pltpu.VMEM((GROUP, 2 * blocks + 8, LANES), f32),
            pltpu.VMEM((n * tb, LANES), f32),
            pltpu.SemaphoreType.DMA((n,)),
        ],
        compiler_params=pltpu.CompilerParams(vmem_limit_bytes=VMEM_LIMIT),
        name="gather_rows",
    )(owner, lists, pltpu.with_memory_space_constraint(wf4, pltpu.HBM))


def energy(y, halo, taps):
    n, blocks, _ = y.shape
    tb = taps // LANES
    rows = blocks + 8
    return pl.pallas_call(
        functools.partial(energy_kernel, taps),
        out_shape=(pltpu.VMEM((n, blocks, LANES), f32), pltpu.VMEM((n, blocks // 2 * (tb + 2), LANES), bf16)),
        in_specs=[vmem_spec(), vmem_spec()],
        out_specs=(vmem_spec(), vmem_spec()),
        scratch_shapes=[
            pltpu.VMEM((GROUP, rows, LANES), f32),
            pltpu.VMEM((GROUP * rows + 8, LANES), f32),
            pltpu.VMEM((GROUP * rows + 8, LANES), f32),
        ],
        compiler_params=pltpu.CompilerParams(vmem_limit_bytes=VMEM_LIMIT),
        name="window_energy",
    )(y, halo)


def correlate(owner, counts, place, w, a, rn, tpb, slots, parts):
    n, taps = w.shape
    nt = n // slots
    blocks = rn.shape[1]
    return pl.pallas_call(
        functools.partial(correlate_kernel, tpb, slots),
        out_shape=tuple(jax.ShapeDtypeStruct((nt, blocks // parts * LANES), f32) for _ in range(parts)),
        in_specs=[smem_spec()] * 3 + [vmem_spec()] * 3,
        out_specs=tuple(vmem_spec() for _ in range(parts)),
        scratch_shapes=[
            pltpu.VMEM((taps // LANES, n + 8, LANES), f32),
            pltpu.VMEM((n + 8, LANES), f32),
            pltpu.VMEM(((blocks + 2) * nt, LANES), f32),
        ],
        compiler_params=pltpu.CompilerParams(vmem_limit_bytes=VMEM_LIMIT),
        name="correlate",
    )(owner, counts, place, w, a, rn)


def turned(i, dy, dz):
    return ((i // 8 + dy) % 4) * 8 + ((i // 2 + dz) % 4) * 2 + i % 2


def sent(x, to):
    return lax.ppermute(x, "tm", [(i, to(i)) for i in range(32)])


def round_the_ring(x, first):
    total = x
    for k in (1, 3, 2):
        total = total + sent(x, lambda i: turned(i, 0, k) if (i % 2 == 0) == first else turned(i, k, 0))
    return total


def shards(waveforms, templates, channel_lists, channel_counts, owner_rounds):
    c, shard_len = waveforms.shape
    tpb, slots, taps = templates.shape
    rounds = owner_rounds.shape[0]
    n = rounds * tpb * slots
    me = lax.axis_index("tm")
    group = lax.axis_index("tmpl")
    groups = lax.axis_size("tmpl")
    wf4 = waveforms.reshape(c // 8, 8, shard_len // LANES, LANES).transpose(0, 2, 1, 3)
    other = sent(templates, lambda i: i ^ 1)
    owned = (owner_rounds == me)[:, None, None, None]
    paired = (owner_rounds == (me ^ 1))[:, None, None, None]
    nil = jnp.zeros((), templates.dtype)
    waves = jnp.where(owned, templates[None], jnp.where(paired, other[None], nil)).reshape(n, taps)
    waves = round_the_ring(waves, True)
    y, heads = gather(owner_rounds, channel_lists.T, wf4, tpb, taps // LANES)
    halo = lax.ppermute(heads, "tm", [(i, i - 1) for i in range(1, 32)])
    waves = round_the_ring(waves, False)
    rn, a = energy(y, halo, taps)
    pieces = correlate(owner_rounds, channel_counts, group.reshape(1), waves, a, rn, tpb, slots, groups)
    out = pieces[0]
    for k in range(1, groups):
        out = out + lax.ppermute(pieces[k], "tmpl", [(i, (i + k) % groups) for i in range(groups)])
    return out


def solution(mesh):
    in_specs = (P(None, "tm"), P("tm", "tmpl", None), P(None, "tmpl"), P(), P())
    return jax.shard_map(shards, mesh=mesh, in_specs=in_specs, out_specs=P(None, ("tm", "tmpl")), check_vma=False)
```

time: 972 us -> 54.9 us (0.06)
  blocking collectives: 531 us -> 0 us
  local copies, waits for them, and re-layouts: 279 us -> 1.71 us
  waiting for transfers between devices: 104 us -> 3.31 us
  matrix products: 29.9 us -> 0 us
  Pallas kernels: 0 us -> 24.4 us
  starting transfers between devices: 1.46 us -> 20.8 us
  between operations: 13.1 us -> 0.15 us
    psum x4 -> x0, blocking collectives: 531 us -> none  [from_root(): return lax.psum(jnp.where(mine, array, jnp.zeros_like(array)), axis)]
    while x8 -> x0, waiting for transfers between devices: 99.7 us -> none
    reshape x20 -> x0, local copies, waits for them, and re-layouts: 94.5 us -> none  [the longest x4 92.1 us: correlate(): tiled.reshape(stacked, block_len, padded_len - 1)[:, :, :kernel_len]]
    while x28 -> x0, local copies, waits for them, and re-layouts: 78.9 us -> none
    gather x8 -> x0, local copies, waits for them, and re-layouts: 45.7 us -> none  [the longest x4 35.7 us: round_step(): picked = jnp.take(waveforms, chosen_flat, axis=0)]
    slice x5 -> x0, local copies, waits for them, and re-layouts: 33.4 us -> none  [the longest x4 31.7 us: correlate(): tiled = jnp.tile(padded, (1, block_len))[:, block_len:]]
    dot_general x8 -> x0, matrix products: 29.9 us -> none  [the longest x4 26.5 us: correlate(): jnp.einsum('sbk,sck->sbc', shifted, toeplitz, preferred_element_type=jnp....]
    pallas_call x0 -> x3, Pallas kernels: none -> 24.4 us  [the longest x1 10.7 us: correlate(): pl.pallas_call(functools.partial(correlate_kernel, tpb, slots), out_shape...]
  transfers between devices with their start and end apart: 5 -> 11, of which waited for: 5 -> 4; matrix products, arithmetic and copies ran while one was open for 0% -> 3% of each run, Pallas kernels for 0% -> 25%
where the time goes in v2:
time: 54.9 us; the launch traced here: 54.6 us
  Pallas kernels  24.4 us (44%)
  starting transfers between devices  20.8 us (38%)
  other arithmetic  4.27 us (8%)
  waiting for transfers between devices  3.31 us (6%)
  local copies, waits for them, and re-layouts  1.71 us (3%)
    ppermute x7, starting transfers between devices, sent(): return lax.ppermute(x, 'tm', [(i, to(i)) for i in range(32)])  13.8 us
    pallas_call x1, Pallas kernels, correlate(): pl.pallas_call(functools.partial(correlate_kernel, tpb, slots), out_shape...  10.7 us
    pallas_call x1, Pallas kernels, gather(): pl.pallas_call(functools.partial(gather_kernel, tpb), out_shape=(pltpu.VM...  8.14 us
    ppermute x3, starting transfers between devices, shards(): lax.ppermute(pieces[k], 'tmpl', [(i, (i + k) % groups) for i in range(gro...  5.73 us
    pallas_call x1, Pallas kernels, energy(): pl.pallas_call(functools.partial(energy_kernel, taps), out_shape=(pltpu.V...  5.52 us
    ppermute x3, waiting for transfers between devices, shards(): lax.ppermute(pieces[k], 'tmpl', [(i, (i + k) % groups) for i in range(gro...  2.48 us
    add x2, other arithmetic, round_the_ring(): total + sent(x, lambda i: turned(i, 0, k) if (i % 2 == 0) == first else t...  2.05 us
    unnamed x14, local copies, waits for them, and re-layouts  1.39 us
  transfers between devices with their start and end apart: 11, of which 4 were waited for; matrix products, arithmetic and copies ran while one was open for 3% of the time, Pallas kernels for 25%

profile of v2, /device:TPU:0, one launch (start us, length us, event | category | flops | bytes accessed | tf_op | source)
XLA Modules:
  0.0 54.6 jit_solution(7501311262929501200)
XLA Ops:
  0.0 0.0 collective-permute-start
  0.0 0.7 %broadcast_compare_fusion.1 = (pred[4]{0:T(512)(128)(4,1)S(1)}, pred[4]{0:T(512)(128)(4,1)S(1)}) fusion(s32[4]{0:T(128)} %owner.3, s32[]{:T(128)S(6)} %axis_index.25, s32[]{:T(128)S(6)} %xor.3), kind=kLoop, calls=%fused_computation.6 | loop fusion | flops 8 | bytes 32 | tf_op jit(solution)/shard_map/eq | solution.py:247
  0.7 0.1 broadcast_in_dim.52
  0.7 0.1 broadcast_in_dim.53
  0.8 0.1 broadcast_in_dim.57
  0.9 0.1 broadcast_in_dim.58
  1.0 0.5 collective-permute-done
  1.4 0.0 copy-start.5
  1.4 0.9 %fusion = bf16[192,512]{1,0:T(8,128)(2,1)S(1)} fusion(pred[192]{0:T(512)(128)(4,1)S(1)} %broadcast_in_dim.58, pred[192]{0:T(512)(128)(4,1)S(1)} %broadcast_in_dim.53, bf16[2,24,512]{2,1,0:T(8,128)(2,1)S(1)} %collective-permute-done, bf16[2,24,512]{2,1,0:T(8,128)(2,1)} %param.6), kind=kLoop, calls=%fused_computation.1 | loop fusion | flops 196608 | bytes 295296 | tf_op jit(solution)/shard_map/jit(_where)/select_n | solution.py:250
  2.4 4.2 %collective-permute-start.2 = (bf16[192,512]{1,0:T(8,128)(2,1)S(1)}, bf16[192,512]{1,0:T(8,128)(2,1)S(1)}, u32[]{:S(2)}, u32[]{:S(2)}) collective-permute-start(bf16[192,512]{1,0:T(8,128)(2,1)S(1)} %fusion), channel_id=1, source_target_pairs={{0,24},{4,100},{8,0},{12,108},{16,8},{20,116},{24,16},{28,124},{32... | collective-permute-start | bytes 589832 | tf_op jit(solution)/shard_map/ppermute | solution.py:227
  6.6 0.0 collective-permute-start.3
  6.6 1.3 %collective-permute-start.1 = (bf16[192,512]{1,0:T(8,128)(2,1)S(1)}, bf16[192,512]{1,0:T(8,128)(2,1)S(1)}, u32[]{:S(2)}, u32[]{:S(2)}) collective-permute-start(bf16[192,512]{1,0:T(8,128)(2,1)S(1)} %fusion), channel_id=1, source_target_pairs={{0,8},{4,36},{8,16},{12,44},{16,24},{20,52},{24,0},{28,60},{32,40}... | collective-permute-start | bytes 589832 | tf_op jit(solution)/shard_map/ppermute | solution.py:227
  7.9 0.0 copy-done.5
  7.9 0.0 copy-start
  7.9 0.7 %copy-done = s32[64,24]{0,1:T(8,128)S(1)} copy-done((s32[64,24]{0,1:T(8,128)S(1)}, s32[64,24]{0,1:T(8,128)}, u32[]{:S(2)}) %copy-start) | copy-done | bytes 6168
  8.6 0.0 copy-start.1
  8.6 0.7 %copy-done.1 = s32[4]{0:T(128)S(1)} copy-done((s32[4]{0:T(128)S(1)}, s32[4]{0:T(128)}, u32[]{:S(2)}) %copy-start.1) | copy-done | bytes 40
  9.2 0.0 copy-start.4
  9.2 0.0 copy-start.6
  9.2 8.1 %gather_rows.1 = (f32[192,32,128]{2,1,0:T(8,128)S(1)}, bf16[768,128]{1,0:T(8,128)(2,1)S(1)}) custom-call(s32[4]{0:T(128)S(1)} %copy-done.1, s32[24,64]{1,0:T(8,128)S(1)} %bitcast.15, bf16[250,32,8,128]{3,2,1,0:T(8,128)(2,1)} %bitcast.16), custom_call_target="tpu_custom_call" | custom-call | tf_op jit(solution)/shard_map/gather_rows/pallas_call | solution.py:168
  17.4 0.0 copy-start.2
  17.4 0.0 copy-start.3
  17.4 1.3 %collective-permute-start.7 = (bf16[768,128]{1,0:T(8,128)(2,1)S(1)}, bf16[768,128]{1,0:T(8,128)(2,1)S(1)}, u32[]{:S(2)}, u32[]{:S(2)}) collective-permute-start(bf16[768,128]{1,0:T(8,128)(2,1)S(1)} %get-tuple-element.14), channel_id=1, source_target_pairs={{4,0},{8,4},{12,8},{16,12},{20,16},{24,20},{28,24},{32,28},{36,32}... | collective-permute-start | bytes 589832 | tf_op jit(solution)/shard_map/ppermute | solution.py:253
  18.7 0.0 collective-permute-done.2
  18.7 0.0 collective-permute-done.3
  18.7 0.0 collective-permute-done.1
  18.7 0.0 copy-done.4
  18.8 0.0 copy-done.6
  18.8 0.8 %add_add_fusion.1 = bf16[192,512]{1,0:T(8,128)(2,1)} fusion(bf16[192,512]{1,0:T(8,128)(2,1)S(1)} %collective-permute-done.3, bf16[192,512]{1,0:T(8,128)(2,1)S(1)} %collective-permute-done.2, bf16[192,512]{1,0:T(8,128)(2,1)S(1)} %collective-permute-done.1, bf16[2,24,512]{2,1,0:T(8,128)(2,1)S(1)} %copy-done.6, pred[192]{0:T(512)(128)(4,1)S(1)} %broadcast_in_dim.58, ...), kind=kLoop, calls=%fused_computation.3 | loop fusion | flops 491520 | bytes 885120 | tf_op jit(solution)/shard_map/add | solution.py:233
  19.6 6.3 %collective-permute-start.6 = (bf16[192,512]{1,0:T(8,128)(2,1)}, bf16[192,512]{1,0:T(8,128)(2,1)}, u32[]{:S(2)}, u32[]{:S(2)}) collective-permute-start(bf16[192,512]{1,0:T(8,128)(2,1)} %add_add_fusion.1), channel_id=1, source_target_pairs={{0,64},{4,20},{8,72},{12,28},{16,80},{20,4},{24,88},{28,12},{32,96... | collective-permute-start | bytes 589832 | tf_op jit(solution)/shard_map/ppermute | solution.py:227
  25.8 0.7 %collective-permute-start.5 = (bf16[192,512]{1,0:T(8,128)(2,1)}, bf16[192,512]{1,0:T(8,128)(2,1)}, u32[]{:S(2)}, u32[]{:S(2)}) collective-permute-start(bf16[192,512]{1,0:T(8,128)(2,1)} %add_add_fusion.1), channel_id=1, source_target_pairs={{0,96},{4,28},{8,104},{12,4},{16,112},{20,12},{24,120},{28,20},{32... | collective-permute-start | bytes 589832 | tf_op jit(solution)/shard_map/ppermute | solution.py:227
  26.6 1.3 %collective-permute-start.4 = (bf16[192,512]{1,0:T(8,128)(2,1)}, bf16[192,512]{1,0:T(8,128)(2,1)}, u32[]{:S(2)}, u32[]{:S(2)}) collective-permute-start(bf16[192,512]{1,0:T(8,128)(2,1)} %add_add_fusion.1), channel_id=1, source_target_pairs={{0,32},{4,12},{8,40},{12,20},{16,48},{20,28},{24,56},{28,4},{32,64... | collective-permute-start | bytes 589832 | tf_op jit(solution)/shard_map/ppermute | solution.py:227
  27.9 0.0 collective-permute-done.7.halo
  27.9 5.5 %window_energy.1 = (f32[192,32,128]{2,1,0:T(8,128)S(1)}, bf16[192,96,128]{2,1,0:T(8,128)(2,1)S(1)}) custom-call(f32[192,32,128]{2,1,0:T(8,128)S(1)} %get-tuple-element.13.y, bf16[768,128]{1,0:T(8,128)(2,1)S(1)} %collective-permute-done.7.halo), custom_call_target="tpu_custom_call" | custom-call | tf_op jit(solution)/shard_map/window_energy/pallas_call | solution.py:188
  33.4 0.0 collective-permute-done.6
  33.4 0.0 collective-permute-done.5
  33.4 0.4 collective-permute-done.4
  33.8 1.3 %add_add_fusion.w = bf16[192,512]{1,0:T(8,128)(2,1)S(1)} fusion(bf16[192,512]{1,0:T(8,128)(2,1)} %collective-permute-done.6, bf16[192,512]{1,0:T(8,128)(2,1)} %collective-permute-done.5, bf16[192,512]{1,0:T(8,128)(2,1)} %add_add_fusion.1, bf16[192,512]{1,0:T(8,128)(2,1)} %collective-permute-done.4), kind=kLoop, calls=%fused_computation.2 | loop fusion | flops 294912 | bytes 983040 | tf_op jit(solution)/shard_map/add | solution.py:233
  35.0 0.0 copy-done.2
  35.1 0.0 copy-done.3
  35.1 10.7 %correlate.1 = (f32[8,1024]{1,0:T(8,128)S(1)}, f32[8,1024]{1,0:T(8,128)S(1)}, f32[8,1024]{1,0:T(8,128)S(1)}, f32[8,1024]{1,0:T(8,128)S(1)}) custom-call(s32[4]{0:T(128)S(1)} %copy-done.2, s32[64]{0:T(128)S(1)} %copy-done.3, s32[1]{0:T(128)} %bitcast.place, bf16[192,512]{1,0:T(8,128)(2,1)S(1)} %add_add_fusion.w, ...), custom_call_target="tpu_custom_call" | custom-call | tf_op jit(solution)/shard_map/correlate/pallas_call | solution.py:207
  45.8 1.6 %collective-permute-start.8 = (f32[8,1024]{1,0:T(8,128)S(1)}, f32[8,1024]{1,0:T(8,128)S(1)}, u32[]{:S(2)}, u32[]{:S(2)}) collective-permute-start(f32[8,1024]{1,0:T(8,128)S(1)} %get-tuple-element.18), channel_id=1, source_target_pairs={{0,1},{1,2},{2,3},{3,0},{4,5},{5,6},{6,7},{7,4},{8,9},{9,10},{10,1... | collective-permute-start | bytes 98312 | tf_op jit(solution)/shard_map/ppermute | solution.py:259
  47.4 2.7 %collective-permute-start.9 = (f32[8,1024]{1,0:T(8,128)S(1)}, f32[8,1024]{1,0:T(8,128)S(1)}, u32[]{:S(2)}, u32[]{:S(2)}) collective-permute-start(f32[8,1024]{1,0:T(8,128)S(1)} %get-tuple-element.19), channel_id=1, source_target_pairs={{0,2},{1,3},{2,0},{3,1},{4,6},{5,7},{6,4},{7,5},{8,10},{9,11},{10,... | collective-permute-start | bytes 98312 | tf_op jit(solution)/shard_map/ppermute | solution.py:259
  50.1 1.4 %collective-permute-start.10 = (f32[8,1024]{1,0:T(8,128)S(1)}, f32[8,1024]{1,0:T(8,128)S(1)}, u32[]{:S(2)}, u32[]{:S(2)}) collective-permute-start(f32[8,1024]{1,0:T(8,128)S(1)} %get-tuple-element.20), channel_id=1, source_target_pairs={{0,3},{1,0},{2,1},{3,2},{4,7},{5,4},{6,5},{7,6},{8,11},{9,8},{10,9... | collective-permute-start | bytes 98312 | tf_op jit(solution)/shard_map/ppermute | solution.py:259
  51.5 0.0 collective-permute-done.8
  51.5 1.2 %collective-permute-done.9 = f32[8,1024]{1,0:T(8,128)S(1)} collective-permute-done((f32[8,1024]{1,0:T(8,128)S(1)}, f32[8,1024]{1,0:T(8,128)S(1)}, u32[]{:S(2)}, u32[]{:S(2)}) %collective-permute-start.9) | collective-permute-done | bytes 32800 | tf_op jit(solution)/shard_map/ppermute | solution.py:259
  52.8 1.2 %collective-permute-done.10 = f32[8,1024]{1,0:T(8,128)S(1)} collective-permute-done((f32[8,1024]{1,0:T(8,128)S(1)}, f32[8,1024]{1,0:T(8,128)S(1)}, u32[]{:S(2)}, u32[]{:S(2)}) %collective-permute-start.10) | collective-permute-done | bytes 32800 | tf_op jit(solution)/shard_map/ppermute | solution.py:259
  54.0 0.6 %add_add_fusion.2 = f32[8,1024]{1,0:T(8,128)} fusion(f32[8,1024]{1,0:T(8,128)S(1)} %collective-permute-done.10, f32[8,1024]{1,0:T(8,128)S(1)} %collective-permute-done.9, f32[8,1024]{1,0:T(8,128)S(1)} %get-tuple-element.17, f32[8,1024]{1,0:T(8,128)S(1)} %collective-permute-done.8), kind=kLoop, calls=%fused_computation.4 | loop fusion | flops 24576 | bytes 163840 | tf_op jit(solution)/shard_map/add | solution.py:259
Async XLA Ops:
  0.0 1.4 %collective-permute-start = (bf16[2,24,512]{2,1,0:T(8,128)(2,1)}, bf16[2,24,512]{2,1,0:T(8,128)(2,1)S(1)}, u32[]{:S(2)}, u32[]{:S(2)}) collective-permute-start(bf16[2,24,512]{2,1,0:T(8,128)(2,1)} %param.6), channel_id=1, source_target_pairs={{0,4},{4,0},{8,12},{12,8},{16,20},{20,16},{24,28},{28,24},{32,36},... | collective-permute-start | bytes 147464 | tf_op jit(solution)/shard_map/ppermute | solution.py:227
  1.4 6.4 %copy-start.5 = (bf16[2,24,512]{2,1,0:T(8,128)(2,1)}, bf16[2,24,512]{2,1,0:T(8,128)(2,1)S(1)}, u32[]{:S(2)}) copy-start(bf16[2,24,512]{2,1,0:T(8,128)(2,1)S(1)} %collective-permute-done) | copy-start | bytes 147460
  2.4 16.3 %collective-permute-start.2 = (bf16[192,512]{1,0:T(8,128)(2,1)S(1)}, bf16[192,512]{1,0:T(8,128)(2,1)S(1)}, u32[]{:S(2)}, u32[]{:S(2)}) collective-permute-start(bf16[192,512]{1,0:T(8,128)(2,1)S(1)} %fusion), channel_id=1, source_target_pairs={{0,24},{4,100},{8,0},{12,108},{16,8},{20,116},{24,16},{28,124},{32... | collective-permute-start | bytes 589832 | tf_op jit(solution)/shard_map/ppermute | solution.py:227
  6.6 12.1 %collective-permute-start.3 = (bf16[192,512]{1,0:T(8,128)(2,1)S(1)}, bf16[192,512]{1,0:T(8,128)(2,1)S(1)}, u32[]{:S(2)}, u32[]{:S(2)}) collective-permute-start(bf16[192,512]{1,0:T(8,128)(2,1)S(1)} %fusion), channel_id=1, source_target_pairs={{0,16},{4,68},{8,24},{12,76},{16,0},{20,84},{24,8},{28,92},{32,48}... | collective-permute-start | bytes 589832 | tf_op jit(solution)/shard_map/ppermute | solution.py:227
  6.6 12.1 %collective-permute-start.1 = (bf16[192,512]{1,0:T(8,128)(2,1)S(1)}, bf16[192,512]{1,0:T(8,128)(2,1)S(1)}, u32[]{:S(2)}, u32[]{:S(2)}) collective-permute-start(bf16[192,512]{1,0:T(8,128)(2,1)S(1)} %fusion), channel_id=1, source_target_pairs={{0,8},{4,36},{8,16},{12,44},{16,24},{20,52},{24,0},{28,60},{32,40}... | collective-permute-start | bytes 589832 | tf_op jit(solution)/shard_map/ppermute | solution.py:227
  7.9 0.7 %copy-start = (s32[64,24]{0,1:T(8,128)S(1)}, s32[64,24]{0,1:T(8,128)}, u32[]{:S(2)}) copy-start(s32[64,24]{0,1:T(8,128)} %param.7) | copy-start | bytes 18436
  8.6 0.7 %copy-start.1 = (s32[4]{0:T(128)S(1)}, s32[4]{0:T(128)}, u32[]{:S(2)}) copy-start(s32[4]{0:T(128)} %owner.3) | copy-start | bytes 52
  9.2 9.5 %copy-start.4 = (bf16[2,24,512]{2,1,0:T(8,128)(2,1)S(1)}, bf16[2,24,512]{2,1,0:T(8,128)(2,1)}, u32[]{:S(2)}) copy-start(bf16[2,24,512]{2,1,0:T(8,128)(2,1)} %param.6) | copy-start | bytes 147460
  9.2 9.5 %copy-start.6 = (bf16[2,24,512]{2,1,0:T(8,128)(2,1)S(1)}, bf16[2,24,512]{2,1,0:T(8,128)(2,1)}, u32[]{:S(2)}) copy-start(bf16[2,24,512]{2,1,0:T(8,128)(2,1)} %copy-done.5) | copy-start | bytes 147460
  17.4 17.7 %copy-start.2 = (s32[4]{0:T(128)S(1)}, s32[4]{0:T(128)}, u32[]{:S(2)}) copy-start(s32[4]{0:T(128)} %owner.3) | copy-start | bytes 52
  17.4 17.7 %copy-start.3 = (s32[64]{0:T(128)S(1)}, s32[64]{0:T(128)}, u32[]{:S(2)}) copy-start(s32[64]{0:T(128)} %counts.1) | copy-start | bytes 772
  17.4 10.5 %collective-permute-start.7 = (bf16[768,128]{1,0:T(8,128)(2,1)S(1)}, bf16[768,128]{1,0:T(8,128)(2,1)S(1)}, u32[]{:S(2)}, u32[]{:S(2)}) collective-permute-start(bf16[768,128]{1,0:T(8,128)(2,1)S(1)} %get-tuple-element.14), channel_id=1, source_target_pairs={{4,0},{8,4},{12,8},{16,12},{20,16},{24,20},{28,24},{32,28},{36,32}... | collective-permute-start | bytes 589832 | tf_op jit(solution)/shard_map/ppermute | solution.py:253
  19.6 13.8 %collective-permute-start.6 = (bf16[192,512]{1,0:T(8,128)(2,1)}, bf16[192,512]{1,0:T(8,128)(2,1)}, u32[]{:S(2)}, u32[]{:S(2)}) collective-permute-start(bf16[192,512]{1,0:T(8,128)(2,1)} %add_add_fusion.1), channel_id=1, source_target_pairs={{0,64},{4,20},{8,72},{12,28},{16,80},{20,4},{24,88},{28,12},{32,96... | collective-permute-start | bytes 589832 | tf_op jit(solution)/shard_map/ppermute | solution.py:227
  25.8 7.6 %collective-permute-start.5 = (bf16[192,512]{1,0:T(8,128)(2,1)}, bf16[192,512]{1,0:T(8,128)(2,1)}, u32[]{:S(2)}, u32[]{:S(2)}) collective-permute-start(bf16[192,512]{1,0:T(8,128)(2,1)} %add_add_fusion.1), channel_id=1, source_target_pairs={{0,96},{4,28},{8,104},{12,4},{16,112},{20,12},{24,120},{28,20},{32... | collective-permute-start | bytes 589832 | tf_op jit(solution)/shard_map/ppermute | solution.py:227
  26.6 7.2 %collective-permute-start.4 = (bf16[192,512]{1,0:T(8,128)(2,1)}, bf16[192,512]{1,0:T(8,128)(2,1)}, u32[]{:S(2)}, u32[]{:S(2)}) collective-permute-start(bf16[192,512]{1,0:T(8,128)(2,1)} %add_add_fusion.1), channel_id=1, source_target_pairs={{0,32},{4,12},{8,40},{12,20},{16,48},{20,28},{24,56},{28,4},{32,64... | collective-permute-start | bytes 589832 | tf_op jit(solution)/shard_map/ppermute | solution.py:227
  45.8 5.7 %collective-permute-start.8 = (f32[8,1024]{1,0:T(8,128)S(1)}, f32[8,1024]{1,0:T(8,128)S(1)}, u32[]{:S(2)}, u32[]{:S(2)}) collective-permute-start(f32[8,1024]{1,0:T(8,128)S(1)} %get-tuple-element.18), channel_id=1, source_target_pairs={{0,1},{1,2},{2,3},{3,0},{4,5},{5,6},{6,7},{7,4},{8,9},{9,10},{10,1... | collective-permute-start | bytes 98312 | tf_op jit(solution)/shard_map/ppermute | solution.py:259
  47.4 5.4 %collective-permute-start.9 = (f32[8,1024]{1,0:T(8,128)S(1)}, f32[8,1024]{1,0:T(8,128)S(1)}, u32[]{:S(2)}, u32[]{:S(2)}) collective-permute-start(f32[8,1024]{1,0:T(8,128)S(1)} %get-tuple-element.19), channel_id=1, source_target_pairs={{0,2},{1,3},{2,0},{3,1},{4,6},{5,7},{6,4},{7,5},{8,10},{9,11},{10,... | collective-permute-start | bytes 98312 | tf_op jit(solution)/shard_map/ppermute | solution.py:259
  50.1 3.9 %collective-permute-start.10 = (f32[8,1024]{1,0:T(8,128)S(1)}, f32[8,1024]{1,0:T(8,128)S(1)}, u32[]{:S(2)}, u32[]{:S(2)}) collective-permute-start(f32[8,1024]{1,0:T(8,128)S(1)} %get-tuple-element.20), channel_id=1, source_target_pairs={{0,3},{1,0},{2,1},{3,2},{4,7},{5,4},{6,5},{7,6},{8,11},{9,8},{10,9... | collective-permute-start | bytes 98312 | tf_op jit(solution)/shard_map/ppermute | solution.py:259

commit v3 on v2

v3 whole, which is shorter than its diff:
```python
import functools

import jax
import jax.numpy as jnp
from jax import lax
from jax.experimental import pallas as pl
from jax.experimental.pallas import tpu as pltpu
from jax.sharding import PartitionSpec as P

bf16, f32, i32 = jnp.bfloat16, jnp.float32, jnp.int32
LANES = 128
FLOOR = 1e-6
GROUP = 8
UNROLL = 12
VMEM_LIMIT = 12 * 1024 * 1024


def in_hbm(x):
    return pltpu.with_memory_space_constraint(x, pltpu.HBM)


def vmem_spec():
    return pl.BlockSpec(memory_space=pltpu.VMEM)


def exact_pair(x):
    hi = x.astype(bf16)
    return hi, (x - hi.astype(f32)).astype(bf16)


def chosen(owner, lists, tpb, t, s):
    return lists[s, owner[lax.div(t, tpb)] * tpb + lax.rem(t, tpb)]


def gather_kernel(tpb, owner, lists, wf, pairs, heads, scr, hs, sem):
    slots = lists.shape[0]
    n = pairs.shape[0]
    hb = heads.shape[0] // n

    def copy(i, c):
        pair = pl.multiple_of((c & 6), 2)
        return pltpu.make_async_copy(wf.at[c >> 3, :, pl.ds(pair, 2), :], pairs.at[i], sem.at[i])

    def start(t, _):
        def one(s, _):
            copy(t * slots + s, chosen(owner, lists, tpb, t, s)).start()
            return 0

        return lax.fori_loop(0, slots, one, 0, unroll=8)

    lax.fori_loop(0, n // slots, start, 0)

    def pick(t, _):
        def group(g, _):
            i = t * slots + g * GROUP
            for k in range(GROUP):
                copy(i + k, 0).wait()
            scr[0 : GROUP * 2 * hb, :] = pairs[pl.ds(i, GROUP), 0:hb].reshape(GROUP * 2 * hb, LANES).astype(f32)
            for k in range(GROUP):
                p = chosen(owner, lists, tpb, t, g * GROUP + k) & 1
                hs[pl.ds((i + k) * hb, hb), :] = scr[pl.ds(2 * hb * k + p, hb, stride=2), :]
            return 0

        return lax.fori_loop(0, slots // GROUP, group, 0)

    lax.fori_loop(0, n // slots, pick, 0)
    heads[...] = hs[...].astype(bf16)


def energy_kernel(tpb, taps, owner, lists, pairs, halo, rn, a, scr, band):
    slots = lists.shape[0]
    n, blocks = rn.shape[0], rn.shape[1]
    tb = taps // LANES
    half = blocks // 2
    l = lax.broadcasted_iota(i32, (LANES, LANES), 0)
    c = lax.broadcasted_iota(i32, (LANES, LANES), 1)
    first = jnp.where(l >= c, 1.0, 0.0).astype(bf16)
    last = jnp.where(l < c, 1.0, 0.0).astype(bf16)
    for k, piece in enumerate((first, first, jnp.ones_like(first), jnp.ones_like(first), last, last)):
        band[LANES * k : LANES * (k + 1), :] = piece

    def template(t, _):
        def group(g, _):
            base = t * slots + g * GROUP
            tails = halo[pl.ds(pl.multiple_of(base * tb, GROUP * tb), GROUP * tb), :].astype(f32)
            lhs = []
            for k in range(GROUP):
                i = base + k
                p = chosen(owner, lists, tpb, t, g * GROUP + k) & 1
                scr[k, 0 : 2 * blocks, :] = pairs[i].reshape(2 * blocks, LANES).astype(f32)
                scr[k, pl.ds(2 * blocks + p, tb, stride=2), :] = tails[tb * k : tb * (k + 1)]
                q = []
                for v in range(tb + 2):
                    x = scr[k, pl.ds(2 * v + p, half, stride=4), :]
                    a[i, half * v : half * (v + 1), :] = x.astype(bf16)
                    q.append(x * x)
                for v in range(2):
                    mid = functools.reduce(jnp.add, [q[v + d] for d in range(1, tb)])
                    lhs.append(jnp.concatenate(sum((exact_pair(z) for z in (q[v], mid, q[v + tb])), ()), axis=1))
            e = jnp.dot(jnp.concatenate(lhs, axis=0), band[...], preferred_element_type=f32)
            e = lax.rsqrt(jnp.maximum(e, taps / 4.0))
            for k in range(GROUP):
                rn[base + k] = e[blocks * k : blocks * (k + 1)]
            return 0

        return lax.fori_loop(0, slots // GROUP, group, 0)

    lax.fori_loop(0, n // slots, template, 0)


def correlate_kernel(tpb, slots, owner, counts, place, w, a, rn, *refs):
    outs, (wr, scale, acc) = refs[:-3], refs[-3:]
    n, taps = w.shape
    tb = taps // LANES
    nt = n // slots
    blocks = rn.shape[1]
    half = blocks // 2
    parts = len(outs)
    group = place[0]
    wf = w[...].astype(f32)
    hi, lo = exact_pair(wf * wf)
    ones = jnp.ones((taps, LANES), bf16)
    power = jnp.dot(hi, ones, preferred_element_type=f32) + jnp.dot(lo, ones, preferred_element_type=f32)
    norm = lax.rsqrt(power + FLOOR)
    slot_ids = lax.broadcasted_iota(i32, (slots, LANES), 0) + group * slots
    for t in range(nt):
        count = counts[owner[t // tpb] * tpb + t % tpb]
        scale[t * slots : (t + 1) * slots, :] = jnp.where(slot_ids < count, norm[t * slots : (t + 1) * slots], 0.0)
    row = lax.broadcasted_iota(i32, (LANES, LANES), 0)
    col = lax.broadcasted_iota(i32, (LANES, LANES), 1)
    flip = jnp.where(row + col == LANES - 1, 1.0, 0.0).astype(bf16)
    for j in range(tb):
        wr[j, 0:n, :] = jnp.dot(w[:, LANES * j : LANES * (j + 1)], flip, preferred_element_type=f32)
    own = row >= col
    zero = jnp.zeros((LANES, LANES), bf16)

    def one(i):
        d = [zero]
        for j in range(tb):
            b = jnp.concatenate([wr[j, pl.ds(i, 8, stride=0), :]] * (LANES // 8), axis=0)
            d.append(pltpu.roll(b, 1, axis=1, stride=1, stride_axis=0).astype(bf16))
        d.append(zero)
        band = jnp.concatenate([jnp.where(own, d[j + 1], d[j]) for j in range(tb + 1)], axis=0)
        x = jnp.concatenate([a[i, half * j : half * (j + 2), :] for j in range(tb + 1)], axis=1)
        out = jnp.dot(x, band, preferred_element_type=f32)
        s = scale[pl.ds(i, 8, stride=0), :]
        return out * rn[i] * jnp.concatenate([s] * (blocks // 8), axis=0)

    def template(t, _):
        r = lax.fori_loop(
            0, slots, lambda k, total: total + one(t * slots + k), jnp.zeros((blocks, LANES), f32), unroll=UNROLL
        )
        for v in range(2):
            acc[pl.ds(v * nt + t, half, stride=2 * nt), :] = r[half * v : half * (v + 1)]
        return 0

    lax.fori_loop(0, nt, template, 0)
    per = blocks // parts
    for k, o in enumerate(outs):
        to = (group + k) % parts
        for b in range(per):
            o[:, LANES * b : LANES * (b + 1)] = acc[pl.ds(pl.multiple_of((to * per + b) * nt, 8), nt), :]


def gather(owner, lists, wf4, tpb, tb):
    slots = lists.shape[0]
    n = owner.shape[0] * tpb * slots
    blocks = wf4.shape[1]
    return pl.pallas_call(
        functools.partial(gather_kernel, tpb),
        out_shape=(pltpu.VMEM((n, blocks, 2, LANES), bf16), jax.ShapeDtypeStruct((n * tb, LANES), bf16)),
        grid_spec=pltpu.PrefetchScalarGridSpec(
            num_scalar_prefetch=2,
            in_specs=[pl.BlockSpec(memory_space=pltpu.HBM)],
            out_specs=(vmem_spec(), vmem_spec()),
            scratch_shapes=[
                pltpu.VMEM((GROUP * 2 * tb + 8, LANES), f32),
                pltpu.VMEM((n * tb, LANES), f32),
                pltpu.SemaphoreType.DMA((n,)),
            ],
        ),
        compiler_params=pltpu.CompilerParams(vmem_limit_bytes=VMEM_LIMIT),
        name="gather_rows",
    )(in_hbm(owner), in_hbm(lists), in_hbm(wf4))


def energy(owner, lists, pairs, halo, tpb, taps):
    n, blocks = pairs.shape[0], pairs.shape[1]
    tb = taps // LANES
    return pl.pallas_call(
        functools.partial(energy_kernel, tpb, taps),
        out_shape=(pltpu.VMEM((n, blocks, LANES), f32), pltpu.VMEM((n, blocks // 2 * (tb + 2), LANES), bf16)),
        grid_spec=pltpu.PrefetchScalarGridSpec(
            num_scalar_prefetch=2,
            in_specs=[vmem_spec(), vmem_spec()],
            out_specs=(vmem_spec(), vmem_spec()),
            scratch_shapes=[
                pltpu.VMEM((GROUP, 2 * (blocks + tb) + 8, LANES), f32),
                pltpu.VMEM((6 * LANES, LANES), bf16),
            ],
        ),
        compiler_params=pltpu.CompilerParams(vmem_limit_bytes=VMEM_LIMIT),
        name="window_energy",
    )(in_hbm(owner), in_hbm(lists), pairs, halo)


def correlate(owner, counts, place, w, a, rn, tpb, slots, parts):
    n, taps = w.shape
    nt = n // slots
    blocks = rn.shape[1]
    return pl.pallas_call(
        functools.partial(correlate_kernel, tpb, slots),
        out_shape=tuple(jax.ShapeDtypeStruct((nt, blocks // parts * LANES), f32) for _ in range(parts)),
        grid_spec=pltpu.PrefetchScalarGridSpec(
            num_scalar_prefetch=3,
            in_specs=[vmem_spec()] * 3,
            out_specs=tuple(vmem_spec() for _ in range(parts)),
            scratch_shapes=[
                pltpu.VMEM((taps // LANES, n + 8, LANES), f32),
                pltpu.VMEM((n + 8, LANES), f32),
                pltpu.VMEM(((blocks + 2) * nt, LANES), f32),
            ],
        ),
        compiler_params=pltpu.CompilerParams(vmem_limit_bytes=VMEM_LIMIT),
        name="correlate",
    )(in_hbm(owner), in_hbm(counts), place, w, a, rn)


def turned(i, dy, dz):
    return ((i // 8 + dy) % 4) * 8 + ((i // 2 + dz) % 4) * 2 + i % 2


def sent(x, to):
    return lax.ppermute(x, "tm", [(i, to(i)) for i in range(32)])


def round_the_ring(x, first):
    total = x
    for k in (1, 3, 2):
        total = total + sent(x, lambda i: turned(i, 0, k) if (i % 2 == 0) == first else turned(i, k, 0))
    return total


def shards(waveforms, templates, channel_lists, channel_counts, owner_rounds):
    c, shard_len = waveforms.shape
    tpb, slots, taps = templates.shape
    rounds = owner_rounds.shape[0]
    n = rounds * tpb * slots
    me = lax.axis_index("tm")
    group = lax.axis_index("tmpl")
    groups = lax.axis_size("tmpl")
    wf4 = waveforms.reshape(c // 8, 8, shard_len // LANES, LANES).transpose(0, 2, 1, 3)
    other = sent(templates, lambda i: i ^ 1)
    owned = (owner_rounds == me)[:, None, None, None]
    paired = (owner_rounds == (me ^ 1))[:, None, None, None]
    nil = jnp.zeros((), templates.dtype)
    waves = jnp.where(owned, templates[None], jnp.where(paired, other[None], nil)).reshape(n, taps)
    waves = round_the_ring(waves, True)
    lists = channel_lists.T
    pairs, heads = gather(owner_rounds, lists, wf4, tpb, taps // LANES)
    heads, waves = lax.optimization_barrier((heads, waves))
    halo = lax.ppermute(heads, "tm", [(i, i - 1) for i in range(1, 32)])
    waves = round_the_ring(waves, False)
    rn, a = energy(owner_rounds, lists, pairs, halo, tpb, taps)
    pieces = correlate(owner_rounds, channel_counts, group.reshape(1), waves, a, rn, tpb, slots, groups)
    out = pieces[0]
    for k in range(1, groups):
        out = out + lax.ppermute(pieces[k], "tmpl", [(i, (i + k) % groups) for i in range(groups)])
    return out


def solution(mesh):
    in_specs = (P(None, "tm"), P("tm", "tmpl", None), P(None, "tmpl"), P(), P())
    return jax.shard_map(shards, mesh=mesh, in_specs=in_specs, out_specs=P(None, ("tm", "tmpl")), check_vma=False)
```

time: 54.9 us -> 55.3 us (level)
  Pallas kernels: 24.4 us -> 26.4 us
  starting transfers between devices: 20.8 us -> 19.1 us
  waiting for transfers between devices: 3.31 us -> 4.73 us
  local copies, waits for them, and re-layouts: 1.71 us -> 0.33 us
    pallas_call x1, Pallas kernels: 5.52 us -> 9.63 us  [energy(): pl.pallas_call(functools.partial(energy_kernel, tpb, taps), out_shape=(pl...]
    pallas_call x1, Pallas kernels: 8.14 us -> 5.93 us  [gather(): pl.pallas_call(functools.partial(gather_kernel, tpb), out_shape=(pltpu.VM...]
    ppermute x7, starting transfers between devices: 13.8 us -> 12.1 us  [sent(): return lax.ppermute(x, 'tm', [(i, to(i)) for i in range(32)])]
    ppermute x7, waiting for transfers between devices: 0.83 us -> 2.24 us  [sent(): return lax.ppermute(x, 'tm', [(i, to(i)) for i in range(32)])]
    unnamed x14 -> x6, local copies, waits for them, and re-layouts: 1.39 us -> 0.01 us
  transfers between devices with their start and end apart: 11 -> 11, of which waited for: 4 -> 5; matrix products, arithmetic and copies ran while one was open for 3% -> 2% of each run, Pallas kernels for 25% -> 28%
where the time goes in v3:
time: 55.3 us; the launch traced here: 55 us
  Pallas kernels  26.4 us (48%)
  starting transfers between devices  19.1 us (35%)
  waiting for transfers between devices  4.73 us (9%)
  other arithmetic  4.28 us (8%)
    ppermute x7, starting transfers between devices, sent(): return lax.ppermute(x, 'tm', [(i, to(i)) for i in range(32)])  12.1 us
    pallas_call x1, Pallas kernels, correlate(): pl.pallas_call(functools.partial(correlate_kernel, tpb, slots), out_shape...  10.9 us
    pallas_call x1, Pallas kernels, energy(): pl.pallas_call(functools.partial(energy_kernel, tpb, taps), out_shape=(pl...  9.63 us
    pallas_call x1, Pallas kernels, gather(): pl.pallas_call(functools.partial(gather_kernel, tpb), out_shape=(pltpu.VM...  5.93 us
    ppermute x3, starting transfers between devices, shards(): lax.ppermute(pieces[k], 'tmpl', [(i, (i + k) % groups) for i in range(gro...  5.72 us
    ppermute x3, waiting for transfers between devices, shards(): lax.ppermute(pieces[k], 'tmpl', [(i, (i + k) % groups) for i in range(gro...  2.49 us
    ppermute x7, waiting for transfers between devices, sent(): return lax.ppermute(x, 'tm', [(i, to(i)) for i in range(32)])  2.24 us
    add x2, other arithmetic, round_the_ring(): total + sent(x, lambda i: turned(i, 0, k) if (i % 2 == 0) == first else t...  2.07 us
  transfers between devices with their start and end apart: 11, of which 5 were waited for; matrix products, arithmetic and copies ran while one was open for 2% of the time, Pallas kernels for 28%

profile of v3, /device:TPU:0, one launch (start us, length us, event | category | flops | bytes accessed | tf_op | source)
XLA Modules:
  0.0 55.0 jit_solution(275700492965130171)
XLA Ops:
  0.0 0.0 collective-permute-start
  0.0 0.7 %broadcast_compare_fusion.1 = (pred[4]{0:T(512)(128)(4,1)S(1)}, pred[4]{0:T(512)(128)(4,1)S(1)}) fusion(s32[4]{0:T(128)} %owner.5, s32[]{:T(128)S(6)} %axis_index.25, s32[]{:T(128)S(6)} %xor.3), kind=kLoop, calls=%fused_computation.6 | loop fusion | flops 8 | bytes 32 | tf_op jit(solution)/shard_map/eq | solution.py:254
  0.7 0.1 broadcast_in_dim.52
  0.7 0.1 broadcast_in_dim.53
  0.8 0.1 broadcast_in_dim.57
  0.9 0.1 broadcast_in_dim.58
  1.0 0.5 collective-permute-done
  1.4 0.0 copy-start.1
  1.4 0.9 %fusion = bf16[192,512]{1,0:T(8,128)(2,1)S(1)} fusion(pred[192]{0:T(512)(128)(4,1)S(1)} %broadcast_in_dim.58, pred[192]{0:T(512)(128)(4,1)S(1)} %broadcast_in_dim.53, bf16[2,24,512]{2,1,0:T(8,128)(2,1)S(1)} %collective-permute-done, bf16[2,24,512]{2,1,0:T(8,128)(2,1)} %param.6), kind=kLoop, calls=%fused_computation.1 | loop fusion | flops 196608 | bytes 295296 | tf_op jit(solution)/shard_map/jit(_where)/select_n | solution.py:257
  2.4 4.2 %collective-permute-start.2 = (bf16[192,512]{1,0:T(8,128)(2,1)S(1)}, bf16[192,512]{1,0:T(8,128)(2,1)S(1)}, u32[]{:S(2)}, u32[]{:S(2)}) collective-permute-start(bf16[192,512]{1,0:T(8,128)(2,1)S(1)} %fusion), channel_id=1, source_target_pairs={{0,24},{4,100},{8,0},{12,108},{16,8},{20,116},{24,16},{28,124},{32... | collective-permute-start | bytes 589832 | tf_op jit(solution)/shard_map/ppermute | solution.py:234
  6.6 0.0 collective-permute-start.3
  6.6 1.3 %collective-permute-start.1 = (bf16[192,512]{1,0:T(8,128)(2,1)S(1)}, bf16[192,512]{1,0:T(8,128)(2,1)S(1)}, u32[]{:S(2)}, u32[]{:S(2)}) collective-permute-start(bf16[192,512]{1,0:T(8,128)(2,1)S(1)} %fusion), channel_id=1, source_target_pairs={{0,8},{4,36},{8,16},{12,44},{16,24},{20,52},{24,0},{28,60},{32,40}... | collective-permute-start | bytes 589832 | tf_op jit(solution)/shard_map/ppermute | solution.py:234
  7.9 0.0 copy-done.1
  7.9 0.0 copy-start
  7.9 0.0 copy-start.2
  7.9 5.9 %gather_rows.1 = (bf16[192,32,2,128]{3,2,1,0:T(2,128)(2,1)S(1)}, bf16[768,128]{1,0:T(8,128)(2,1)S(1)}) custom-call(s32[4]{0:T(128)} %owner.5, s32[24,64]{1,0:T(8,128)} %bitcast.16, bf16[250,32,8,128]{3,2,1,0:T(8,128)(2,1)} %bitcast.15), custom_call_target="tpu_custom_call" | custom-call | tf_op jit(solution)/shard_map/gather_rows/pallas_call | solution.py:169
  13.8 0.0 collective-permute-done.2
  13.8 0.1 collective-permute-done.3
  13.9 1.7 %collective-permute-done.1 = bf16[192,512]{1,0:T(8,128)(2,1)S(1)} collective-permute-done((bf16[192,512]{1,0:T(8,128)(2,1)S(1)}, bf16[192,512]{1,0:T(8,128)(2,1)S(1)}, u32[]{:S(2)}, u32[]{:S(2)}) %collective-permute-start.1) | collective-permute-done | bytes 196640 | tf_op jit(solution)/shard_map/ppermute | solution.py:234
  15.6 0.0 copy-done
  15.6 0.0 copy-done.2
  15.6 0.8 %add_add_fusion.1 = bf16[192,512]{1,0:T(8,128)(2,1)} fusion(bf16[192,512]{1,0:T(8,128)(2,1)S(1)} %collective-permute-done.3, bf16[192,512]{1,0:T(8,128)(2,1)S(1)} %collective-permute-done.2, bf16[192,512]{1,0:T(8,128)(2,1)S(1)} %collective-permute-done.1, bf16[2,24,512]{2,1,0:T(8,128)(2,1)S(1)} %copy-done.2, pred[192]{0:T(512)(128)(4,1)S(1)} %broadcast_in_dim.58, ...), kind=kLoop, calls=%fused_computation.3 | loop fusion | flops 491520 | bytes 885120 | tf_op jit(solution)/shard_map/add | solution.py:240
  16.4 1.3 %collective-permute-start.7 = (bf16[768,128]{1,0:T(8,128)(2,1)S(1)}, bf16[768,128]{1,0:T(8,128)(2,1)S(1)}, u32[]{:S(2)}, u32[]{:S(2)}) collective-permute-start(bf16[768,128]{1,0:T(8,128)(2,1)S(1)} %get-tuple-element.18), channel_id=1, source_target_pairs={{4,0},{8,4},{12,8},{16,12},{20,16},{24,20},{28,24},{32,28},{36,32}... | collective-permute-start | bytes 589832 | tf_op jit(solution)/shard_map/ppermute | solution.py:262
  17.7 4.6 %collective-permute-start.6 = (bf16[192,512]{1,0:T(8,128)(2,1)}, bf16[192,512]{1,0:T(8,128)(2,1)}, u32[]{:S(2)}, u32[]{:S(2)}) collective-permute-start(bf16[192,512]{1,0:T(8,128)(2,1)} %add_add_fusion.1), channel_id=1, source_target_pairs={{0,64},{4,20},{8,72},{12,28},{16,80},{20,4},{24,88},{28,12},{32,96... | collective-permute-start | bytes 589832 | tf_op jit(solution)/shard_map/ppermute | solution.py:234
  22.3 1.8 %collective-permute-start.5 = (bf16[192,512]{1,0:T(8,128)(2,1)}, bf16[192,512]{1,0:T(8,128)(2,1)}, u32[]{:S(2)}, u32[]{:S(2)}) collective-permute-start(bf16[192,512]{1,0:T(8,128)(2,1)} %add_add_fusion.1), channel_id=1, source_target_pairs={{0,96},{4,28},{8,104},{12,4},{16,112},{20,12},{24,120},{28,20},{32... | collective-permute-start | bytes 589832 | tf_op jit(solution)/shard_map/ppermute | solution.py:234
  24.2 0.2 collective-permute-start.4
  24.3 0.0 collective-permute-done.7.halo
  24.4 9.6 %window_energy.1 = (f32[192,32,128]{2,1,0:T(8,128)S(1)}, bf16[192,96,128]{2,1,0:T(8,128)(2,1)S(1)}) custom-call(s32[4]{0:T(128)} %owner.5, s32[24,64]{1,0:T(8,128)} %bitcast.17, bf16[192,32,2,128]{3,2,1,0:T(2,128)(2,1)S(1)} %get-tuple-element.17.pairs, bf16[768,128]{1,0:T(8,128)(2,1)S(1)} %collective-permute-done.7.halo), custom_call_target="tpu_custom_call" | custom-call | tf_op jit(solution)/shard_map/window_energy/pallas_call | solution.py:190
  34.0 0.0 collective-permute-done.6
  34.0 0.0 collective-permute-done.5
  34.0 0.0 collective-permute-done.4
  34.0 1.3 %add_add_fusion.w = bf16[192,512]{1,0:T(8,128)(2,1)S(1)} fusion(bf16[192,512]{1,0:T(8,128)(2,1)} %collective-permute-done.6, bf16[192,512]{1,0:T(8,128)(2,1)} %collective-permute-done.5, bf16[192,512]{1,0:T(8,128)(2,1)} %add_add_fusion.1, bf16[192,512]{1,0:T(8,128)(2,1)} %collective-permute-done.4), kind=kLoop, calls=%fused_computation.2 | loop fusion | flops 294912 | bytes 983040 | tf_op jit(solution)/shard_map/add | solution.py:240
  35.3 10.9 %correlate.1 = (f32[8,1024]{1,0:T(8,128)S(1)}, f32[8,1024]{1,0:T(8,128)S(1)}, f32[8,1024]{1,0:T(8,128)S(1)}, f32[8,1024]{1,0:T(8,128)S(1)}) custom-call(s32[4]{0:T(128)} %owner.5, s32[64]{0:T(128)} %counts.1, s32[1]{0:T(128)} %bitcast.place, bf16[192,512]{1,0:T(8,128)(2,1)S(1)} %add_add_fusion.w, bf16[192,96,128]{2,1,0:T(8,128)(2,1)S(1)} %get-tuple-element.19.a, ...), custom_call_target="tpu_custom_call" | custom-call | tf_op jit(solution)/shard_map/correlate/pallas_call | solution.py:211
  46.2 1.6 %collective-permute-start.8 = (f32[8,1024]{1,0:T(8,128)S(1)}, f32[8,1024]{1,0:T(8,128)S(1)}, u32[]{:S(2)}, u32[]{:S(2)}) collective-permute-start(f32[8,1024]{1,0:T(8,128)S(1)} %get-tuple-element.22), channel_id=1, source_target_pairs={{0,1},{1,2},{2,3},{3,0},{4,5},{5,6},{6,7},{7,4},{8,9},{9,10},{10,1... | collective-permute-start | bytes 98312 | tf_op jit(solution)/shard_map/ppermute | solution.py:268
  47.7 2.7 %collective-permute-start.9 = (f32[8,1024]{1,0:T(8,128)S(1)}, f32[8,1024]{1,0:T(8,128)S(1)}, u32[]{:S(2)}, u32[]{:S(2)}) collective-permute-start(f32[8,1024]{1,0:T(8,128)S(1)} %get-tuple-element.23), channel_id=1, source_target_pairs={{0,2},{1,3},{2,0},{3,1},{4,6},{5,7},{6,4},{7,5},{8,10},{9,11},{10,... | collective-permute-start | bytes 98312 | tf_op jit(solution)/shard_map/ppermute | solution.py:268
  50.4 1.4 %collective-permute-start.10 = (f32[8,1024]{1,0:T(8,128)S(1)}, f32[8,1024]{1,0:T(8,128)S(1)}, u32[]{:S(2)}, u32[]{:S(2)}) collective-permute-start(f32[8,1024]{1,0:T(8,128)S(1)} %get-tuple-element.24), channel_id=1, source_target_pairs={{0,3},{1,0},{2,1},{3,2},{4,7},{5,4},{6,5},{7,6},{8,11},{9,8},{10,9... | collective-permute-start | bytes 98312 | tf_op jit(solution)/shard_map/ppermute | solution.py:268
  51.9 0.0 collective-permute-done.8
  51.9 1.3 %collective-permute-done.9 = f32[8,1024]{1,0:T(8,128)S(1)} collective-permute-done((f32[8,1024]{1,0:T(8,128)S(1)}, f32[8,1024]{1,0:T(8,128)S(1)}, u32[]{:S(2)}, u32[]{:S(2)}) %collective-permute-start.9) | collective-permute-done | bytes 32800 | tf_op jit(solution)/shard_map/ppermute | solution.py:268
  53.1 1.2 %collective-permute-done.10 = f32[8,1024]{1,0:T(8,128)S(1)} collective-permute-done((f32[8,1024]{1,0:T(8,128)S(1)}, f32[8,1024]{1,0:T(8,128)S(1)}, u32[]{:S(2)}, u32[]{:S(2)}) %collective-permute-start.10) | collective-permute-done | bytes 32800 | tf_op jit(solution)/shard_map/ppermute | solution.py:268
  54.4 0.6 %add_add_fusion.2 = f32[8,1024]{1,0:T(8,128)} fusion(f32[8,1024]{1,0:T(8,128)S(1)} %collective-permute-done.10, f32[8,1024]{1,0:T(8,128)S(1)} %collective-permute-done.9, f32[8,1024]{1,0:T(8,128)S(1)} %get-tuple-element.21, f32[8,1024]{1,0:T(8,128)S(1)} %collective-permute-done.8), kind=kLoop, calls=%fused_computation.4 | loop fusion | flops 24576 | bytes 163840 | tf_op jit(solution)/shard_map/add | solution.py:268
Async XLA Ops:
  0.0 1.4 %collective-permute-start = (bf16[2,24,512]{2,1,0:T(8,128)(2,1)}, bf16[2,24,512]{2,1,0:T(8,128)(2,1)S(1)}, u32[]{:S(2)}, u32[]{:S(2)}) collective-permute-start(bf16[2,24,512]{2,1,0:T(8,128)(2,1)} %param.6), channel_id=1, source_target_pairs={{0,4},{4,0},{8,12},{12,8},{16,20},{20,16},{24,28},{28,24},{32,36},... | collective-permute-start | bytes 147464 | tf_op jit(solution)/shard_map/ppermute | solution.py:234
  1.4 6.4 %copy-start.1 = (bf16[2,24,512]{2,1,0:T(8,128)(2,1)}, bf16[2,24,512]{2,1,0:T(8,128)(2,1)S(1)}, u32[]{:S(2)}) copy-start(bf16[2,24,512]{2,1,0:T(8,128)(2,1)S(1)} %collective-permute-done) | copy-start | bytes 147460
  2.4 11.4 %collective-permute-start.2 = (bf16[192,512]{1,0:T(8,128)(2,1)S(1)}, bf16[192,512]{1,0:T(8,128)(2,1)S(1)}, u32[]{:S(2)}, u32[]{:S(2)}) collective-permute-start(bf16[192,512]{1,0:T(8,128)(2,1)S(1)} %fusion), channel_id=1, source_target_pairs={{0,24},{4,100},{8,0},{12,108},{16,8},{20,116},{24,16},{28,124},{32... | collective-permute-start | bytes 589832 | tf_op jit(solution)/shard_map/ppermute | solution.py:234
  6.6 7.3 %collective-permute-start.3 = (bf16[192,512]{1,0:T(8,128)(2,1)S(1)}, bf16[192,512]{1,0:T(8,128)(2,1)S(1)}, u32[]{:S(2)}, u32[]{:S(2)}) collective-permute-start(bf16[192,512]{1,0:T(8,128)(2,1)S(1)} %fusion), channel_id=1, source_target_pairs={{0,16},{4,68},{8,24},{12,76},{16,0},{20,84},{24,8},{28,92},{32,48}... | collective-permute-start | bytes 589832 | tf_op jit(solution)/shard_map/ppermute | solution.py:234
  6.6 9.0 %collective-permute-start.1 = (bf16[192,512]{1,0:T(8,128)(2,1)S(1)}, bf16[192,512]{1,0:T(8,128)(2,1)S(1)}, u32[]{:S(2)}, u32[]{:S(2)}) collective-permute-start(bf16[192,512]{1,0:T(8,128)(2,1)S(1)} %fusion), channel_id=1, source_target_pairs={{0,8},{4,36},{8,16},{12,44},{16,24},{20,52},{24,0},{28,60},{32,40}... | collective-permute-start | bytes 589832 | tf_op jit(solution)/shard_map/ppermute | solution.py:234
  7.9 7.7 %copy-start = (bf16[2,24,512]{2,1,0:T(8,128)(2,1)S(1)}, bf16[2,24,512]{2,1,0:T(8,128)(2,1)}, u32[]{:S(2)}) copy-start(bf16[2,24,512]{2,1,0:T(8,128)(2,1)} %param.6) | copy-start | bytes 147460
  7.9 7.7 %copy-start.2 = (bf16[2,24,512]{2,1,0:T(8,128)(2,1)S(1)}, bf16[2,24,512]{2,1,0:T(8,128)(2,1)}, u32[]{:S(2)}) copy-start(bf16[2,24,512]{2,1,0:T(8,128)(2,1)} %copy-done.1) | copy-start | bytes 147460
  16.4 7.9 %collective-permute-start.7 = (bf16[768,128]{1,0:T(8,128)(2,1)S(1)}, bf16[768,128]{1,0:T(8,128)(2,1)S(1)}, u32[]{:S(2)}, u32[]{:S(2)}) collective-permute-start(bf16[768,128]{1,0:T(8,128)(2,1)S(1)} %get-tuple-element.18), channel_id=1, source_target_pairs={{4,0},{8,4},{12,8},{16,12},{20,16},{24,20},{28,24},{32,28},{36,32}... | collective-permute-start | bytes 589832 | tf_op jit(solution)/shard_map/ppermute | solution.py:262
  17.7 16.3 %collective-permute-start.6 = (bf16[192,512]{1,0:T(8,128)(2,1)}, bf16[192,512]{1,0:T(8,128)(2,1)}, u32[]{:S(2)}, u32[]{:S(2)}) collective-permute-start(bf16[192,512]{1,0:T(8,128)(2,1)} %add_add_fusion.1), channel_id=1, source_target_pairs={{0,64},{4,20},{8,72},{12,28},{16,80},{20,4},{24,88},{28,12},{32,96... | collective-permute-start | bytes 589832 | tf_op jit(solution)/shard_map/ppermute | solution.py:234
  22.3 11.7 %collective-permute-start.5 = (bf16[192,512]{1,0:T(8,128)(2,1)}, bf16[192,512]{1,0:T(8,128)(2,1)}, u32[]{:S(2)}, u32[]{:S(2)}) collective-permute-start(bf16[192,512]{1,0:T(8,128)(2,1)} %add_add_fusion.1), channel_id=1, source_target_pairs={{0,96},{4,28},{8,104},{12,4},{16,112},{20,12},{24,120},{28,20},{32... | collective-permute-start | bytes 589832 | tf_op jit(solution)/shard_map/ppermute | solution.py:234
  24.2 9.8 %collective-permute-start.4 = (bf16[192,512]{1,0:T(8,128)(2,1)}, bf16[192,512]{1,0:T(8,128)(2,1)}, u32[]{:S(2)}, u32[]{:S(2)}) collective-permute-start(bf16[192,512]{1,0:T(8,128)(2,1)} %add_add_fusion.1), channel_id=1, source_target_pairs={{0,32},{4,12},{8,40},{12,20},{16,48},{20,28},{24,56},{28,4},{32,64... | collective-permute-start | bytes 589832 | tf_op jit(solution)/shard_map/ppermute | solution.py:234
  46.2 5.7 %collective-permute-start.8 = (f32[8,1024]{1,0:T(8,128)S(1)}, f32[8,1024]{1,0:T(8,128)S(1)}, u32[]{:S(2)}, u32[]{:S(2)}) collective-permute-start(f32[8,1024]{1,0:T(8,128)S(1)} %get-tuple-element.22), channel_id=1, source_target_pairs={{0,1},{1,2},{2,3},{3,0},{4,5},{5,6},{6,7},{7,4},{8,9},{9,10},{10,1... | collective-permute-start | bytes 98312 | tf_op jit(solution)/shard_map/ppermute | solution.py:268
  47.7 5.4 %collective-permute-start.9 = (f32[8,1024]{1,0:T(8,128)S(1)}, f32[8,1024]{1,0:T(8,128)S(1)}, u32[]{:S(2)}, u32[]{:S(2)}) collective-permute-start(f32[8,1024]{1,0:T(8,128)S(1)} %get-tuple-element.23), channel_id=1, source_target_pairs={{0,2},{1,3},{2,0},{3,1},{4,6},{5,7},{6,4},{7,5},{8,10},{9,11},{10,... | collective-permute-start | bytes 98312 | tf_op jit(solution)/shard_map/ppermute | solution.py:268
  50.4 3.9 %collective-permute-start.10 = (f32[8,1024]{1,0:T(8,128)S(1)}, f32[8,1024]{1,0:T(8,128)S(1)}, u32[]{:S(2)}, u32[]{:S(2)}) collective-permute-start(f32[8,1024]{1,0:T(8,128)S(1)} %get-tuple-element.24), channel_id=1, source_target_pairs={{0,3},{1,0},{2,1},{3,2},{4,7},{5,4},{6,5},{7,6},{8,11},{9,8},{10,9... | collective-permute-start | bytes 98312 | tf_op jit(solution)/shard_map/ppermute | solution.py:268

commit v4 on v3

--- a/solution.py
+++ b/solution.py
@@ -23,7 +23,7 @@
     return pl.BlockSpec(memory_space=pltpu.VMEM)
 
 
-def exact_pair(x):
+def two_parts(x):
     hi = x.astype(bf16)
     return hi, (x - hi.astype(f32)).astype(bf16)
 
@@ -74,36 +74,37 @@
     half = blocks // 2
     l = lax.broadcasted_iota(i32, (LANES, LANES), 0)
     c = lax.broadcasted_iota(i32, (LANES, LANES), 1)
-    first = jnp.where(l >= c, 1.0, 0.0).astype(bf16)
-    last = jnp.where(l < c, 1.0, 0.0).astype(bf16)
-    for k, piece in enumerate((first, first, jnp.ones_like(first), jnp.ones_like(first), last, last)):
+    before = jnp.where(l < c, 1.0, 0.0).astype(bf16)
+    for k, piece in enumerate((jnp.ones_like(before), jnp.ones_like(before), before, before)):
         band[LANES * k : LANES * (k + 1), :] = piece
 
     def template(t, _):
-        def group(g, _):
+        def group(g):
             base = t * slots + g * GROUP
             tails = halo[pl.ds(pl.multiple_of(base * tb, GROUP * tb), GROUP * tb), :].astype(f32)
             lhs = []
             for k in range(GROUP):
                 i = base + k
                 p = chosen(owner, lists, tpb, t, g * GROUP + k) & 1
-                scr[k, 0 : 2 * blocks, :] = pairs[i].reshape(2 * blocks, LANES).astype(f32)
-                scr[k, pl.ds(2 * blocks + p, tb, stride=2), :] = tails[tb * k : tb * (k + 1)]
+                scr[g * GROUP + k, 0 : 2 * blocks, :] = pairs[i].astype(f32)
+                scr[g * GROUP + k, pl.ds(2 * blocks + p, tb, stride=2), :] = tails[tb * k : tb * (k + 1)]
                 q = []
                 for v in range(tb + 2):
-                    x = scr[k, pl.ds(2 * v + p, half, stride=4), :]
+                    x = scr[g * GROUP + k, pl.ds(2 * v + p, half, stride=4), :]
                     a[i, half * v : half * (v + 1), :] = x.astype(bf16)
                     q.append(x * x)
+                mid = functools.reduce(jnp.add, q[1:tb])
                 for v in range(2):
-                    mid = functools.reduce(jnp.add, [q[v + d] for d in range(1, tb)])
-                    lhs.append(jnp.concatenate(sum((exact_pair(z) for z in (q[v], mid, q[v + tb])), ()), axis=1))
+                    whole, change = mid + q[v * tb], q[v + tb] - q[v]
+                    lhs.append(jnp.concatenate(two_parts(whole) + two_parts(change), axis=1))
             e = jnp.dot(jnp.concatenate(lhs, axis=0), band[...], preferred_element_type=f32)
             e = lax.rsqrt(jnp.maximum(e, taps / 4.0))
             for k in range(GROUP):
                 rn[base + k] = e[blocks * k : blocks * (k + 1)]
-            return 0
-
-        return lax.fori_loop(0, slots // GROUP, group, 0)
+
+        for g in range(slots // GROUP):
+            group(g)
+        return 0
 
     lax.fori_loop(0, n // slots, template, 0)
 
@@ -118,7 +119,7 @@
     parts = len(outs)
     group = place[0]
     wf = w[...].astype(f32)
-    hi, lo = exact_pair(wf * wf)
+    hi, lo = two_parts(wf * wf)
     ones = jnp.ones((taps, LANES), bf16)
     power = jnp.dot(hi, ones, preferred_element_type=f32) + jnp.dot(lo, ones, preferred_element_type=f32)
     norm = lax.rsqrt(power + FLOOR)
@@ -185,7 +186,7 @@
 
 
 def energy(owner, lists, pairs, halo, tpb, taps):
-    n, blocks = pairs.shape[0], pairs.shape[1]
+    n, blocks = pairs.shape[0], pairs.shape[1] // 2
     tb = taps // LANES
     return pl.pallas_call(
         functools.partial(energy_kernel, tpb, taps),
@@ -195,8 +196,8 @@
             in_specs=[vmem_spec(), vmem_spec()],
             out_specs=(vmem_spec(), vmem_spec()),
             scratch_shapes=[
-                pltpu.VMEM((GROUP, 2 * (blocks + tb) + 8, LANES), f32),
-                pltpu.VMEM((6 * LANES, LANES), bf16),
+                pltpu.VMEM((lists.shape[0], 2 * (blocks + tb) + 8, LANES), f32),
+                pltpu.VMEM((4 * LANES, LANES), bf16),
             ],
         ),
         compiler_params=pltpu.CompilerParams(vmem_limit_bytes=VMEM_LIMIT),
@@ -258,6 +259,7 @@
     waves = round_the_ring(waves, True)
     lists = channel_lists.T
     pairs, heads = gather(owner_rounds, lists, wf4, tpb, taps // LANES)
+    pairs = pairs.reshape(n, -1, LANES)
     heads, waves = lax.optimization_barrier((heads, waves))
     halo = lax.ppermute(heads, "tm", [(i, i - 1) for i in range(1, 32)])
     waves = round_the_ring(waves, False)

time: 55.3 us -> 52.7 us (0.953)
  Pallas kernels: 26.4 us -> 22.3 us
  waiting for transfers between devices: 4.73 us -> 6.24 us
    pallas_call x1, Pallas kernels: 9.63 us -> 5.47 us  [energy(): pl.pallas_call(functools.partial(energy_kernel, tpb, taps), out_shape=(pl...]
    ppermute x7, waiting for transfers between devices: 2.24 us -> 3.76 us  [sent(): return lax.ppermute(x, 'tm', [(i, to(i)) for i in range(32)])]
  transfers between devices with their start and end apart: 11 -> 11, of which waited for: 5 -> 7; matrix products, arithmetic and copies ran while one was open for 2% -> 2% of each run, Pallas kernels for 28% -> 22%
where the time goes in v4:
time: 52.7 us; the launch traced here: 52.3 us
  Pallas kernels  22.3 us (42%)
  starting transfers between devices  19.1 us (36%)
  waiting for transfers between devices  6.24 us (12%)
  other arithmetic  4.28 us (8%)
    ppermute x7, starting transfers between devices, sent(): return lax.ppermute(x, 'tm', [(i, to(i)) for i in range(32)])  12.1 us
    pallas_call x1, Pallas kernels, correlate(): pl.pallas_call(functools.partial(correlate_kernel, tpb, slots), out_shape...  10.9 us
    pallas_call x1, Pallas kernels, gather(): pl.pallas_call(functools.partial(gather_kernel, tpb), out_shape=(pltpu.VM...  5.93 us
    ppermute x3, starting transfers between devices, shards(): lax.ppermute(pieces[k], 'tmpl', [(i, (i + k) % groups) for i in range(gro...  5.72 us
    pallas_call x1, Pallas kernels, energy(): pl.pallas_call(functools.partial(energy_kernel, tpb, taps), out_shape=(pl...  5.47 us
    ppermute x7, waiting for transfers between devices, sent(): return lax.ppermute(x, 'tm', [(i, to(i)) for i in range(32)])  3.76 us
    ppermute x3, waiting for transfers between devices, shards(): lax.ppermute(pieces[k], 'tmpl', [(i, (i + k) % groups) for i in range(gro...  2.48 us
    add x2, other arithmetic, round_the_ring(): total + sent(x, lambda i: turned(i, 0, k) if (i % 2 == 0) == first else t...  2.06 us
  transfers between devices with their start and end apart: 11, of which 7 were waited for; matrix products, arithmetic and copies ran while one was open for 2% of the time, Pallas kernels for 22%

profile of v4, /device:TPU:0, one launch (start us, length us, event | category | flops | bytes accessed | tf_op | source)
XLA Modules:
  0.0 52.3 jit_solution(13543674283410858542)
XLA Ops:
  0.0 0.0 collective-permute-start
  0.0 0.7 %broadcast_compare_fusion.1 = (pred[4]{0:T(512)(128)(4,1)S(1)}, pred[4]{0:T(512)(128)(4,1)S(1)}) fusion(s32[4]{0:T(128)} %owner.5, s32[]{:T(128)S(6)} %axis_index.25, s32[]{:T(128)S(6)} %xor.3), kind=kLoop, calls=%fused_computation.6 | loop fusion | flops 8 | bytes 32 | tf_op jit(solution)/shard_map/eq | solution.py:255
  0.7 0.1 broadcast_in_dim.52
  0.7 0.1 broadcast_in_dim.53
  0.8 0.1 broadcast_in_dim.57
  0.9 0.1 broadcast_in_dim.58
  1.0 0.5 collective-permute-done
  1.4 0.0 copy-start.1
  1.4 0.9 %fusion = bf16[192,512]{1,0:T(8,128)(2,1)S(1)} fusion(pred[192]{0:T(512)(128)(4,1)S(1)} %broadcast_in_dim.58, pred[192]{0:T(512)(128)(4,1)S(1)} %broadcast_in_dim.53, bf16[2,24,512]{2,1,0:T(8,128)(2,1)S(1)} %collective-permute-done, bf16[2,24,512]{2,1,0:T(8,128)(2,1)} %param.6), kind=kLoop, calls=%fused_computation.1 | loop fusion | flops 196608 | bytes 295296 | tf_op jit(solution)/shard_map/jit(_where)/select_n | solution.py:258
  2.4 4.2 %collective-permute-start.2 = (bf16[192,512]{1,0:T(8,128)(2,1)S(1)}, bf16[192,512]{1,0:T(8,128)(2,1)S(1)}, u32[]{:S(2)}, u32[]{:S(2)}) collective-permute-start(bf16[192,512]{1,0:T(8,128)(2,1)S(1)} %fusion), channel_id=1, source_target_pairs={{0,24},{4,100},{8,0},{12,108},{16,8},{20,116},{24,16},{28,124},{32... | collective-permute-start | bytes 589832 | tf_op jit(solution)/shard_map/ppermute | solution.py:235
  6.6 0.0 collective-permute-start.3
  6.6 1.3 %collective-permute-start.1 = (bf16[192,512]{1,0:T(8,128)(2,1)S(1)}, bf16[192,512]{1,0:T(8,128)(2,1)S(1)}, u32[]{:S(2)}, u32[]{:S(2)}) collective-permute-start(bf16[192,512]{1,0:T(8,128)(2,1)S(1)} %fusion), channel_id=1, source_target_pairs={{0,8},{4,36},{8,16},{12,44},{16,24},{20,52},{24,0},{28,60},{32,40}... | collective-permute-start | bytes 589832 | tf_op jit(solution)/shard_map/ppermute | solution.py:235
  7.9 0.0 copy-done.1
  7.9 0.0 copy-start
  7.9 0.0 copy-start.2
  7.9 5.9 %gather_rows.1 = (bf16[192,32,2,128]{3,2,1,0:T(2,128)(2,1)S(1)}, bf16[768,128]{1,0:T(8,128)(2,1)S(1)}) custom-call(s32[4]{0:T(128)} %owner.5, s32[24,64]{1,0:T(8,128)} %bitcast.18, bf16[250,32,8,128]{3,2,1,0:T(8,128)(2,1)} %bitcast.17), custom_call_target="tpu_custom_call" | custom-call | tf_op jit(solution)/shard_map/gather_rows/pallas_call | solution.py:170
  13.8 0.0 collective-permute-done.2
  13.8 0.1 collective-permute-done.3
  13.9 1.7 %collective-permute-done.1 = bf16[192,512]{1,0:T(8,128)(2,1)S(1)} collective-permute-done((bf16[192,512]{1,0:T(8,128)(2,1)S(1)}, bf16[192,512]{1,0:T(8,128)(2,1)S(1)}, u32[]{:S(2)}, u32[]{:S(2)}) %collective-permute-start.1) | collective-permute-done | bytes 196640 | tf_op jit(solution)/shard_map/ppermute | solution.py:235
  15.6 0.0 copy-done
  15.6 0.0 copy-done.2
  15.6 0.8 %add_add_fusion.1 = bf16[192,512]{1,0:T(8,128)(2,1)} fusion(bf16[192,512]{1,0:T(8,128)(2,1)S(1)} %collective-permute-done.3, bf16[192,512]{1,0:T(8,128)(2,1)S(1)} %collective-permute-done.2, bf16[192,512]{1,0:T(8,128)(2,1)S(1)} %collective-permute-done.1, bf16[2,24,512]{2,1,0:T(8,128)(2,1)S(1)} %copy-done.2, pred[192]{0:T(512)(128)(4,1)S(1)} %broadcast_in_dim.58, ...), kind=kLoop, calls=%fused_computation.3 | loop fusion | flops 491520 | bytes 885120 | tf_op jit(solution)/shard_map/add | solution.py:241
  16.4 1.3 %collective-permute-start.7 = (bf16[768,128]{1,0:T(8,128)(2,1)S(1)}, bf16[768,128]{1,0:T(8,128)(2,1)S(1)}, u32[]{:S(2)}, u32[]{:S(2)}) collective-permute-start(bf16[768,128]{1,0:T(8,128)(2,1)S(1)} %get-tuple-element.18), channel_id=1, source_target_pairs={{4,0},{8,4},{12,8},{16,12},{20,16},{24,20},{28,24},{32,28},{36,32}... | collective-permute-start | bytes 589832 | tf_op jit(solution)/shard_map/ppermute | solution.py:264
  17.7 4.6 %collective-permute-start.6 = (bf16[192,512]{1,0:T(8,128)(2,1)}, bf16[192,512]{1,0:T(8,128)(2,1)}, u32[]{:S(2)}, u32[]{:S(2)}) collective-permute-start(bf16[192,512]{1,0:T(8,128)(2,1)} %add_add_fusion.1), channel_id=1, source_target_pairs={{0,64},{4,20},{8,72},{12,28},{16,80},{20,4},{24,88},{28,12},{32,96... | collective-permute-start | bytes 589832 | tf_op jit(solution)/shard_map/ppermute | solution.py:235
  22.3 1.8 %collective-permute-start.5 = (bf16[192,512]{1,0:T(8,128)(2,1)}, bf16[192,512]{1,0:T(8,128)(2,1)}, u32[]{:S(2)}, u32[]{:S(2)}) collective-permute-start(bf16[192,512]{1,0:T(8,128)(2,1)} %add_add_fusion.1), channel_id=1, source_target_pairs={{0,96},{4,28},{8,104},{12,4},{16,112},{20,12},{24,120},{28,20},{32... | collective-permute-start | bytes 589832 | tf_op jit(solution)/shard_map/ppermute | solution.py:235
  24.2 0.2 collective-permute-start.4
  24.3 0.0 collective-permute-done.7.halo
  24.4 5.5 %window_energy.1 = (f32[192,32,128]{2,1,0:T(8,128)S(1)}, bf16[192,96,128]{2,1,0:T(8,128)(2,1)S(1)}) custom-call(s32[4]{0:T(128)} %owner.5, s32[24,64]{1,0:T(8,128)} %bitcast.19, bf16[192,64,128]{2,1,0:T(8,128)(2,1)S(1)} %bitcast.16, bf16[768,128]{1,0:T(8,128)(2,1)S(1)} %collective-permute-done.7.halo), custom_call_target="tpu_custom_call" | custom-call | tf_op jit(solution)/shard_map/window_energy/pallas_call | solution.py:191
  29.8 0.0 collective-permute-done.6
  29.8 0.7 %collective-permute-done.5 = bf16[192,512]{1,0:T(8,128)(2,1)} collective-permute-done((bf16[192,512]{1,0:T(8,128)(2,1)}, bf16[192,512]{1,0:T(8,128)(2,1)}, u32[]{:S(2)}, u32[]{:S(2)}) %collective-permute-start.5) | collective-permute-done | bytes 196640 | tf_op jit(solution)/shard_map/ppermute | solution.py:235
  30.6 0.8 %collective-permute-done.4 = bf16[192,512]{1,0:T(8,128)(2,1)} collective-permute-done((bf16[192,512]{1,0:T(8,128)(2,1)}, bf16[192,512]{1,0:T(8,128)(2,1)}, u32[]{:S(2)}, u32[]{:S(2)}) %collective-permute-start.4) | collective-permute-done | bytes 196640 | tf_op jit(solution)/shard_map/ppermute | solution.py:235
  31.4 1.3 %add_add_fusion.w = bf16[192,512]{1,0:T(8,128)(2,1)S(1)} fusion(bf16[192,512]{1,0:T(8,128)(2,1)} %collective-permute-done.6, bf16[192,512]{1,0:T(8,128)(2,1)} %collective-permute-done.5, bf16[192,512]{1,0:T(8,128)(2,1)} %add_add_fusion.1, bf16[192,512]{1,0:T(8,128)(2,1)} %collective-permute-done.4), kind=kLoop, calls=%fused_computation.2 | loop fusion | flops 294912 | bytes 983040 | tf_op jit(solution)/shard_map/add | solution.py:241
  32.6 10.9 %correlate.1 = (f32[8,1024]{1,0:T(8,128)S(1)}, f32[8,1024]{1,0:T(8,128)S(1)}, f32[8,1024]{1,0:T(8,128)S(1)}, f32[8,1024]{1,0:T(8,128)S(1)}) custom-call(s32[4]{0:T(128)} %owner.5, s32[64]{0:T(128)} %counts.1, s32[1]{0:T(128)} %bitcast.place, bf16[192,512]{1,0:T(8,128)(2,1)S(1)} %add_add_fusion.w, bf16[192,96,128]{2,1,0:T(8,128)(2,1)S(1)} %get-tuple-element.19.a, ...), custom_call_target="tpu_custom_call" | custom-call | tf_op jit(solution)/shard_map/correlate/pallas_call | solution.py:212
  43.5 1.6 %collective-permute-start.8 = (f32[8,1024]{1,0:T(8,128)S(1)}, f32[8,1024]{1,0:T(8,128)S(1)}, u32[]{:S(2)}, u32[]{:S(2)}) collective-permute-start(f32[8,1024]{1,0:T(8,128)S(1)} %get-tuple-element.22), channel_id=1, source_target_pairs={{0,1},{1,2},{2,3},{3,0},{4,5},{5,6},{6,7},{7,4},{8,9},{9,10},{10,1... | collective-permute-start | bytes 98312 | tf_op jit(solution)/shard_map/ppermute | solution.py:270
  45.0 2.7 %collective-permute-start.9 = (f32[8,1024]{1,0:T(8,128)S(1)}, f32[8,1024]{1,0:T(8,128)S(1)}, u32[]{:S(2)}, u32[]{:S(2)}) collective-permute-start(f32[8,1024]{1,0:T(8,128)S(1)} %get-tuple-element.23), channel_id=1, source_target_pairs={{0,2},{1,3},{2,0},{3,1},{4,6},{5,7},{6,4},{7,5},{8,10},{9,11},{10,... | collective-permute-start | bytes 98312 | tf_op jit(solution)/shard_map/ppermute | solution.py:270
  47.8 1.4 %collective-permute-start.10 = (f32[8,1024]{1,0:T(8,128)S(1)}, f32[8,1024]{1,0:T(8,128)S(1)}, u32[]{:S(2)}, u32[]{:S(2)}) collective-permute-start(f32[8,1024]{1,0:T(8,128)S(1)} %get-tuple-element.24), channel_id=1, source_target_pairs={{0,3},{1,0},{2,1},{3,2},{4,7},{5,4},{6,5},{7,6},{8,11},{9,8},{10,9... | collective-permute-start | bytes 98312 | tf_op jit(solution)/shard_map/ppermute | solution.py:270
  49.2 0.0 collective-permute-done.8
  49.2 1.2 %collective-permute-done.9 = f32[8,1024]{1,0:T(8,128)S(1)} collective-permute-done((f32[8,1024]{1,0:T(8,128)S(1)}, f32[8,1024]{1,0:T(8,128)S(1)}, u32[]{:S(2)}, u32[]{:S(2)}) %collective-permute-start.9) | collective-permute-done | bytes 32800 | tf_op jit(solution)/shard_map/ppermute | solution.py:270
  50.5 1.2 %collective-permute-done.10 = f32[8,1024]{1,0:T(8,128)S(1)} collective-permute-done((f32[8,1024]{1,0:T(8,128)S(1)}, f32[8,1024]{1,0:T(8,128)S(1)}, u32[]{:S(2)}, u32[]{:S(2)}) %collective-permute-start.10) | collective-permute-done | bytes 32800 | tf_op jit(solution)/shard_map/ppermute | solution.py:270
  51.7 0.6 %add_add_fusion.2 = f32[8,1024]{1,0:T(8,128)} fusion(f32[8,1024]{1,0:T(8,128)S(1)} %collective-permute-done.10, f32[8,1024]{1,0:T(8,128)S(1)} %collective-permute-done.9, f32[8,1024]{1,0:T(8,128)S(1)} %get-tuple-element.21, f32[8,1024]{1,0:T(8,128)S(1)} %collective-permute-done.8), kind=kLoop, calls=%fused_computation.4 | loop fusion | flops 24576 | bytes 163840 | tf_op jit(solution)/shard_map/add | solution.py:270
Async XLA Ops:
  0.0 1.4 %collective-permute-start = (bf16[2,24,512]{2,1,0:T(8,128)(2,1)}, bf16[2,24,512]{2,1,0:T(8,128)(2,1)S(1)}, u32[]{:S(2)}, u32[]{:S(2)}) collective-permute-start(bf16[2,24,512]{2,1,0:T(8,128)(2,1)} %param.6), channel_id=1, source_target_pairs={{0,4},{4,0},{8,12},{12,8},{16,20},{20,16},{24,28},{28,24},{32,36},... | collective-permute-start | bytes 147464 | tf_op jit(solution)/shard_map/ppermute | solution.py:235
  1.4 6.4 %copy-start.1 = (bf16[2,24,512]{2,1,0:T(8,128)(2,1)}, bf16[2,24,512]{2,1,0:T(8,128)(2,1)S(1)}, u32[]{:S(2)}) copy-start(bf16[2,24,512]{2,1,0:T(8,128)(2,1)S(1)} %collective-permute-done) | copy-start | bytes 147460
  2.4 11.4 %collective-permute-start.2 = (bf16[192,512]{1,0:T(8,128)(2,1)S(1)}, bf16[192,512]{1,0:T(8,128)(2,1)S(1)}, u32[]{:S(2)}, u32[]{:S(2)}) collective-permute-start(bf16[192,512]{1,0:T(8,128)(2,1)S(1)} %fusion), channel_id=1, source_target_pairs={{0,24},{4,100},{8,0},{12,108},{16,8},{20,116},{24,16},{28,124},{32... | collective-permute-start | bytes 589832 | tf_op jit(solution)/shard_map/ppermute | solution.py:235
  6.6 7.3 %collective-permute-start.3 = (bf16[192,512]{1,0:T(8,128)(2,1)S(1)}, bf16[192,512]{1,0:T(8,128)(2,1)S(1)}, u32[]{:S(2)}, u32[]{:S(2)}) collective-permute-start(bf16[192,512]{1,0:T(8,128)(2,1)S(1)} %fusion), channel_id=1, source_target_pairs={{0,16},{4,68},{8,24},{12,76},{16,0},{20,84},{24,8},{28,92},{32,48}... | collective-permute-start | bytes 589832 | tf_op jit(solution)/shard_map/ppermute | solution.py:235
  6.6 9.0 %collective-permute-start.1 = (bf16[192,512]{1,0:T(8,128)(2,1)S(1)}, bf16[192,512]{1,0:T(8,128)(2,1)S(1)}, u32[]{:S(2)}, u32[]{:S(2)}) collective-permute-start(bf16[192,512]{1,0:T(8,128)(2,1)S(1)} %fusion), channel_id=1, source_target_pairs={{0,8},{4,36},{8,16},{12,44},{16,24},{20,52},{24,0},{28,60},{32,40}... | collective-permute-start | bytes 589832 | tf_op jit(solution)/shard_map/ppermute | solution.py:235
  7.9 7.7 %copy-start = (bf16[2,24,512]{2,1,0:T(8,128)(2,1)S(1)}, bf16[2,24,512]{2,1,0:T(8,128)(2,1)}, u32[]{:S(2)}) copy-start(bf16[2,24,512]{2,1,0:T(8,128)(2,1)} %param.6) | copy-start | bytes 147460
  7.9 7.7 %copy-start.2 = (bf16[2,24,512]{2,1,0:T(8,128)(2,1)S(1)}, bf16[2,24,512]{2,1,0:T(8,128)(2,1)}, u32[]{:S(2)}) copy-start(bf16[2,24,512]{2,1,0:T(8,128)(2,1)} %copy-done.1) | copy-start | bytes 147460
  16.4 7.9 %collective-permute-start.7 = (bf16[768,128]{1,0:T(8,128)(2,1)S(1)}, bf16[768,128]{1,0:T(8,128)(2,1)S(1)}, u32[]{:S(2)}, u32[]{:S(2)}) collective-permute-start(bf16[768,128]{1,0:T(8,128)(2,1)S(1)} %get-tuple-element.18), channel_id=1, source_target_pairs={{4,0},{8,4},{12,8},{16,12},{20,16},{24,20},{28,24},{32,28},{36,32}... | collective-permute-start | bytes 589832 | tf_op jit(solution)/shard_map/ppermute | solution.py:264
  17.7 12.1 %collective-permute-start.6 = (bf16[192,512]{1,0:T(8,128)(2,1)}, bf16[192,512]{1,0:T(8,128)(2,1)}, u32[]{:S(2)}, u32[]{:S(2)}) collective-permute-start(bf16[192,512]{1,0:T(8,128)(2,1)} %add_add_fusion.1), channel_id=1, source_target_pairs={{0,64},{4,20},{8,72},{12,28},{16,80},{20,4},{24,88},{28,12},{32,96... | collective-permute-start | bytes 589832 | tf_op jit(solution)/shard_map/ppermute | solution.py:235
  22.3 8.3 %collective-permute-start.5 = (bf16[192,512]{1,0:T(8,128)(2,1)}, bf16[192,512]{1,0:T(8,128)(2,1)}, u32[]{:S(2)}, u32[]{:S(2)}) collective-permute-start(bf16[192,512]{1,0:T(8,128)(2,1)} %add_add_fusion.1), channel_id=1, source_target_pairs={{0,96},{4,28},{8,104},{12,4},{16,112},{20,12},{24,120},{28,20},{32... | collective-permute-start | bytes 589832 | tf_op jit(solution)/shard_map/ppermute | solution.py:235
  24.2 7.2 %collective-permute-start.4 = (bf16[192,512]{1,0:T(8,128)(2,1)}, bf16[192,512]{1,0:T(8,128)(2,1)}, u32[]{:S(2)}, u32[]{:S(2)}) collective-permute-start(bf16[192,512]{1,0:T(8,128)(2,1)} %add_add_fusion.1), channel_id=1, source_target_pairs={{0,32},{4,12},{8,40},{12,20},{16,48},{20,28},{24,56},{28,4},{32,64... | collective-permute-start | bytes 589832 | tf_op jit(solution)/shard_map/ppermute | solution.py:235
  43.5 5.7 %collective-permute-start.8 = (f32[8,1024]{1,0:T(8,128)S(1)}, f32[8,1024]{1,0:T(8,128)S(1)}, u32[]{:S(2)}, u32[]{:S(2)}) collective-permute-start(f32[8,1024]{1,0:T(8,128)S(1)} %get-tuple-element.22), channel_id=1, source_target_pairs={{0,1},{1,2},{2,3},{3,0},{4,5},{5,6},{6,7},{7,4},{8,9},{9,10},{10,1... | collective-permute-start | bytes 98312 | tf_op jit(solution)/shard_map/ppermute | solution.py:270
  45.0 5.4 %collective-permute-start.9 = (f32[8,1024]{1,0:T(8,128)S(1)}, f32[8,1024]{1,0:T(8,128)S(1)}, u32[]{:S(2)}, u32[]{:S(2)}) collective-permute-start(f32[8,1024]{1,0:T(8,128)S(1)} %get-tuple-element.23), channel_id=1, source_target_pairs={{0,2},{1,3},{2,0},{3,1},{4,6},{5,7},{6,4},{7,5},{8,10},{9,11},{10,... | collective-permute-start | bytes 98312 | tf_op jit(solution)/shard_map/ppermute | solution.py:270
  47.8 3.9 %collective-permute-start.10 = (f32[8,1024]{1,0:T(8,128)S(1)}, f32[8,1024]{1,0:T(8,128)S(1)}, u32[]{:S(2)}, u32[]{:S(2)}) collective-permute-start(f32[8,1024]{1,0:T(8,128)S(1)} %get-tuple-element.24), channel_id=1, source_target_pairs={{0,3},{1,0},{2,1},{3,2},{4,7},{5,4},{6,5},{7,6},{8,11},{9,8},{10,9... | collective-permute-start | bytes 98312 | tf_op jit(solution)/shard_map/ppermute | solution.py:270

commit v5 on v4

--- a/solution.py
+++ b/solution.py
@@ -11,8 +11,8 @@
 LANES = 128
 FLOOR = 1e-6
 GROUP = 8
-UNROLL = 12
-VMEM_LIMIT = 12 * 1024 * 1024
+UNROLL = 24
+VMEM_LIMIT = 6 * 1024 * 1024
 
 
 def in_hbm(x):
@@ -28,8 +28,8 @@
     return hi, (x - hi.astype(f32)).astype(bf16)
 
 
-def chosen(owner, lists, tpb, t, s):
-    return lists[s, owner[lax.div(t, tpb)] * tpb + lax.rem(t, tpb)]
+def template_id(owner, tpb, t):
+    return owner[lax.div(t, tpb)] * tpb + lax.rem(t, tpb)
 
 
 def gather_kernel(tpb, owner, lists, wf, pairs, heads, scr, hs, sem):
@@ -38,30 +38,28 @@
     hb = heads.shape[0] // n
 
     def copy(i, c):
-        pair = pl.multiple_of((c & 6), 2)
+        pair = pl.multiple_of(c & 6, 2)
         return pltpu.make_async_copy(wf.at[c >> 3, :, pl.ds(pair, 2), :], pairs.at[i], sem.at[i])
 
     def start(t, _):
-        def one(s, _):
-            copy(t * slots + s, chosen(owner, lists, tpb, t, s)).start()
-            return 0
-
-        return lax.fori_loop(0, slots, one, 0, unroll=8)
+        tid = template_id(owner, tpb, t)
+        for s in range(slots):
+            copy(t * slots + s, lists[s, tid]).start()
+        return 0
 
     lax.fori_loop(0, n // slots, start, 0)
 
     def pick(t, _):
-        def group(g, _):
+        tid = template_id(owner, tpb, t)
+        for g in range(slots // GROUP):
             i = t * slots + g * GROUP
             for k in range(GROUP):
                 copy(i + k, 0).wait()
-            scr[0 : GROUP * 2 * hb, :] = pairs[pl.ds(i, GROUP), 0:hb].reshape(GROUP * 2 * hb, LANES).astype(f32)
-            for k in range(GROUP):
-                p = chosen(owner, lists, tpb, t, g * GROUP + k) & 1
-                hs[pl.ds((i + k) * hb, hb), :] = scr[pl.ds(2 * hb * k + p, hb, stride=2), :]
-            return 0
-
-        return lax.fori_loop(0, slots // GROUP, group, 0)
+            scr[g, 0 : GROUP * 2 * hb, :] = pairs[pl.ds(i, GROUP), 0:hb].reshape(GROUP * 2 * hb, LANES).astype(f32)
+            for k in range(GROUP):
+                p = lists[g * GROUP + k, tid] & 1
+                hs[pl.ds((i + k) * hb, hb), :] = scr[g, pl.ds(2 * hb * k + p, hb, stride=2), :]
+        return 0
 
     lax.fori_loop(0, n // slots, pick, 0)
     heads[...] = hs[...].astype(bf16)
@@ -79,13 +77,15 @@
         band[LANES * k : LANES * (k + 1), :] = piece
 
     def template(t, _):
+        tid = template_id(owner, tpb, t)
+
         def group(g):
             base = t * slots + g * GROUP
             tails = halo[pl.ds(pl.multiple_of(base * tb, GROUP * tb), GROUP * tb), :].astype(f32)
             lhs = []
             for k in range(GROUP):
                 i = base + k
-                p = chosen(owner, lists, tpb, t, g * GROUP + k) & 1
+                p = lists[g * GROUP + k, tid] & 1
                 scr[g * GROUP + k, 0 : 2 * blocks, :] = pairs[i].astype(f32)
                 scr[g * GROUP + k, pl.ds(2 * blocks + p, tb, stride=2), :] = tails[tb * k : tb * (k + 1)]
                 q = []
@@ -109,8 +109,9 @@
     lax.fori_loop(0, n // slots, template, 0)
 
 
-def correlate_kernel(tpb, slots, owner, counts, place, w, a, rn, *refs):
+def correlate_kernel(tpb, slots, owner, counts, place, w0, w1, w2, w3, a, rn, *refs):
     outs, (wr, scale, acc) = refs[:-3], refs[-3:]
+    w = (w0[...] + w1[...]) + (w2[...] + w3[...])
     n, taps = w.shape
     tb = taps // LANES
     nt = n // slots
@@ -118,7 +119,7 @@
     half = blocks // 2
     parts = len(outs)
     group = place[0]
-    wf = w[...].astype(f32)
+    wf = w.astype(f32)
     hi, lo = two_parts(wf * wf)
     ones = jnp.ones((taps, LANES), bf16)
     power = jnp.dot(hi, ones, preferred_element_type=f32) + jnp.dot(lo, ones, preferred_element_type=f32)
@@ -175,7 +176,7 @@
             in_specs=[pl.BlockSpec(memory_space=pltpu.HBM)],
             out_specs=(vmem_spec(), vmem_spec()),
             scratch_shapes=[
-                pltpu.VMEM((GROUP * 2 * tb + 8, LANES), f32),
+                pltpu.VMEM((slots // GROUP, GROUP * 2 * tb + 8, LANES), f32),
                 pltpu.VMEM((n * tb, LANES), f32),
                 pltpu.SemaphoreType.DMA((n,)),
             ],
@@ -205,8 +206,8 @@
     )(in_hbm(owner), in_hbm(lists), pairs, halo)
 
 
-def correlate(owner, counts, place, w, a, rn, tpb, slots, parts):
-    n, taps = w.shape
+def correlate(owner, counts, place, ws, a, rn, tpb, slots, parts):
+    n, taps = ws[0].shape
     nt = n // slots
     blocks = rn.shape[1]
     return pl.pallas_call(
@@ -214,7 +215,7 @@
         out_shape=tuple(jax.ShapeDtypeStruct((nt, blocks // parts * LANES), f32) for _ in range(parts)),
         grid_spec=pltpu.PrefetchScalarGridSpec(
             num_scalar_prefetch=3,
-            in_specs=[vmem_spec()] * 3,
+            in_specs=[vmem_spec()] * (len(ws) + 2),
             out_specs=tuple(vmem_spec() for _ in range(parts)),
             scratch_shapes=[
                 pltpu.VMEM((taps // LANES, n + 8, LANES), f32),
@@ -224,7 +225,7 @@
         ),
         compiler_params=pltpu.CompilerParams(vmem_limit_bytes=VMEM_LIMIT),
         name="correlate",
-    )(in_hbm(owner), in_hbm(counts), place, w, a, rn)
+    )(in_hbm(owner), in_hbm(counts), place, *ws, a, rn)
 
 
 def turned(i, dy, dz):
@@ -236,10 +237,8 @@
 
 
 def round_the_ring(x, first):
-    total = x
-    for k in (1, 3, 2):
-        total = total + sent(x, lambda i: turned(i, 0, k) if (i % 2 == 0) == first else turned(i, k, 0))
-    return total
+    turn = lambda k: lambda i: turned(i, 0, k) if (i % 2 == 0) == first else turned(i, k, 0)
+    return [x] + [sent(x, turn(k)) for k in (1, 3, 2)]
 
 
 def shards(waveforms, templates, channel_lists, channel_counts, owner_rounds):
@@ -256,7 +255,7 @@
     paired = (owner_rounds == (me ^ 1))[:, None, None, None]
     nil = jnp.zeros((), templates.dtype)
     waves = jnp.where(owned, templates[None], jnp.where(paired, other[None], nil)).reshape(n, taps)
-    waves = round_the_ring(waves, True)
+    waves = functools.reduce(jnp.add, round_the_ring(waves, True))
     lists = channel_lists.T
     pairs, heads = gather(owner_rounds, lists, wf4, tpb, taps // LANES)
     pairs = pairs.reshape(n, -1, LANES)

time: 52.7 us -> 48.4 us (0.918)
  waiting for transfers between devices: 6.24 us -> 3.66 us
  other arithmetic: 4.28 us -> 2.33 us
  Pallas kernels: 22.3 us -> 21.5 us
  starting transfers between devices: 19.1 us -> 19.7 us
    ppermute x7, waiting for transfers between devices: 3.76 us -> 0.47 us  [sent(): return lax.ppermute(x, 'tm', [(i, to(i)) for i in range(32)])]
    add x2 -> x1, other arithmetic: 2.06 us -> 0.13 us  [shards(): waves = functools.reduce(jnp.add, round_the_ring(waves, True))]
    ppermute x7, starting transfers between devices: 12.1 us -> 13.3 us  [sent(): return lax.ppermute(x, 'tm', [(i, to(i)) for i in range(32)])]
    ppermute x3, waiting for transfers between devices: 2.48 us -> 3.18 us  [shards(): lax.ppermute(pieces[k], 'tmpl', [(i, (i + k) % groups) for i in range(gro...]
    ppermute x3, starting transfers between devices: 5.72 us -> 5.12 us  [shards(): lax.ppermute(pieces[k], 'tmpl', [(i, (i + k) % groups) for i in range(gro...]
  transfers between devices with their start and end apart: 11 -> 11, of which waited for: 7 -> 3; matrix products, arithmetic and copies ran while one was open for 2% -> 2% of each run, Pallas kernels for 22% -> 23%
where the time goes in v5:
time: 48.4 us; the launch traced here: 47.6 us
  Pallas kernels  21.5 us (44%)
  starting transfers between devices  19.7 us (41%)
  waiting for transfers between devices  3.66 us (8%)
  other arithmetic  2.33 us (5%)
    ppermute x7, starting transfers between devices, sent(): return lax.ppermute(x, 'tm', [(i, to(i)) for i in range(32)])  13.3 us
    pallas_call x1, Pallas kernels, correlate(): pl.pallas_call(functools.partial(correlate_kernel, tpb, slots), out_shape...  10.3 us
    pallas_call x1, Pallas kernels, energy(): pl.pallas_call(functools.partial(energy_kernel, tpb, taps), out_shape=(pl...  5.59 us
    pallas_call x1, Pallas kernels, gather(): pl.pallas_call(functools.partial(gather_kernel, tpb), out_shape=(pltpu.VM...  5.58 us
    ppermute x3, starting transfers between devices, shards(): lax.ppermute(pieces[k], 'tmpl', [(i, (i + k) % groups) for i in range(gro...  5.12 us
    ppermute x3, waiting for transfers between devices, shards(): lax.ppermute(pieces[k], 'tmpl', [(i, (i + k) % groups) for i in range(gro...  3.18 us
    ppermute x1, starting transfers between devices, shards(): halo = lax.ppermute(heads, 'tm', [(i, i - 1) for i in range(1, 32)])  1.29 us
  transfers between devices with their start and end apart: 11, of which 3 were waited for; matrix products, arithmetic and copies ran while one was open for 2% of the time, Pallas kernels for 23%

profile of v5, /device:TPU:0, one launch (start us, length us, event | category | flops | bytes accessed | tf_op | source)
XLA Modules:
  0.0 47.6 jit_solution(1709354455208769142)
XLA Ops:
  0.0 0.0 collective-permute-start
  0.0 0.7 %broadcast_compare_fusion.1 = (pred[4]{0:T(512)(128)(4,1)S(1)}, pred[4]{0:T(512)(128)(4,1)S(1)}) fusion(s32[4]{0:T(128)} %owner.5, s32[]{:T(128)S(6)} %axis_index.25, s32[]{:T(128)S(6)} %xor.3), kind=kLoop, calls=%fused_computation.5 | loop fusion | flops 8 | bytes 32 | tf_op jit(solution)/shard_map/eq | solution.py:254
  0.7 0.1 broadcast_in_dim.52
  0.7 0.1 broadcast_in_dim.53
  0.8 0.1 broadcast_in_dim.57
  0.9 0.1 broadcast_in_dim.58
  1.0 0.5 collective-permute-done
  1.4 0.9 %fusion = bf16[192,512]{1,0:T(8,128)(2,1)S(1)} fusion(pred[192]{0:T(512)(128)(4,1)S(1)} %broadcast_in_dim.58, pred[192]{0:T(512)(128)(4,1)S(1)} %broadcast_in_dim.53, bf16[2,24,512]{2,1,0:T(8,128)(2,1)S(1)} %collective-permute-done, bf16[2,24,512]{2,1,0:T(8,128)(2,1)} %param.6), kind=kLoop, calls=%fused_computation.1 | loop fusion | flops 196608 | bytes 295296 | tf_op jit(solution)/shard_map/jit(_where)/select_n | solution.py:257
  2.4 2.1 %collective-permute-start.1 = (bf16[192,512]{1,0:T(8,128)(2,1)S(1)}, bf16[192,512]{1,0:T(8,128)(2,1)S(1)}, u32[]{:S(2)}, u32[]{:S(2)}) collective-permute-start(bf16[192,512]{1,0:T(8,128)(2,1)S(1)} %fusion), channel_id=1, source_target_pairs={{0,8},{4,36},{8,16},{12,44},{16,24},{20,52},{24,0},{28,60},{32,40}... | collective-permute-start | bytes 589832 | tf_op jit(solution)/shard_map/ppermute | solution.py:236
  4.5 2.2 %collective-permute-start.2 = (bf16[192,512]{1,0:T(8,128)(2,1)S(1)}, bf16[192,512]{1,0:T(8,128)(2,1)S(1)}, u32[]{:S(2)}, u32[]{:S(2)}) collective-permute-start(bf16[192,512]{1,0:T(8,128)(2,1)S(1)} %fusion), channel_id=1, source_target_pairs={{0,24},{4,100},{8,0},{12,108},{16,8},{20,116},{24,16},{28,124},{32... | collective-permute-start | bytes 589832 | tf_op jit(solution)/shard_map/ppermute | solution.py:236
  6.7 1.8 %collective-permute-start.3 = (bf16[192,512]{1,0:T(8,128)(2,1)S(1)}, bf16[192,512]{1,0:T(8,128)(2,1)S(1)}, u32[]{:S(2)}, u32[]{:S(2)}) collective-permute-start(bf16[192,512]{1,0:T(8,128)(2,1)S(1)} %fusion), channel_id=1, source_target_pairs={{0,16},{4,68},{8,24},{12,76},{16,0},{20,84},{24,8},{28,92},{32,48}... | collective-permute-start | bytes 589832 | tf_op jit(solution)/shard_map/ppermute | solution.py:236
  8.5 0.0 copy-start
  8.5 5.6 %gather_rows.1 = (bf16[192,32,2,128]{3,2,1,0:T(2,128)(2,1)S(1)}, bf16[768,128]{1,0:T(8,128)(2,1)}) custom-call(s32[4]{0:T(128)} %owner.5, s32[24,64]{1,0:T(8,128)} %bitcast.18, bf16[250,32,8,128]{3,2,1,0:T(8,128)(2,1)} %bitcast.17), custom_call_target="tpu_custom_call" | custom-call | tf_op jit(solution)/shard_map/gather_rows/pallas_call | solution.py:171
  14.0 0.0 collective-permute-done.1
  14.1 0.0 collective-permute-done.2
  14.1 0.0 collective-permute-done.3
  14.1 0.0 copy-done
  14.1 0.1 add_add_fusion.w0
  14.2 1.3 %collective-permute-start.7 = (bf16[768,128]{1,0:T(8,128)(2,1)}, bf16[768,128]{1,0:T(8,128)(2,1)S(1)}, u32[]{:S(2)}, u32[]{:S(2)}) collective-permute-start(bf16[768,128]{1,0:T(8,128)(2,1)} %get-tuple-element.18), channel_id=1, source_target_pairs={{4,0},{8,4},{12,8},{16,12},{20,16},{24,20},{28,24},{32,28},{36,32}... | collective-permute-start | bytes 589832 | tf_op jit(solution)/shard_map/ppermute | solution.py:263
  15.5 4.4 %collective-permute-start.4 = (bf16[192,512]{1,0:T(8,128)(2,1)S(1)}, bf16[192,512]{1,0:T(8,128)(2,1)}, u32[]{:S(2)}, u32[]{:S(2)}) collective-permute-start(bf16[192,512]{1,0:T(8,128)(2,1)S(1)} %add_add_fusion.w0), channel_id=1, source_target_pairs={{0,32},{4,12},{8,40},{12,20},{16,48},{20,28},{24,56},{28,4},{32,64... | collective-permute-start | bytes 589832 | tf_op jit(solution)/shard_map/ppermute | solution.py:236
  19.9 0.3 collective-permute-start.5
  20.3 2.4 %collective-permute-start.6 = (bf16[192,512]{1,0:T(8,128)(2,1)S(1)}, bf16[192,512]{1,0:T(8,128)(2,1)}, u32[]{:S(2)}, u32[]{:S(2)}) collective-permute-start(bf16[192,512]{1,0:T(8,128)(2,1)S(1)} %add_add_fusion.w0), channel_id=1, source_target_pairs={{0,64},{4,20},{8,72},{12,28},{16,80},{20,4},{24,88},{28,12},{32,96... | collective-permute-start | bytes 589832 | tf_op jit(solution)/shard_map/ppermute | solution.py:236
  22.7 0.0 collective-permute-done.7.halo
  22.7 5.6 %window_energy.1 = (f32[192,32,128]{2,1,0:T(8,128)S(1)}, bf16[192,96,128]{2,1,0:T(8,128)(2,1)S(1)}) custom-call(s32[4]{0:T(128)} %owner.5, s32[24,64]{1,0:T(8,128)} %bitcast.19, bf16[192,64,128]{2,1,0:T(8,128)(2,1)S(1)} %bitcast.16, bf16[768,128]{1,0:T(8,128)(2,1)S(1)} %collective-permute-done.7.halo), custom_call_target="tpu_custom_call" | custom-call | tf_op jit(solution)/shard_map/window_energy/pallas_call | solution.py:192
  28.3 0.0 collective-permute-done.4.w1
  28.3 0.0 collective-permute-done.5.w2
  28.3 0.0 collective-permute-done.6.w3
  28.3 10.3 %correlate.1 = (f32[8,1024]{1,0:T(8,128)S(1)}, f32[8,1024]{1,0:T(8,128)S(1)}, f32[8,1024]{1,0:T(8,128)S(1)}, f32[8,1024]{1,0:T(8,128)S(1)}) custom-call(s32[4]{0:T(128)} %owner.5, s32[64]{0:T(128)} %counts.1, s32[1]{0:T(128)} %bitcast.place, bf16[192,512]{1,0:T(8,128)(2,1)S(1)} %add_add_fusion.w0, bf16[192,512]{1,0:T(8,128)(2,1)} %collective-permute-done.4.w1, ...), custom_call_target="tpu_custom_call" | custom-call | tf_op jit(solution)/shard_map/correlate/pallas_call | solution.py:213
  38.7 2.8 %collective-permute-start.10 = (f32[8,1024]{1,0:T(8,128)S(1)}, f32[8,1024]{1,0:T(8,128)S(1)}, u32[]{:S(2)}, u32[]{:S(2)}) collective-permute-start(f32[8,1024]{1,0:T(8,128)S(1)} %get-tuple-element.24), channel_id=1, source_target_pairs={{0,3},{1,0},{2,1},{3,2},{4,7},{5,4},{6,5},{7,6},{8,11},{9,8},{10,9... | collective-permute-start | bytes 98312 | tf_op jit(solution)/shard_map/ppermute | solution.py:269
  41.5 0.0 collective-permute-start.8
  41.5 2.3 %collective-permute-start.9 = (f32[8,1024]{1,0:T(8,128)S(1)}, f32[8,1024]{1,0:T(8,128)S(1)}, u32[]{:S(2)}, u32[]{:S(2)}) collective-permute-start(f32[8,1024]{1,0:T(8,128)S(1)} %get-tuple-element.23), channel_id=1, source_target_pairs={{0,2},{1,3},{2,0},{3,1},{4,6},{5,7},{6,4},{7,5},{8,10},{9,11},{10,... | collective-permute-start | bytes 98312 | tf_op jit(solution)/shard_map/ppermute | solution.py:269
  43.8 0.0 collective-permute-done.10
  43.8 2.8 %collective-permute-done.8 = f32[8,1024]{1,0:T(8,128)S(1)} collective-permute-done((f32[8,1024]{1,0:T(8,128)S(1)}, f32[8,1024]{1,0:T(8,128)S(1)}, u32[]{:S(2)}, u32[]{:S(2)}) %collective-permute-start.8) | collective-permute-done | bytes 32800 | tf_op jit(solution)/shard_map/ppermute | solution.py:269
  46.6 0.3 collective-permute-done.9
  47.0 0.6 %add_add_fusion.1 = f32[8,1024]{1,0:T(8,128)} fusion(f32[8,1024]{1,0:T(8,128)S(1)} %collective-permute-done.10, f32[8,1024]{1,0:T(8,128)S(1)} %collective-permute-done.9, f32[8,1024]{1,0:T(8,128)S(1)} %get-tuple-element.21, f32[8,1024]{1,0:T(8,128)S(1)} %collective-permute-done.8), kind=kLoop, calls=%fused_computation.3 | loop fusion | flops 24576 | bytes 163840 | tf_op jit(solution)/shard_map/add | solution.py:269
Async XLA Ops:
  0.0 1.4 %collective-permute-start = (bf16[2,24,512]{2,1,0:T(8,128)(2,1)}, bf16[2,24,512]{2,1,0:T(8,128)(2,1)S(1)}, u32[]{:S(2)}, u32[]{:S(2)}) collective-permute-start(bf16[2,24,512]{2,1,0:T(8,128)(2,1)} %param.6), channel_id=1, source_target_pairs={{0,4},{4,0},{8,12},{12,8},{16,20},{20,16},{24,28},{28,24},{32,36},... | collective-permute-start | bytes 147464 | tf_op jit(solution)/shard_map/ppermute | solution.py:236
  2.4 11.7 %collective-permute-start.1 = (bf16[192,512]{1,0:T(8,128)(2,1)S(1)}, bf16[192,512]{1,0:T(8,128)(2,1)S(1)}, u32[]{:S(2)}, u32[]{:S(2)}) collective-permute-start(bf16[192,512]{1,0:T(8,128)(2,1)S(1)} %fusion), channel_id=1, source_target_pairs={{0,8},{4,36},{8,16},{12,44},{16,24},{20,52},{24,0},{28,60},{32,40}... | collective-permute-start | bytes 589832 | tf_op jit(solution)/shard_map/ppermute | solution.py:236
  4.5 9.6 %collective-permute-start.2 = (bf16[192,512]{1,0:T(8,128)(2,1)S(1)}, bf16[192,512]{1,0:T(8,128)(2,1)S(1)}, u32[]{:S(2)}, u32[]{:S(2)}) collective-permute-start(bf16[192,512]{1,0:T(8,128)(2,1)S(1)} %fusion), channel_id=1, source_target_pairs={{0,24},{4,100},{8,0},{12,108},{16,8},{20,116},{24,16},{28,124},{32... | collective-permute-start | bytes 589832 | tf_op jit(solution)/shard_map/ppermute | solution.py:236
  6.7 7.4 %collective-permute-start.3 = (bf16[192,512]{1,0:T(8,128)(2,1)S(1)}, bf16[192,512]{1,0:T(8,128)(2,1)S(1)}, u32[]{:S(2)}, u32[]{:S(2)}) collective-permute-start(bf16[192,512]{1,0:T(8,128)(2,1)S(1)} %fusion), channel_id=1, source_target_pairs={{0,16},{4,68},{8,24},{12,76},{16,0},{20,84},{24,8},{28,92},{32,48}... | collective-permute-start | bytes 589832 | tf_op jit(solution)/shard_map/ppermute | solution.py:236
  8.5 5.6 %copy-start = (bf16[2,24,512]{2,1,0:T(8,128)(2,1)S(1)}, bf16[2,24,512]{2,1,0:T(8,128)(2,1)}, u32[]{:S(2)}) copy-start(bf16[2,24,512]{2,1,0:T(8,128)(2,1)} %param.6) | copy-start | bytes 147460
  14.2 8.5 %collective-permute-start.7 = (bf16[768,128]{1,0:T(8,128)(2,1)}, bf16[768,128]{1,0:T(8,128)(2,1)S(1)}, u32[]{:S(2)}, u32[]{:S(2)}) collective-permute-start(bf16[768,128]{1,0:T(8,128)(2,1)} %get-tuple-element.18), channel_id=1, source_target_pairs={{4,0},{8,4},{12,8},{16,12},{20,16},{24,20},{28,24},{32,28},{36,32}... | collective-permute-start | bytes 589832 | tf_op jit(solution)/shard_map/ppermute | solution.py:263
  15.5 12.8 %collective-permute-start.4 = (bf16[192,512]{1,0:T(8,128)(2,1)S(1)}, bf16[192,512]{1,0:T(8,128)(2,1)}, u32[]{:S(2)}, u32[]{:S(2)}) collective-permute-start(bf16[192,512]{1,0:T(8,128)(2,1)S(1)} %add_add_fusion.w0), channel_id=1, source_target_pairs={{0,32},{4,12},{8,40},{12,20},{16,48},{20,28},{24,56},{28,4},{32,64... | collective-permute-start | bytes 589832 | tf_op jit(solution)/shard_map/ppermute | solution.py:236
  19.9 8.4 %collective-permute-start.5 = (bf16[192,512]{1,0:T(8,128)(2,1)S(1)}, bf16[192,512]{1,0:T(8,128)(2,1)}, u32[]{:S(2)}, u32[]{:S(2)}) collective-permute-start(bf16[192,512]{1,0:T(8,128)(2,1)S(1)} %add_add_fusion.w0), channel_id=1, source_target_pairs={{0,96},{4,28},{8,104},{12,4},{16,112},{20,12},{24,120},{28,20},{32... | collective-permute-start | bytes 589832 | tf_op jit(solution)/shard_map/ppermute | solution.py:236
  20.3 8.1 %collective-permute-start.6 = (bf16[192,512]{1,0:T(8,128)(2,1)S(1)}, bf16[192,512]{1,0:T(8,128)(2,1)}, u32[]{:S(2)}, u32[]{:S(2)}) collective-permute-start(bf16[192,512]{1,0:T(8,128)(2,1)S(1)} %add_add_fusion.w0), channel_id=1, source_target_pairs={{0,64},{4,20},{8,72},{12,28},{16,80},{20,4},{24,88},{28,12},{32,96... | collective-permute-start | bytes 589832 | tf_op jit(solution)/shard_map/ppermute | solution.py:236
  38.7 5.1 %collective-permute-start.10 = (f32[8,1024]{1,0:T(8,128)S(1)}, f32[8,1024]{1,0:T(8,128)S(1)}, u32[]{:S(2)}, u32[]{:S(2)}) collective-permute-start(f32[8,1024]{1,0:T(8,128)S(1)} %get-tuple-element.24), channel_id=1, source_target_pairs={{0,3},{1,0},{2,1},{3,2},{4,7},{5,4},{6,5},{7,6},{8,11},{9,8},{10,9... | collective-permute-start | bytes 98312 | tf_op jit(solution)/shard_map/ppermute | solution.py:269
  41.5 5.1 %collective-permute-start.8 = (f32[8,1024]{1,0:T(8,128)S(1)}, f32[8,1024]{1,0:T(8,128)S(1)}, u32[]{:S(2)}, u32[]{:S(2)}) collective-permute-start(f32[8,1024]{1,0:T(8,128)S(1)} %get-tuple-element.22), channel_id=1, source_target_pairs={{0,1},{1,2},{2,3},{3,0},{4,5},{5,6},{6,7},{7,4},{8,9},{9,10},{10,1... | collective-permute-start | bytes 98312 | tf_op jit(solution)/shard_map/ppermute | solution.py:269
  41.5 5.5 %collective-permute-start.9 = (f32[8,1024]{1,0:T(8,128)S(1)}, f32[8,1024]{1,0:T(8,128)S(1)}, u32[]{:S(2)}, u32[]{:S(2)}) collective-permute-start(f32[8,1024]{1,0:T(8,128)S(1)} %get-tuple-element.23), channel_id=1, source_target_pairs={{0,2},{1,3},{2,0},{3,1},{4,6},{5,7},{6,4},{7,5},{8,10},{9,11},{10,... | collective-permute-start | bytes 98312 | tf_op jit(solution)/shard_map/ppermute | solution.py:269

commit v6 on v5

--- a/solution.py
+++ b/solution.py
@@ -12,6 +12,7 @@
 FLOOR = 1e-6
 GROUP = 8
 UNROLL = 24
+EACH = 2
 VMEM_LIMIT = 6 * 1024 * 1024
 
 
@@ -76,7 +77,7 @@
     for k, piece in enumerate((jnp.ones_like(before), jnp.ones_like(before), before, before)):
         band[LANES * k : LANES * (k + 1), :] = piece
 
-    def template(t, _):
+    def template(t, at):
         tid = template_id(owner, tpb, t)
 
         def group(g):
@@ -86,11 +87,11 @@
             for k in range(GROUP):
                 i = base + k
                 p = lists[g * GROUP + k, tid] & 1
-                scr[g * GROUP + k, 0 : 2 * blocks, :] = pairs[i].astype(f32)
-                scr[g * GROUP + k, pl.ds(2 * blocks + p, tb, stride=2), :] = tails[tb * k : tb * (k + 1)]
+                scr[at * slots + g * GROUP + k, 0 : 2 * blocks, :] = pairs[i].astype(f32)
+                scr[at * slots + g * GROUP + k, pl.ds(2 * blocks + p, tb, stride=2), :] = tails[tb * k : tb * (k + 1)]
                 q = []
                 for v in range(tb + 2):
-                    x = scr[g * GROUP + k, pl.ds(2 * v + p, half, stride=4), :]
+                    x = scr[at * slots + g * GROUP + k, pl.ds(2 * v + p, half, stride=4), :]
                     a[i, half * v : half * (v + 1), :] = x.astype(bf16)
                     q.append(x * x)
                 mid = functools.reduce(jnp.add, q[1:tb])
@@ -104,9 +105,13 @@
 
         for g in range(slots // GROUP):
             group(g)
-        return 0
-
-    lax.fori_loop(0, n // slots, template, 0)
+
+    def step(u, _):
+        for at in range(EACH):
+            template(u * EACH + at, at)
+        return 0
+
+    lax.fori_loop(0, n // slots // EACH, step, 0)
 
 
 def correlate_kernel(tpb, slots, owner, counts, place, w0, w1, w2, w3, a, rn, *refs):
@@ -197,7 +202,7 @@
             in_specs=[vmem_spec(), vmem_spec()],
             out_specs=(vmem_spec(), vmem_spec()),
             scratch_shapes=[
-                pltpu.VMEM((lists.shape[0], 2 * (blocks + tb) + 8, LANES), f32),
+                pltpu.VMEM((EACH * lists.shape[0], 2 * (blocks + tb) + 8, LANES), f32),
                 pltpu.VMEM((4 * LANES, LANES), bf16),
             ],
         ),
@@ -263,11 +268,12 @@
     halo = lax.ppermute(heads, "tm", [(i, i - 1) for i in range(1, 32)])
     waves = round_the_ring(waves, False)
     rn, a = energy(owner_rounds, lists, pairs, halo, tpb, taps)
-    pieces = correlate(owner_rounds, channel_counts, group.reshape(1), waves, a, rn, tpb, slots, groups)
-    out = pieces[0]
+    pieces = list(
+        correlate(owner_rounds, channel_counts, group.reshape(1), waves, a, rn, tpb, slots, groups)
+    )
     for k in range(1, groups):
-        out = out + lax.ppermute(pieces[k], "tmpl", [(i, (i + k) % groups) for i in range(groups)])
-    return out
+        pieces[k] = lax.ppermute(pieces[k], "tmpl", [(i, (i + k) % groups) for i in range(groups)])
+    return (pieces[0] + pieces[1]) + (pieces[2] + pieces[3])
 
 
 def solution(mesh):

time: 48.4 us -> 48.1 us (level)
  no operation moved by 1% of the time
where the time goes in v6:
time: 48.1 us; the launch traced here: 47.3 us
  Pallas kernels  21.2 us (44%)
  starting transfers between devices  19.7 us (41%)
  waiting for transfers between devices  3.66 us (8%)
  other arithmetic  2.33 us (5%)
    ppermute x7, starting transfers between devices, sent(): return lax.ppermute(x, 'tm', [(i, to(i)) for i in range(32)])  13.3 us
    pallas_call x1, Pallas kernels, correlate(): pl.pallas_call(functools.partial(correlate_kernel, tpb, slots), out_shape...  10.3 us
    pallas_call x1, Pallas kernels, gather(): pl.pallas_call(functools.partial(gather_kernel, tpb), out_shape=(pltpu.VM...  5.58 us
    pallas_call x1, Pallas kernels, energy(): pl.pallas_call(functools.partial(energy_kernel, tpb, taps), out_shape=(pl...  5.3 us
    ppermute x3, starting transfers between devices, shards(): lax.ppermute(pieces[k], 'tmpl', [(i, (i + k) % groups) for i in range(gro...  5.12 us
    ppermute x3, waiting for transfers between devices, shards(): lax.ppermute(pieces[k], 'tmpl', [(i, (i + k) % groups) for i in range(gro...  3.18 us
    ppermute x1, starting transfers between devices, shards(): halo = lax.ppermute(heads, 'tm', [(i, i - 1) for i in range(1, 32)])  1.29 us
  transfers between devices with their start and end apart: 11, of which 3 were waited for; matrix products, arithmetic and copies ran while one was open for 2% of the time, Pallas kernels for 23%

profile of v6, /device:TPU:0, one launch (start us, length us, event | category | flops | bytes accessed | tf_op | source)
XLA Modules:
  0.0 47.3 jit_solution(2090951016583292617)
XLA Ops:
  0.0 0.0 collective-permute-start
  0.0 0.7 %broadcast_compare_fusion.1 = (pred[4]{0:T(512)(128)(4,1)S(1)}, pred[4]{0:T(512)(128)(4,1)S(1)}) fusion(s32[4]{0:T(128)} %owner.5, s32[]{:T(128)S(6)} %axis_index.25, s32[]{:T(128)S(6)} %xor.3), kind=kLoop, calls=%fused_computation.5 | loop fusion | flops 8 | bytes 32 | tf_op jit(solution)/shard_map/eq | solution.py:259
  0.7 0.1 broadcast_in_dim.52
  0.7 0.1 broadcast_in_dim.53
  0.8 0.1 broadcast_in_dim.57
  0.9 0.1 broadcast_in_dim.58
  1.0 0.5 collective-permute-done
  1.4 0.9 %fusion = bf16[192,512]{1,0:T(8,128)(2,1)S(1)} fusion(pred[192]{0:T(512)(128)(4,1)S(1)} %broadcast_in_dim.58, pred[192]{0:T(512)(128)(4,1)S(1)} %broadcast_in_dim.53, bf16[2,24,512]{2,1,0:T(8,128)(2,1)S(1)} %collective-permute-done, bf16[2,24,512]{2,1,0:T(8,128)(2,1)} %param.6), kind=kLoop, calls=%fused_computation.1 | loop fusion | flops 196608 | bytes 295296 | tf_op jit(solution)/shard_map/jit(_where)/select_n | solution.py:262
  2.4 2.1 %collective-permute-start.1 = (bf16[192,512]{1,0:T(8,128)(2,1)S(1)}, bf16[192,512]{1,0:T(8,128)(2,1)S(1)}, u32[]{:S(2)}, u32[]{:S(2)}) collective-permute-start(bf16[192,512]{1,0:T(8,128)(2,1)S(1)} %fusion), channel_id=1, source_target_pairs={{0,8},{4,36},{8,16},{12,44},{16,24},{20,52},{24,0},{28,60},{32,40}... | collective-permute-start | bytes 589832 | tf_op jit(solution)/shard_map/ppermute | solution.py:241
  4.5 2.2 %collective-permute-start.2 = (bf16[192,512]{1,0:T(8,128)(2,1)S(1)}, bf16[192,512]{1,0:T(8,128)(2,1)S(1)}, u32[]{:S(2)}, u32[]{:S(2)}) collective-permute-start(bf16[192,512]{1,0:T(8,128)(2,1)S(1)} %fusion), channel_id=1, source_target_pairs={{0,24},{4,100},{8,0},{12,108},{16,8},{20,116},{24,16},{28,124},{32... | collective-permute-start | bytes 589832 | tf_op jit(solution)/shard_map/ppermute | solution.py:241
  6.7 1.8 %collective-permute-start.3 = (bf16[192,512]{1,0:T(8,128)(2,1)S(1)}, bf16[192,512]{1,0:T(8,128)(2,1)S(1)}, u32[]{:S(2)}, u32[]{:S(2)}) collective-permute-start(bf16[192,512]{1,0:T(8,128)(2,1)S(1)} %fusion), channel_id=1, source_target_pairs={{0,16},{4,68},{8,24},{12,76},{16,0},{20,84},{24,8},{28,92},{32,48}... | collective-permute-start | bytes 589832 | tf_op jit(solution)/shard_map/ppermute | solution.py:241
  8.5 0.0 copy-start
  8.5 5.6 %gather_rows.1 = (bf16[192,32,2,128]{3,2,1,0:T(2,128)(2,1)S(1)}, bf16[768,128]{1,0:T(8,128)(2,1)}) custom-call(s32[4]{0:T(128)} %owner.5, s32[24,64]{1,0:T(8,128)} %bitcast.18, bf16[250,32,8,128]{3,2,1,0:T(8,128)(2,1)} %bitcast.17), custom_call_target="tpu_custom_call" | custom-call | tf_op jit(solution)/shard_map/gather_rows/pallas_call | solution.py:176
  14.0 0.0 collective-permute-done.1
  14.1 0.0 collective-permute-done.2
  14.1 0.0 collective-permute-done.3
  14.1 0.0 copy-done
  14.1 0.1 add_add_fusion.w0
  14.2 1.3 %collective-permute-start.7 = (bf16[768,128]{1,0:T(8,128)(2,1)}, bf16[768,128]{1,0:T(8,128)(2,1)S(1)}, u32[]{:S(2)}, u32[]{:S(2)}) collective-permute-start(bf16[768,128]{1,0:T(8,128)(2,1)} %get-tuple-element.18), channel_id=1, source_target_pairs={{4,0},{8,4},{12,8},{16,12},{20,16},{24,20},{28,24},{32,28},{36,32}... | collective-permute-start | bytes 589832 | tf_op jit(solution)/shard_map/ppermute | solution.py:268
  15.5 4.4 %collective-permute-start.4 = (bf16[192,512]{1,0:T(8,128)(2,1)S(1)}, bf16[192,512]{1,0:T(8,128)(2,1)}, u32[]{:S(2)}, u32[]{:S(2)}) collective-permute-start(bf16[192,512]{1,0:T(8,128)(2,1)S(1)} %add_add_fusion.w0), channel_id=1, source_target_pairs={{0,32},{4,12},{8,40},{12,20},{16,48},{20,28},{24,56},{28,4},{32,64... | collective-permute-start | bytes 589832 | tf_op jit(solution)/shard_map/ppermute | solution.py:241
  19.9 0.3 collective-permute-start.5
  20.3 2.4 %collective-permute-start.6 = (bf16[192,512]{1,0:T(8,128)(2,1)S(1)}, bf16[192,512]{1,0:T(8,128)(2,1)}, u32[]{:S(2)}, u32[]{:S(2)}) collective-permute-start(bf16[192,512]{1,0:T(8,128)(2,1)S(1)} %add_add_fusion.w0), channel_id=1, source_target_pairs={{0,64},{4,20},{8,72},{12,28},{16,80},{20,4},{24,88},{28,12},{32,96... | collective-permute-start | bytes 589832 | tf_op jit(solution)/shard_map/ppermute | solution.py:241
  22.7 0.0 collective-permute-done.7.halo
  22.7 5.3 %window_energy.1 = (f32[192,32,128]{2,1,0:T(8,128)S(1)}, bf16[192,96,128]{2,1,0:T(8,128)(2,1)S(1)}) custom-call(s32[4]{0:T(128)} %owner.5, s32[24,64]{1,0:T(8,128)} %bitcast.19, bf16[192,64,128]{2,1,0:T(8,128)(2,1)S(1)} %bitcast.16, bf16[768,128]{1,0:T(8,128)(2,1)S(1)} %collective-permute-done.7.halo), custom_call_target="tpu_custom_call" | custom-call | tf_op jit(solution)/shard_map/window_energy/pallas_call | solution.py:197
  28.0 0.0 collective-permute-done.4.w1
  28.0 0.0 collective-permute-done.5.w2
  28.0 0.0 collective-permute-done.6.w3
  28.0 10.3 %correlate.1 = (f32[8,1024]{1,0:T(8,128)S(1)}, f32[8,1024]{1,0:T(8,128)S(1)}, f32[8,1024]{1,0:T(8,128)S(1)}, f32[8,1024]{1,0:T(8,128)S(1)}) custom-call(s32[4]{0:T(128)} %owner.5, s32[64]{0:T(128)} %counts.1, s32[1]{0:T(128)} %bitcast.place, bf16[192,512]{1,0:T(8,128)(2,1)S(1)} %add_add_fusion.w0, bf16[192,512]{1,0:T(8,128)(2,1)} %collective-permute-done.4.w1, ...), custom_call_target="tpu_custom_call" | custom-call | tf_op jit(solution)/shard_map/correlate/pallas_call | solution.py:218
  38.4 2.8 %collective-permute-start.10 = (f32[8,1024]{1,0:T(8,128)S(1)}, f32[8,1024]{1,0:T(8,128)S(1)}, u32[]{:S(2)}, u32[]{:S(2)}) collective-permute-start(f32[8,1024]{1,0:T(8,128)S(1)} %get-tuple-element.24), channel_id=1, source_target_pairs={{0,3},{1,0},{2,1},{3,2},{4,7},{5,4},{6,5},{7,6},{8,11},{9,8},{10,9... | collective-permute-start | bytes 98312 | tf_op jit(solution)/shard_map/ppermute | solution.py:275
  41.2 0.0 collective-permute-start.8
  41.2 2.3 %collective-permute-start.9 = (f32[8,1024]{1,0:T(8,128)S(1)}, f32[8,1024]{1,0:T(8,128)S(1)}, u32[]{:S(2)}, u32[]{:S(2)}) collective-permute-start(f32[8,1024]{1,0:T(8,128)S(1)} %get-tuple-element.23), channel_id=1, source_target_pairs={{0,2},{1,3},{2,0},{3,1},{4,6},{5,7},{6,4},{7,5},{8,10},{9,11},{10,... | collective-permute-start | bytes 98312 | tf_op jit(solution)/shard_map/ppermute | solution.py:275
  43.5 0.0 collective-permute-done.10
  43.5 2.8 %collective-permute-done.8 = f32[8,1024]{1,0:T(8,128)S(1)} collective-permute-done((f32[8,1024]{1,0:T(8,128)S(1)}, f32[8,1024]{1,0:T(8,128)S(1)}, u32[]{:S(2)}, u32[]{:S(2)}) %collective-permute-start.8) | collective-permute-done | bytes 32800 | tf_op jit(solution)/shard_map/ppermute | solution.py:275
  46.3 0.3 collective-permute-done.9
  46.7 0.6 %add_add_fusion.1 = f32[8,1024]{1,0:T(8,128)} fusion(f32[8,1024]{1,0:T(8,128)S(1)} %collective-permute-done.9, f32[8,1024]{1,0:T(8,128)S(1)} %collective-permute-done.10, f32[8,1024]{1,0:T(8,128)S(1)} %get-tuple-element.21, f32[8,1024]{1,0:T(8,128)S(1)} %collective-permute-done.8), kind=kLoop, calls=%fused_computation.3 | loop fusion | flops 24576 | bytes 163840 | tf_op jit(solution)/shard_map/add | solution.py:276
Async XLA Ops:
  0.0 1.4 %collective-permute-start = (bf16[2,24,512]{2,1,0:T(8,128)(2,1)}, bf16[2,24,512]{2,1,0:T(8,128)(2,1)S(1)}, u32[]{:S(2)}, u32[]{:S(2)}) collective-permute-start(bf16[2,24,512]{2,1,0:T(8,128)(2,1)} %param.6), channel_id=1, source_target_pairs={{0,4},{4,0},{8,12},{12,8},{16,20},{20,16},{24,28},{28,24},{32,36},... | collective-permute-start | bytes 147464 | tf_op jit(solution)/shard_map/ppermute | solution.py:241
  2.4 11.7 %collective-permute-start.1 = (bf16[192,512]{1,0:T(8,128)(2,1)S(1)}, bf16[192,512]{1,0:T(8,128)(2,1)S(1)}, u32[]{:S(2)}, u32[]{:S(2)}) collective-permute-start(bf16[192,512]{1,0:T(8,128)(2,1)S(1)} %fusion), channel_id=1, source_target_pairs={{0,8},{4,36},{8,16},{12,44},{16,24},{20,52},{24,0},{28,60},{32,40}... | collective-permute-start | bytes 589832 | tf_op jit(solution)/shard_map/ppermute | solution.py:241
  4.5 9.6 %collective-permute-start.2 = (bf16[192,512]{1,0:T(8,128)(2,1)S(1)}, bf16[192,512]{1,0:T(8,128)(2,1)S(1)}, u32[]{:S(2)}, u32[]{:S(2)}) collective-permute-start(bf16[192,512]{1,0:T(8,128)(2,1)S(1)} %fusion), channel_id=1, source_target_pairs={{0,24},{4,100},{8,0},{12,108},{16,8},{20,116},{24,16},{28,124},{32... | collective-permute-start | bytes 589832 | tf_op jit(solution)/shard_map/ppermute | solution.py:241
  6.7 7.4 %collective-permute-start.3 = (bf16[192,512]{1,0:T(8,128)(2,1)S(1)}, bf16[192,512]{1,0:T(8,128)(2,1)S(1)}, u32[]{:S(2)}, u32[]{:S(2)}) collective-permute-start(bf16[192,512]{1,0:T(8,128)(2,1)S(1)} %fusion), channel_id=1, source_target_pairs={{0,16},{4,68},{8,24},{12,76},{16,0},{20,84},{24,8},{28,92},{32,48}... | collective-permute-start | bytes 589832 | tf_op jit(solution)/shard_map/ppermute | solution.py:241
  8.5 5.6 %copy-start = (bf16[2,24,512]{2,1,0:T(8,128)(2,1)S(1)}, bf16[2,24,512]{2,1,0:T(8,128)(2,1)}, u32[]{:S(2)}) copy-start(bf16[2,24,512]{2,1,0:T(8,128)(2,1)} %param.6) | copy-start | bytes 147460
  14.2 8.5 %collective-permute-start.7 = (bf16[768,128]{1,0:T(8,128)(2,1)}, bf16[768,128]{1,0:T(8,128)(2,1)S(1)}, u32[]{:S(2)}, u32[]{:S(2)}) collective-permute-start(bf16[768,128]{1,0:T(8,128)(2,1)} %get-tuple-element.18), channel_id=1, source_target_pairs={{4,0},{8,4},{12,8},{16,12},{20,16},{24,20},{28,24},{32,28},{36,32}... | collective-permute-start | bytes 589832 | tf_op jit(solution)/shard_map/ppermute | solution.py:268
  15.5 12.5 %collective-permute-start.4 = (bf16[192,512]{1,0:T(8,128)(2,1)S(1)}, bf16[192,512]{1,0:T(8,128)(2,1)}, u32[]{:S(2)}, u32[]{:S(2)}) collective-permute-start(bf16[192,512]{1,0:T(8,128)(2,1)S(1)} %add_add_fusion.w0), channel_id=1, source_target_pairs={{0,32},{4,12},{8,40},{12,20},{16,48},{20,28},{24,56},{28,4},{32,64... | collective-permute-start | bytes 589832 | tf_op jit(solution)/shard_map/ppermute | solution.py:241
  19.9 8.1 %collective-permute-start.5 = (bf16[192,512]{1,0:T(8,128)(2,1)S(1)}, bf16[192,512]{1,0:T(8,128)(2,1)}, u32[]{:S(2)}, u32[]{:S(2)}) collective-permute-start(bf16[192,512]{1,0:T(8,128)(2,1)S(1)} %add_add_fusion.w0), channel_id=1, source_target_pairs={{0,96},{4,28},{8,104},{12,4},{16,112},{20,12},{24,120},{28,20},{32... | collective-permute-start | bytes 589832 | tf_op jit(solution)/shard_map/ppermute | solution.py:241
  20.3 7.8 %collective-permute-start.6 = (bf16[192,512]{1,0:T(8,128)(2,1)S(1)}, bf16[192,512]{1,0:T(8,128)(2,1)}, u32[]{:S(2)}, u32[]{:S(2)}) collective-permute-start(bf16[192,512]{1,0:T(8,128)(2,1)S(1)} %add_add_fusion.w0), channel_id=1, source_target_pairs={{0,64},{4,20},{8,72},{12,28},{16,80},{20,4},{24,88},{28,12},{32,96... | collective-permute-start | bytes 589832 | tf_op jit(solution)/shard_map/ppermute | solution.py:241
  38.4 5.1 %collective-permute-start.10 = (f32[8,1024]{1,0:T(8,128)S(1)}, f32[8,1024]{1,0:T(8,128)S(1)}, u32[]{:S(2)}, u32[]{:S(2)}) collective-permute-start(f32[8,1024]{1,0:T(8,128)S(1)} %get-tuple-element.24), channel_id=1, source_target_pairs={{0,3},{1,0},{2,1},{3,2},{4,7},{5,4},{6,5},{7,6},{8,11},{9,8},{10,9... | collective-permute-start | bytes 98312 | tf_op jit(solution)/shard_map/ppermute | solution.py:275
  41.2 5.1 %collective-permute-start.8 = (f32[8,1024]{1,0:T(8,128)S(1)}, f32[8,1024]{1,0:T(8,128)S(1)}, u32[]{:S(2)}, u32[]{:S(2)}) collective-permute-start(f32[8,1024]{1,0:T(8,128)S(1)} %get-tuple-element.22), channel_id=1, source_target_pairs={{0,1},{1,2},{2,3},{3,0},{4,5},{5,6},{6,7},{7,4},{8,9},{9,10},{10,1... | collective-permute-start | bytes 98312 | tf_op jit(solution)/shard_map/ppermute | solution.py:275
  41.2 5.5 %collective-permute-start.9 = (f32[8,1024]{1,0:T(8,128)S(1)}, f32[8,1024]{1,0:T(8,128)S(1)}, u32[]{:S(2)}, u32[]{:S(2)}) collective-permute-start(f32[8,1024]{1,0:T(8,128)S(1)} %get-tuple-element.23), channel_id=1, source_target_pairs={{0,2},{1,3},{2,0},{3,1},{4,6},{5,7},{6,4},{7,5},{8,10},{9,11},{10,... | collective-permute-start | bytes 98312 | tf_op jit(solution)/shard_map/ppermute | solution.py:275

commit v7 on v6

--- a/solution.py
+++ b/solution.py
@@ -122,7 +122,7 @@
     nt = n // slots
     blocks = rn.shape[1]
     half = blocks // 2
-    parts = len(outs)
+    parts = 4
     group = place[0]
     wf = w.astype(f32)
     hi, lo = two_parts(wf * wf)
@@ -163,10 +163,17 @@
 
     lax.fori_loop(0, nt, template, 0)
     per = blocks // parts
-    for k, o in enumerate(outs):
-        to = (group + k) % parts
+    aside = group ^ 1
+    last = parts - 1
+    for o, row, to in (
+        (outs[0], 0, group),
+        (outs[1], 0, last - group),
+        (outs[2], 0, last - aside),
+        (outs[2], nt, aside),
+    ):
         for b in range(per):
-            o[:, LANES * b : LANES * (b + 1)] = acc[pl.ds(pl.multiple_of((to * per + b) * nt, 8), nt), :]
+            piece = acc[pl.ds(pl.multiple_of((to * per + b) * nt, 8), nt), :]
+            o[row : row + nt, LANES * b : LANES * (b + 1)] = piece
 
 
 def gather(owner, lists, wf4, tpb, tb):
@@ -175,7 +182,7 @@
     blocks = wf4.shape[1]
     return pl.pallas_call(
         functools.partial(gather_kernel, tpb),
-        out_shape=(pltpu.VMEM((n, blocks, 2, LANES), bf16), jax.ShapeDtypeStruct((n * tb, LANES), bf16)),
+        out_shape=(pltpu.VMEM((n, blocks, 2, LANES), bf16), pltpu.VMEM((n * tb, LANES), bf16)),
         grid_spec=pltpu.PrefetchScalarGridSpec(
             num_scalar_prefetch=2,
             in_specs=[pl.BlockSpec(memory_space=pltpu.HBM)],
@@ -217,11 +224,11 @@
     blocks = rn.shape[1]
     return pl.pallas_call(
         functools.partial(correlate_kernel, tpb, slots),
-        out_shape=tuple(jax.ShapeDtypeStruct((nt, blocks // parts * LANES), f32) for _ in range(parts)),
+        out_shape=tuple(jax.ShapeDtypeStruct((r * nt, blocks // parts * LANES), f32) for r in (1, 1, 2)),
         grid_spec=pltpu.PrefetchScalarGridSpec(
             num_scalar_prefetch=3,
             in_specs=[vmem_spec()] * (len(ws) + 2),
-            out_specs=tuple(vmem_spec() for _ in range(parts)),
+            out_specs=tuple(vmem_spec() for _ in range(3)),
             scratch_shapes=[
                 pltpu.VMEM((taps // LANES, n + 8, LANES), f32),
                 pltpu.VMEM((n + 8, LANES), f32),
@@ -268,12 +275,13 @@
     halo = lax.ppermute(heads, "tm", [(i, i - 1) for i in range(1, 32)])
     waves = round_the_ring(waves, False)
     rn, a = energy(owner_rounds, lists, pairs, halo, tpb, taps)
-    pieces = list(
-        correlate(owner_rounds, channel_counts, group.reshape(1), waves, a, rn, tpb, slots, groups)
+    nt = rounds * tpb
+    mine, later, given = correlate(
+        owner_rounds, channel_counts, group.reshape(1), waves, a, rn, tpb, slots, groups
     )
-    for k in range(1, groups):
-        pieces[k] = lax.ppermute(pieces[k], "tmpl", [(i, (i + k) % groups) for i in range(groups)])
-    return (pieces[0] + pieces[1]) + (pieces[2] + pieces[3])
+    taken = lax.ppermute(given, "tmpl", [(i, i ^ 1) for i in range(groups)])
+    share = lax.ppermute(later + taken[0:nt], "tmpl", [(i, groups - 1 - i) for i in range(groups)])
+    return mine + taken[nt:] + share
 
 
 def solution(mesh):

time: 48.1 us -> 48.9 us (1.017)
  waiting for transfers between devices: 3.66 us -> 5.61 us
  starting transfers between devices: 19.7 us -> 18.9 us
    ppermute x3 -> x2, waiting for transfers between devices: 3.18 us -> 5.13 us  [the longest x1 2.77 us: shards(): taken = lax.ppermute(given, 'tmpl', [(i, i ^ 1) for i in range(groups)])]
    ppermute x3 -> x2, starting transfers between devices: 5.12 us -> 4.34 us  [the longest x1 2.76 us: shards(): lax.ppermute(later + taken[0:nt], 'tmpl', [(i, groups - 1 - i) for i in r...]
  transfers between devices with their start and end apart: 11 -> 10, of which waited for: 3 -> 3; matrix products, arithmetic and copies ran while one was open for 2% -> 2% of each run, Pallas kernels for 23% -> 22%
where the time goes in v7:
time: 48.9 us; the launch traced here: 48.5 us
  Pallas kernels  21.2 us (43%)
  starting transfers between devices  18.9 us (39%)
  waiting for transfers between devices  5.61 us (11%)
  other arithmetic  2.33 us (5%)
    ppermute x7, starting transfers between devices, sent(): return lax.ppermute(x, 'tm', [(i, to(i)) for i in range(32)])  13.3 us
    pallas_call x1, Pallas kernels, correlate(): pl.pallas_call(functools.partial(correlate_kernel, tpb, slots), out_shape...  10.3 us
    pallas_call x1, Pallas kernels, gather(): pl.pallas_call(functools.partial(gather_kernel, tpb), out_shape=(pltpu.VM...  5.6 us
    pallas_call x1, Pallas kernels, energy(): pl.pallas_call(functools.partial(energy_kernel, tpb, taps), out_shape=(pl...  5.3 us
    ppermute x1, waiting for transfers between devices, shards(): taken = lax.ppermute(given, 'tmpl', [(i, i ^ 1) for i in range(groups)])  2.77 us
    ppermute x1, starting transfers between devices, shards(): lax.ppermute(later + taken[0:nt], 'tmpl', [(i, groups - 1 - i) for i in r...  2.76 us
    ppermute x1, waiting for transfers between devices, shards(): lax.ppermute(later + taken[0:nt], 'tmpl', [(i, groups - 1 - i) for i in r...  2.36 us
    ppermute x1, starting transfers between devices, shards(): taken = lax.ppermute(given, 'tmpl', [(i, i ^ 1) for i in range(groups)])  1.57 us
  transfers between devices with their start and end apart: 10, of which 3 were waited for; matrix products, arithmetic and copies ran while one was open for 2% of the time, Pallas kernels for 22%

profile of v7, /device:TPU:0, one launch (start us, length us, event | category | flops | bytes accessed | tf_op | source)
XLA Modules:
  0.0 48.5 jit_solution(3036041375736983896)
XLA Ops:
  0.0 0.0 collective-permute-start
  0.0 0.7 %broadcast_compare_fusion.1 = (pred[4]{0:T(512)(128)(4,1)S(1)}, pred[4]{0:T(512)(128)(4,1)S(1)}) fusion(s32[4]{0:T(128)} %owner.5, s32[]{:T(128)S(6)} %axis_index.25, s32[]{:T(128)S(6)} %xor.3), kind=kLoop, calls=%fused_computation.7 | loop fusion | flops 8 | bytes 32 | tf_op jit(solution)/shard_map/eq | solution.py:266
  0.7 0.1 broadcast_in_dim.52
  0.7 0.1 broadcast_in_dim.53
  0.8 0.1 broadcast_in_dim.57
  0.9 0.1 broadcast_in_dim.58
  1.0 0.5 collective-permute-done
  1.4 0.9 %fusion = bf16[192,512]{1,0:T(8,128)(2,1)S(1)} fusion(pred[192]{0:T(512)(128)(4,1)S(1)} %broadcast_in_dim.58, pred[192]{0:T(512)(128)(4,1)S(1)} %broadcast_in_dim.53, bf16[2,24,512]{2,1,0:T(8,128)(2,1)S(1)} %collective-permute-done, bf16[2,24,512]{2,1,0:T(8,128)(2,1)} %param.6), kind=kLoop, calls=%fused_computation.1 | loop fusion | flops 196608 | bytes 295296 | tf_op jit(solution)/shard_map/jit(_where)/select_n | solution.py:269
  2.4 2.1 %collective-permute-start.1 = (bf16[192,512]{1,0:T(8,128)(2,1)S(1)}, bf16[192,512]{1,0:T(8,128)(2,1)S(1)}, u32[]{:S(2)}, u32[]{:S(2)}) collective-permute-start(bf16[192,512]{1,0:T(8,128)(2,1)S(1)} %fusion), channel_id=1, source_target_pairs={{0,8},{4,36},{8,16},{12,44},{16,24},{20,52},{24,0},{28,60},{32,40}... | collective-permute-start | bytes 589832 | tf_op jit(solution)/shard_map/ppermute | solution.py:248
  4.5 2.2 %collective-permute-start.2 = (bf16[192,512]{1,0:T(8,128)(2,1)S(1)}, bf16[192,512]{1,0:T(8,128)(2,1)S(1)}, u32[]{:S(2)}, u32[]{:S(2)}) collective-permute-start(bf16[192,512]{1,0:T(8,128)(2,1)S(1)} %fusion), channel_id=1, source_target_pairs={{0,24},{4,100},{8,0},{12,108},{16,8},{20,116},{24,16},{28,124},{32... | collective-permute-start | bytes 589832 | tf_op jit(solution)/shard_map/ppermute | solution.py:248
  6.7 1.8 %collective-permute-start.3 = (bf16[192,512]{1,0:T(8,128)(2,1)S(1)}, bf16[192,512]{1,0:T(8,128)(2,1)S(1)}, u32[]{:S(2)}, u32[]{:S(2)}) collective-permute-start(bf16[192,512]{1,0:T(8,128)(2,1)S(1)} %fusion), channel_id=1, source_target_pairs={{0,16},{4,68},{8,24},{12,76},{16,0},{20,84},{24,8},{28,92},{32,48}... | collective-permute-start | bytes 589832 | tf_op jit(solution)/shard_map/ppermute | solution.py:248
  8.5 0.0 copy-start
  8.5 5.6 %gather_rows.1 = (bf16[192,32,2,128]{3,2,1,0:T(2,128)(2,1)S(1)}, bf16[768,128]{1,0:T(8,128)(2,1)}) custom-call(s32[4]{0:T(128)} %owner.5, s32[24,64]{1,0:T(8,128)} %bitcast.18, bf16[250,32,8,128]{3,2,1,0:T(8,128)(2,1)} %bitcast.17), custom_call_target="tpu_custom_call" | custom-call | tf_op jit(solution)/shard_map/gather_rows/pallas_call | solution.py:183
  14.1 0.0 collective-permute-done.1
  14.1 0.0 collective-permute-done.2
  14.1 0.0 collective-permute-done.3
  14.1 0.0 copy-done
  14.1 0.1 add_add_fusion.w0
  14.2 1.3 %collective-permute-start.7 = (bf16[768,128]{1,0:T(8,128)(2,1)}, bf16[768,128]{1,0:T(8,128)(2,1)S(1)}, u32[]{:S(2)}, u32[]{:S(2)}) collective-permute-start(bf16[768,128]{1,0:T(8,128)(2,1)} %get-tuple-element.17), channel_id=1, source_target_pairs={{4,0},{8,4},{12,8},{16,12},{20,16},{24,20},{28,24},{32,28},{36,32}... | collective-permute-start | bytes 589832 | tf_op jit(solution)/shard_map/ppermute | solution.py:275
  15.5 4.4 %collective-permute-start.4 = (bf16[192,512]{1,0:T(8,128)(2,1)S(1)}, bf16[192,512]{1,0:T(8,128)(2,1)}, u32[]{:S(2)}, u32[]{:S(2)}) collective-permute-start(bf16[192,512]{1,0:T(8,128)(2,1)S(1)} %add_add_fusion.w0), channel_id=1, source_target_pairs={{0,32},{4,12},{8,40},{12,20},{16,48},{20,28},{24,56},{28,4},{32,64... | collective-permute-start | bytes 589832 | tf_op jit(solution)/shard_map/ppermute | solution.py:248
  20.0 0.3 collective-permute-start.5
  20.3 2.4 %collective-permute-start.6 = (bf16[192,512]{1,0:T(8,128)(2,1)S(1)}, bf16[192,512]{1,0:T(8,128)(2,1)}, u32[]{:S(2)}, u32[]{:S(2)}) collective-permute-start(bf16[192,512]{1,0:T(8,128)(2,1)S(1)} %add_add_fusion.w0), channel_id=1, source_target_pairs={{0,64},{4,20},{8,72},{12,28},{16,80},{20,4},{24,88},{28,12},{32,96... | collective-permute-start | bytes 589832 | tf_op jit(solution)/shard_map/ppermute | solution.py:248
  22.7 0.0 collective-permute-done.7.halo
  22.7 5.3 %window_energy.1 = (f32[192,32,128]{2,1,0:T(8,128)S(1)}, bf16[192,96,128]{2,1,0:T(8,128)(2,1)S(1)}) custom-call(s32[4]{0:T(128)} %owner.5, s32[24,64]{1,0:T(8,128)} %bitcast.19, bf16[192,64,128]{2,1,0:T(8,128)(2,1)S(1)} %bitcast.16, bf16[768,128]{1,0:T(8,128)(2,1)S(1)} %collective-permute-done.7.halo), custom_call_target="tpu_custom_call" | custom-call | tf_op jit(solution)/shard_map/window_energy/pallas_call | solution.py:204
  28.0 0.0 collective-permute-done.4.w1
  28.0 0.0 collective-permute-done.5.w2
  28.0 0.0 collective-permute-done.6.w3
  28.0 10.3 %correlate.1 = (f32[8,1024]{1,0:T(8,128)S(1)}, f32[8,1024]{1,0:T(8,128)S(1)}, f32[16,1024]{1,0:T(8,128)S(1)}) custom-call(s32[4]{0:T(128)} %owner.5, s32[64]{0:T(128)} %counts.1, s32[1]{0:T(128)} %bitcast.place, bf16[192,512]{1,0:T(8,128)(2,1)S(1)} %add_add_fusion.w0, bf16[192,512]{1,0:T(8,128)(2,1)} %collective-permute-done.4.w1, ...), custom_call_target="tpu_custom_call" | custom-call | tf_op jit(solution)/shard_map/correlate/pallas_call | solution.py:225
  38.4 1.6 %collective-permute-start.8 = (f32[16,1024]{1,0:T(8,128)S(1)}, f32[16,1024]{1,0:T(8,128)S(1)}, u32[]{:S(2)}, u32[]{:S(2)}) collective-permute-start(f32[16,1024]{1,0:T(8,128)S(1)} %get-tuple-element.21), channel_id=1, source_target_pairs={{0,1},{1,0},{2,3},{3,2},{4,5},{5,4},{6,7},{7,6},{8,9},{9,8},{10,11... | collective-permute-start | bytes 196616 | tf_op jit(solution)/shard_map/ppermute | solution.py:282
  40.0 2.8 %collective-permute-done.8 = f32[16,1024]{1,0:T(8,128)S(1)} collective-permute-done((f32[16,1024]{1,0:T(8,128)S(1)}, f32[16,1024]{1,0:T(8,128)S(1)}, u32[]{:S(2)}, u32[]{:S(2)}) %collective-permute-start.8) | collective-permute-done | bytes 65568 | tf_op jit(solution)/shard_map/ppermute | solution.py:282
  42.7 2.8 %collective-permute-start.9 = (f32[8,1024]{1,0:T(8,128)S(1)}, f32[8,1024]{1,0:T(8,128)S(1)}, u32[]{:S(2)}, u32[]{:S(2)}) collective-permute-start(f32[8,1024]{1,0:T(8,128)S(1)} %slice_add_fusion), channel_id=1, source_target_pairs={{0,3},{1,2},{2,1},{3,0},{4,7},{5,6},{6,5},{7,4},{8,11},{9,10},{10,... | collective-permute-start | bytes 98312 | tf_op jit(solution)/shard_map/ppermute | solution.py:283
  45.5 2.4 %collective-permute-done.9 = f32[8,1024]{1,0:T(8,128)S(1)} collective-permute-done((f32[8,1024]{1,0:T(8,128)S(1)}, f32[8,1024]{1,0:T(8,128)S(1)}, u32[]{:S(2)}, u32[]{:S(2)}) %collective-permute-start.9) | collective-permute-done | bytes 32800 | tf_op jit(solution)/shard_map/ppermute | solution.py:283
  47.9 0.6 %fusion.1 = f32[8,1024]{1,0:T(8,128)} fusion(f32[8,1024]{1,0:T(8,128)S(1)} %collective-permute-done.9, f32[8,1024]{1,0:T(8,128)S(1)} %get-tuple-element.20, f32[16,1024]{1,0:T(8,128)S(1)} %collective-permute-done.8), kind=kLoop, calls=%fused_computation.5 | loop fusion | flops 16384 | bytes 131072 | tf_op jit(solution)/shard_map/add | solution.py:284
  (1 shorter events, 0.0 us)
Async XLA Ops:
  0.0 1.4 %collective-permute-start = (bf16[2,24,512]{2,1,0:T(8,128)(2,1)}, bf16[2,24,512]{2,1,0:T(8,128)(2,1)S(1)}, u32[]{:S(2)}, u32[]{:S(2)}) collective-permute-start(bf16[2,24,512]{2,1,0:T(8,128)(2,1)} %param.6), channel_id=1, source_target_pairs={{0,4},{4,0},{8,12},{12,8},{16,20},{20,16},{24,28},{28,24},{32,36},... | collective-permute-start | bytes 147464 | tf_op jit(solution)/shard_map/ppermute | solution.py:248
  2.4 11.7 %collective-permute-start.1 = (bf16[192,512]{1,0:T(8,128)(2,1)S(1)}, bf16[192,512]{1,0:T(8,128)(2,1)S(1)}, u32[]{:S(2)}, u32[]{:S(2)}) collective-permute-start(bf16[192,512]{1,0:T(8,128)(2,1)S(1)} %fusion), channel_id=1, source_target_pairs={{0,8},{4,36},{8,16},{12,44},{16,24},{20,52},{24,0},{28,60},{32,40}... | collective-permute-start | bytes 589832 | tf_op jit(solution)/shard_map/ppermute | solution.py:248
  4.5 9.6 %collective-permute-start.2 = (bf16[192,512]{1,0:T(8,128)(2,1)S(1)}, bf16[192,512]{1,0:T(8,128)(2,1)S(1)}, u32[]{:S(2)}, u32[]{:S(2)}) collective-permute-start(bf16[192,512]{1,0:T(8,128)(2,1)S(1)} %fusion), channel_id=1, source_target_pairs={{0,24},{4,100},{8,0},{12,108},{16,8},{20,116},{24,16},{28,124},{32... | collective-permute-start | bytes 589832 | tf_op jit(solution)/shard_map/ppermute | solution.py:248
  6.7 7.4 %collective-permute-start.3 = (bf16[192,512]{1,0:T(8,128)(2,1)S(1)}, bf16[192,512]{1,0:T(8,128)(2,1)S(1)}, u32[]{:S(2)}, u32[]{:S(2)}) collective-permute-start(bf16[192,512]{1,0:T(8,128)(2,1)S(1)} %fusion), channel_id=1, source_target_pairs={{0,16},{4,68},{8,24},{12,76},{16,0},{20,84},{24,8},{28,92},{32,48}... | collective-permute-start | bytes 589832 | tf_op jit(solution)/shard_map/ppermute | solution.py:248
  8.5 5.6 %copy-start = (bf16[2,24,512]{2,1,0:T(8,128)(2,1)S(1)}, bf16[2,24,512]{2,1,0:T(8,128)(2,1)}, u32[]{:S(2)}) copy-start(bf16[2,24,512]{2,1,0:T(8,128)(2,1)} %param.6) | copy-start | bytes 147460
  14.2 8.5 %collective-permute-start.7 = (bf16[768,128]{1,0:T(8,128)(2,1)}, bf16[768,128]{1,0:T(8,128)(2,1)S(1)}, u32[]{:S(2)}, u32[]{:S(2)}) collective-permute-start(bf16[768,128]{1,0:T(8,128)(2,1)} %get-tuple-element.17), channel_id=1, source_target_pairs={{4,0},{8,4},{12,8},{16,12},{20,16},{24,20},{28,24},{32,28},{36,32}... | collective-permute-start | bytes 589832 | tf_op jit(solution)/shard_map/ppermute | solution.py:275
  15.5 12.5 %collective-permute-start.4 = (bf16[192,512]{1,0:T(8,128)(2,1)S(1)}, bf16[192,512]{1,0:T(8,128)(2,1)}, u32[]{:S(2)}, u32[]{:S(2)}) collective-permute-start(bf16[192,512]{1,0:T(8,128)(2,1)S(1)} %add_add_fusion.w0), channel_id=1, source_target_pairs={{0,32},{4,12},{8,40},{12,20},{16,48},{20,28},{24,56},{28,4},{32,64... | collective-permute-start | bytes 589832 | tf_op jit(solution)/shard_map/ppermute | solution.py:248
  20.0 8.1 %collective-permute-start.5 = (bf16[192,512]{1,0:T(8,128)(2,1)S(1)}, bf16[192,512]{1,0:T(8,128)(2,1)}, u32[]{:S(2)}, u32[]{:S(2)}) collective-permute-start(bf16[192,512]{1,0:T(8,128)(2,1)S(1)} %add_add_fusion.w0), channel_id=1, source_target_pairs={{0,96},{4,28},{8,104},{12,4},{16,112},{20,12},{24,120},{28,20},{32... | collective-permute-start | bytes 589832 | tf_op jit(solution)/shard_map/ppermute | solution.py:248
  20.3 7.8 %collective-permute-start.6 = (bf16[192,512]{1,0:T(8,128)(2,1)S(1)}, bf16[192,512]{1,0:T(8,128)(2,1)}, u32[]{:S(2)}, u32[]{:S(2)}) collective-permute-start(bf16[192,512]{1,0:T(8,128)(2,1)S(1)} %add_add_fusion.w0), channel_id=1, source_target_pairs={{0,64},{4,20},{8,72},{12,28},{16,80},{20,4},{24,88},{28,12},{32,96... | collective-permute-start | bytes 589832 | tf_op jit(solution)/shard_map/ppermute | solution.py:248
  38.4 4.3 %collective-permute-start.8 = (f32[16,1024]{1,0:T(8,128)S(1)}, f32[16,1024]{1,0:T(8,128)S(1)}, u32[]{:S(2)}, u32[]{:S(2)}) collective-permute-start(f32[16,1024]{1,0:T(8,128)S(1)} %get-tuple-element.21), channel_id=1, source_target_pairs={{0,1},{1,0},{2,3},{3,2},{4,5},{5,4},{6,7},{7,6},{8,9},{9,8},{10,11... | collective-permute-start | bytes 196616 | tf_op jit(solution)/shard_map/ppermute | solution.py:282
  42.7 5.1 %collective-permute-start.9 = (f32[8,1024]{1,0:T(8,128)S(1)}, f32[8,1024]{1,0:T(8,128)S(1)}, u32[]{:S(2)}, u32[]{:S(2)}) collective-permute-start(f32[8,1024]{1,0:T(8,128)S(1)} %slice_add_fusion), channel_id=1, source_target_pairs={{0,3},{1,2},{2,1},{3,0},{4,7},{5,6},{6,5},{7,4},{8,11},{9,10},{10,... | collective-permute-start | bytes 98312 | tf_op jit(solution)/shard_map/ppermute | solution.py:283

commit v8 on v6

--- a/solution.py
+++ b/solution.py
@@ -243,7 +243,10 @@
 
 def round_the_ring(x, first):
     turn = lambda k: lambda i: turned(i, 0, k) if (i % 2 == 0) == first else turned(i, k, 0)
-    return [x] + [sent(x, turn(k)) for k in (1, 3, 2)]
+    all_four = [x]
+    for k in (1, 3, 2):
+        all_four.append(sent(x, turn(k)))
+    return all_four
 
 
 def shards(waveforms, templates, channel_lists, channel_counts, owner_rounds):
@@ -264,7 +267,6 @@
     lists = channel_lists.T
     pairs, heads = gather(owner_rounds, lists, wf4, tpb, taps // LANES)
     pairs = pairs.reshape(n, -1, LANES)
-    heads, waves = lax.optimization_barrier((heads, waves))
     halo = lax.ppermute(heads, "tm", [(i, i - 1) for i in range(1, 32)])
     waves = round_the_ring(waves, False)
     rn, a = energy(owner_rounds, lists, pairs, halo, tpb, taps)

time: 48.1 us -> 48.7 us (1.012)
  waiting for transfers between devices: 3.66 us -> 4.15 us
    ppermute x7, waiting for transfers between devices: 0.47 us -> 1.67 us  [sent(): return lax.ppermute(x, 'tm', [(i, to(i)) for i in range(32)])]
    ppermute x3, waiting for transfers between devices: 3.18 us -> 2.48 us  [shards(): lax.ppermute(pieces[k], 'tmpl', [(i, (i + k) % groups) for i in range(gro...]
    ppermute x3, starting transfers between devices: 5.12 us -> 5.73 us  [shards(): lax.ppermute(pieces[k], 'tmpl', [(i, (i + k) % groups) for i in range(gro...]
  transfers between devices with their start and end apart: 11 -> 11, of which waited for: 3 -> 5; matrix products, arithmetic and copies ran while one was open for 2% -> 2% of each run, Pallas kernels for 23% -> 23%
where the time goes in v8:
time: 48.7 us; the launch traced here: 48.2 us
  Pallas kernels  21.2 us (44%)
  starting transfers between devices  20.1 us (41%)
  waiting for transfers between devices  4.15 us (9%)
  other arithmetic  2.35 us (5%)
    ppermute x7, starting transfers between devices, sent(): return lax.ppermute(x, 'tm', [(i, to(i)) for i in range(32)])  13.1 us
    pallas_call x1, Pallas kernels, correlate(): pl.pallas_call(functools.partial(correlate_kernel, tpb, slots), out_shape...  10.3 us
    ppermute x3, starting transfers between devices, shards(): lax.ppermute(pieces[k], 'tmpl', [(i, (i + k) % groups) for i in range(gro...  5.73 us
    pallas_call x1, Pallas kernels, gather(): pl.pallas_call(functools.partial(gather_kernel, tpb), out_shape=(pltpu.VM...  5.57 us
    pallas_call x1, Pallas kernels, energy(): pl.pallas_call(functools.partial(energy_kernel, tpb, taps), out_shape=(pl...  5.3 us
    ppermute x3, waiting for transfers between devices, shards(): lax.ppermute(pieces[k], 'tmpl', [(i, (i + k) % groups) for i in range(gro...  2.48 us
    ppermute x7, waiting for transfers between devices, sent(): return lax.ppermute(x, 'tm', [(i, to(i)) for i in range(32)])  1.67 us
    ppermute x1, starting transfers between devices, shards(): halo = lax.ppermute(heads, 'tm', [(i, i - 1) for i in range(1, 32)])  1.29 us
  transfers between devices with their start and end apart: 11, of which 5 were waited for; matrix products, arithmetic and copies ran while one was open for 2% of the time, Pallas kernels for 23%

profile of v8, /device:TPU:0, one launch (start us, length us, event | category | flops | bytes accessed | tf_op | source)
XLA Modules:
  0.0 48.2 jit_solution(4756601606550426781)
XLA Ops:
  0.0 0.0 collective-permute-start
  0.0 0.7 %broadcast_compare_fusion.1 = (pred[4]{0:T(512)(128)(4,1)S(1)}, pred[4]{0:T(512)(128)(4,1)S(1)}) fusion(s32[4]{0:T(128)} %owner.5, s32[]{:T(128)S(6)} %axis_index.25, s32[]{:T(128)S(6)} %xor.3), kind=kLoop, calls=%fused_computation.5 | loop fusion | flops 8 | bytes 32 | tf_op jit(solution)/shard_map/eq | solution.py:262
  0.7 0.1 broadcast_in_dim.52
  0.7 0.1 broadcast_in_dim.53
  0.8 0.1 broadcast_in_dim.57
  0.9 0.1 broadcast_in_dim.58
  1.0 0.5 collective-permute-done
  1.4 0.0 copy-start.1
  1.4 0.9 %fusion = bf16[192,512]{1,0:T(8,128)(2,1)S(1)} fusion(pred[192]{0:T(512)(128)(4,1)S(1)} %broadcast_in_dim.58, pred[192]{0:T(512)(128)(4,1)S(1)} %broadcast_in_dim.53, bf16[2,24,512]{2,1,0:T(8,128)(2,1)S(1)} %collective-permute-done, bf16[2,24,512]{2,1,0:T(8,128)(2,1)} %param.6), kind=kLoop, calls=%fused_computation.1 | loop fusion | flops 196608 | bytes 295296 | tf_op jit(solution)/shard_map/jit(_where)/select_n | solution.py:265
  2.4 4.2 %collective-permute-start.2 = (bf16[192,512]{1,0:T(8,128)(2,1)S(1)}, bf16[192,512]{1,0:T(8,128)(2,1)S(1)}, u32[]{:S(2)}, u32[]{:S(2)}) collective-permute-start(bf16[192,512]{1,0:T(8,128)(2,1)S(1)} %fusion), channel_id=1, source_target_pairs={{0,24},{4,100},{8,0},{12,108},{16,8},{20,116},{24,16},{28,124},{32... | collective-permute-start | bytes 589832 | tf_op jit(solution)/shard_map/ppermute | solution.py:241
  6.6 0.0 collective-permute-start.3
  6.6 1.3 %collective-permute-start.1 = (bf16[192,512]{1,0:T(8,128)(2,1)S(1)}, bf16[192,512]{1,0:T(8,128)(2,1)S(1)}, u32[]{:S(2)}, u32[]{:S(2)}) collective-permute-start(bf16[192,512]{1,0:T(8,128)(2,1)S(1)} %fusion), channel_id=1, source_target_pairs={{0,8},{4,36},{8,16},{12,44},{16,24},{20,52},{24,0},{28,60},{32,40}... | collective-permute-start | bytes 589832 | tf_op jit(solution)/shard_map/ppermute | solution.py:241
  7.9 0.0 copy-done.1
  7.9 0.0 copy-start
  7.9 0.0 copy-start.2
  7.9 5.6 %gather_rows.1 = (bf16[192,32,2,128]{3,2,1,0:T(2,128)(2,1)S(1)}, bf16[768,128]{1,0:T(8,128)(2,1)}) custom-call(s32[4]{0:T(128)} %owner.5, s32[24,64]{1,0:T(8,128)} %bitcast.18, bf16[250,32,8,128]{3,2,1,0:T(8,128)(2,1)} %bitcast.17), custom_call_target="tpu_custom_call" | custom-call | tf_op jit(solution)/shard_map/gather_rows/pallas_call | solution.py:176
  13.4 1.3 %collective-permute-start.7 = (bf16[768,128]{1,0:T(8,128)(2,1)}, bf16[768,128]{1,0:T(8,128)(2,1)S(1)}, u32[]{:S(2)}, u32[]{:S(2)}) collective-permute-start(bf16[768,128]{1,0:T(8,128)(2,1)} %get-tuple-element.14), channel_id=1, source_target_pairs={{4,0},{8,4},{12,8},{16,12},{20,16},{24,20},{28,24},{32,28},{36,32}... | collective-permute-start | bytes 589832 | tf_op jit(solution)/shard_map/ppermute | solution.py:270
  14.7 0.0 collective-permute-done.2
  14.8 0.0 collective-permute-done.3
  14.8 0.8 %collective-permute-done.1 = bf16[192,512]{1,0:T(8,128)(2,1)S(1)} collective-permute-done((bf16[192,512]{1,0:T(8,128)(2,1)S(1)}, bf16[192,512]{1,0:T(8,128)(2,1)S(1)}, u32[]{:S(2)}, u32[]{:S(2)}) %collective-permute-start.1) | collective-permute-done | bytes 196640 | tf_op jit(solution)/shard_map/ppermute | solution.py:241
  15.6 0.0 copy-done
  15.6 0.0 copy-done.2
  15.6 0.1 add_add_fusion.w0
  15.7 5.6 %collective-permute-start.6 = (bf16[192,512]{1,0:T(8,128)(2,1)S(1)}, bf16[192,512]{1,0:T(8,128)(2,1)}, u32[]{:S(2)}, u32[]{:S(2)}) collective-permute-start(bf16[192,512]{1,0:T(8,128)(2,1)S(1)} %add_add_fusion.w0), channel_id=1, source_target_pairs={{0,64},{4,20},{8,72},{12,28},{16,80},{20,4},{24,88},{28,12},{32,96... | collective-permute-start | bytes 589832 | tf_op jit(solution)/shard_map/ppermute | solution.py:241
  21.3 0.7 %collective-permute-start.5 = (bf16[192,512]{1,0:T(8,128)(2,1)S(1)}, bf16[192,512]{1,0:T(8,128)(2,1)}, u32[]{:S(2)}, u32[]{:S(2)}) collective-permute-start(bf16[192,512]{1,0:T(8,128)(2,1)S(1)} %add_add_fusion.w0), channel_id=1, source_target_pairs={{0,96},{4,28},{8,104},{12,4},{16,112},{20,12},{24,120},{28,20},{32... | collective-permute-start | bytes 589832 | tf_op jit(solution)/shard_map/ppermute | solution.py:241
  22.1 1.3 %collective-permute-start.4 = (bf16[192,512]{1,0:T(8,128)(2,1)S(1)}, bf16[192,512]{1,0:T(8,128)(2,1)}, u32[]{:S(2)}, u32[]{:S(2)}) collective-permute-start(bf16[192,512]{1,0:T(8,128)(2,1)S(1)} %add_add_fusion.w0), channel_id=1, source_target_pairs={{0,32},{4,12},{8,40},{12,20},{16,48},{20,28},{24,56},{28,4},{32,64... | collective-permute-start | bytes 589832 | tf_op jit(solution)/shard_map/ppermute | solution.py:241
  23.3 0.0 collective-permute-done.7.halo
  23.3 5.3 %window_energy.1 = (f32[192,32,128]{2,1,0:T(8,128)S(1)}, bf16[192,96,128]{2,1,0:T(8,128)(2,1)S(1)}) custom-call(s32[4]{0:T(128)} %owner.5, s32[24,64]{1,0:T(8,128)} %bitcast.19, bf16[192,64,128]{2,1,0:T(8,128)(2,1)S(1)} %bitcast.16, bf16[768,128]{1,0:T(8,128)(2,1)S(1)} %collective-permute-done.7.halo), custom_call_target="tpu_custom_call" | custom-call | tf_op jit(solution)/shard_map/window_energy/pallas_call | solution.py:197
  28.6 0.0 collective-permute-done.6.w3
  28.6 0.0 collective-permute-done.5.w2
  28.7 0.4 collective-permute-done.4.w1
  29.0 10.3 %correlate.1 = (f32[8,1024]{1,0:T(8,128)S(1)}, f32[8,1024]{1,0:T(8,128)S(1)}, f32[8,1024]{1,0:T(8,128)S(1)}, f32[8,1024]{1,0:T(8,128)S(1)}) custom-call(s32[4]{0:T(128)} %owner.5, s32[64]{0:T(128)} %counts.1, s32[1]{0:T(128)} %bitcast.place, bf16[192,512]{1,0:T(8,128)(2,1)S(1)} %add_add_fusion.w0, bf16[192,512]{1,0:T(8,128)(2,1)} %collective-permute-done.4.w1, ...), custom_call_target="tpu_custom_call" | custom-call | tf_op jit(solution)/shard_map/correlate/pallas_call | solution.py:218
  39.4 1.6 %collective-permute-start.8 = (f32[8,1024]{1,0:T(8,128)S(1)}, f32[8,1024]{1,0:T(8,128)S(1)}, u32[]{:S(2)}, u32[]{:S(2)}) collective-permute-start(f32[8,1024]{1,0:T(8,128)S(1)} %get-tuple-element.18), channel_id=1, source_target_pairs={{0,1},{1,2},{2,3},{3,0},{4,5},{5,6},{6,7},{7,4},{8,9},{9,10},{10,1... | collective-permute-start | bytes 98312 | tf_op jit(solution)/shard_map/ppermute | solution.py:277
  40.9 2.7 %collective-permute-start.9 = (f32[8,1024]{1,0:T(8,128)S(1)}, f32[8,1024]{1,0:T(8,128)S(1)}, u32[]{:S(2)}, u32[]{:S(2)}) collective-permute-start(f32[8,1024]{1,0:T(8,128)S(1)} %get-tuple-element.19), channel_id=1, source_target_pairs={{0,2},{1,3},{2,0},{3,1},{4,6},{5,7},{6,4},{7,5},{8,10},{9,11},{10,... | collective-permute-start | bytes 98312 | tf_op jit(solution)/shard_map/ppermute | solution.py:277
  43.7 1.4 %collective-permute-start.10 = (f32[8,1024]{1,0:T(8,128)S(1)}, f32[8,1024]{1,0:T(8,128)S(1)}, u32[]{:S(2)}, u32[]{:S(2)}) collective-permute-start(f32[8,1024]{1,0:T(8,128)S(1)} %get-tuple-element.20), channel_id=1, source_target_pairs={{0,3},{1,0},{2,1},{3,2},{4,7},{5,4},{6,5},{7,6},{8,11},{9,8},{10,9... | collective-permute-start | bytes 98312 | tf_op jit(solution)/shard_map/ppermute | solution.py:277
  45.1 0.0 collective-permute-done.8
  45.1 1.3 %collective-permute-done.9 = f32[8,1024]{1,0:T(8,128)S(1)} collective-permute-done((f32[8,1024]{1,0:T(8,128)S(1)}, f32[8,1024]{1,0:T(8,128)S(1)}, u32[]{:S(2)}, u32[]{:S(2)}) %collective-permute-start.9) | collective-permute-done | bytes 32800 | tf_op jit(solution)/shard_map/ppermute | solution.py:277
  46.4 1.2 %collective-permute-done.10 = f32[8,1024]{1,0:T(8,128)S(1)} collective-permute-done((f32[8,1024]{1,0:T(8,128)S(1)}, f32[8,1024]{1,0:T(8,128)S(1)}, u32[]{:S(2)}, u32[]{:S(2)}) %collective-permute-start.10) | collective-permute-done | bytes 32800 | tf_op jit(solution)/shard_map/ppermute | solution.py:277
  47.6 0.6 %add_add_fusion.1 = f32[8,1024]{1,0:T(8,128)} fusion(f32[8,1024]{1,0:T(8,128)S(1)} %collective-permute-done.9, f32[8,1024]{1,0:T(8,128)S(1)} %collective-permute-done.10, f32[8,1024]{1,0:T(8,128)S(1)} %get-tuple-element.17, f32[8,1024]{1,0:T(8,128)S(1)} %collective-permute-done.8), kind=kLoop, calls=%fused_computation.3 | loop fusion | flops 24576 | bytes 163840 | tf_op jit(solution)/shard_map/add | solution.py:278
Async XLA Ops:
  0.0 1.4 %collective-permute-start = (bf16[2,24,512]{2,1,0:T(8,128)(2,1)}, bf16[2,24,512]{2,1,0:T(8,128)(2,1)S(1)}, u32[]{:S(2)}, u32[]{:S(2)}) collective-permute-start(bf16[2,24,512]{2,1,0:T(8,128)(2,1)} %param.6), channel_id=1, source_target_pairs={{0,4},{4,0},{8,12},{12,8},{16,20},{20,16},{24,28},{28,24},{32,36},... | collective-permute-start | bytes 147464 | tf_op jit(solution)/shard_map/ppermute | solution.py:241
  1.4 6.4 %copy-start.1 = (bf16[2,24,512]{2,1,0:T(8,128)(2,1)}, bf16[2,24,512]{2,1,0:T(8,128)(2,1)S(1)}, u32[]{:S(2)}) copy-start(bf16[2,24,512]{2,1,0:T(8,128)(2,1)S(1)} %collective-permute-done) | copy-start | bytes 147460
  2.4 12.4 %collective-permute-start.2 = (bf16[192,512]{1,0:T(8,128)(2,1)S(1)}, bf16[192,512]{1,0:T(8,128)(2,1)S(1)}, u32[]{:S(2)}, u32[]{:S(2)}) collective-permute-start(bf16[192,512]{1,0:T(8,128)(2,1)S(1)} %fusion), channel_id=1, source_target_pairs={{0,24},{4,100},{8,0},{12,108},{16,8},{20,116},{24,16},{28,124},{32... | collective-permute-start | bytes 589832 | tf_op jit(solution)/shard_map/ppermute | solution.py:241
  6.6 8.2 %collective-permute-start.3 = (bf16[192,512]{1,0:T(8,128)(2,1)S(1)}, bf16[192,512]{1,0:T(8,128)(2,1)S(1)}, u32[]{:S(2)}, u32[]{:S(2)}) collective-permute-start(bf16[192,512]{1,0:T(8,128)(2,1)S(1)} %fusion), channel_id=1, source_target_pairs={{0,16},{4,68},{8,24},{12,76},{16,0},{20,84},{24,8},{28,92},{32,48}... | collective-permute-start | bytes 589832 | tf_op jit(solution)/shard_map/ppermute | solution.py:241
  6.6 9.0 %collective-permute-start.1 = (bf16[192,512]{1,0:T(8,128)(2,1)S(1)}, bf16[192,512]{1,0:T(8,128)(2,1)S(1)}, u32[]{:S(2)}, u32[]{:S(2)}) collective-permute-start(bf16[192,512]{1,0:T(8,128)(2,1)S(1)} %fusion), channel_id=1, source_target_pairs={{0,8},{4,36},{8,16},{12,44},{16,24},{20,52},{24,0},{28,60},{32,40}... | collective-permute-start | bytes 589832 | tf_op jit(solution)/shard_map/ppermute | solution.py:241
  7.9 7.7 %copy-start = (bf16[2,24,512]{2,1,0:T(8,128)(2,1)S(1)}, bf16[2,24,512]{2,1,0:T(8,128)(2,1)}, u32[]{:S(2)}) copy-start(bf16[2,24,512]{2,1,0:T(8,128)(2,1)} %param.6) | copy-start | bytes 147460
  7.9 7.7 %copy-start.2 = (bf16[2,24,512]{2,1,0:T(8,128)(2,1)S(1)}, bf16[2,24,512]{2,1,0:T(8,128)(2,1)}, u32[]{:S(2)}) copy-start(bf16[2,24,512]{2,1,0:T(8,128)(2,1)} %copy-done.1) | copy-start | bytes 147460
  13.4 9.9 %collective-permute-start.7 = (bf16[768,128]{1,0:T(8,128)(2,1)}, bf16[768,128]{1,0:T(8,128)(2,1)S(1)}, u32[]{:S(2)}, u32[]{:S(2)}) collective-permute-start(bf16[768,128]{1,0:T(8,128)(2,1)} %get-tuple-element.14), channel_id=1, source_target_pairs={{4,0},{8,4},{12,8},{16,12},{20,16},{24,20},{28,24},{32,28},{36,32}... | collective-permute-start | bytes 589832 | tf_op jit(solution)/shard_map/ppermute | solution.py:270
  15.7 12.9 %collective-permute-start.6 = (bf16[192,512]{1,0:T(8,128)(2,1)S(1)}, bf16[192,512]{1,0:T(8,128)(2,1)}, u32[]{:S(2)}, u32[]{:S(2)}) collective-permute-start(bf16[192,512]{1,0:T(8,128)(2,1)S(1)} %add_add_fusion.w0), channel_id=1, source_target_pairs={{0,64},{4,20},{8,72},{12,28},{16,80},{20,4},{24,88},{28,12},{32,96... | collective-permute-start | bytes 589832 | tf_op jit(solution)/shard_map/ppermute | solution.py:241
  21.3 7.3 %collective-permute-start.5 = (bf16[192,512]{1,0:T(8,128)(2,1)S(1)}, bf16[192,512]{1,0:T(8,128)(2,1)}, u32[]{:S(2)}, u32[]{:S(2)}) collective-permute-start(bf16[192,512]{1,0:T(8,128)(2,1)S(1)} %add_add_fusion.w0), channel_id=1, source_target_pairs={{0,96},{4,28},{8,104},{12,4},{16,112},{20,12},{24,120},{28,20},{32... | collective-permute-start | bytes 589832 | tf_op jit(solution)/shard_map/ppermute | solution.py:241
  22.1 7.0 %collective-permute-start.4 = (bf16[192,512]{1,0:T(8,128)(2,1)S(1)}, bf16[192,512]{1,0:T(8,128)(2,1)}, u32[]{:S(2)}, u32[]{:S(2)}) collective-permute-start(bf16[192,512]{1,0:T(8,128)(2,1)S(1)} %add_add_fusion.w0), channel_id=1, source_target_pairs={{0,32},{4,12},{8,40},{12,20},{16,48},{20,28},{24,56},{28,4},{32,64... | collective-permute-start | bytes 589832 | tf_op jit(solution)/shard_map/ppermute | solution.py:241
  39.4 5.7 %collective-permute-start.8 = (f32[8,1024]{1,0:T(8,128)S(1)}, f32[8,1024]{1,0:T(8,128)S(1)}, u32[]{:S(2)}, u32[]{:S(2)}) collective-permute-start(f32[8,1024]{1,0:T(8,128)S(1)} %get-tuple-element.18), channel_id=1, source_target_pairs={{0,1},{1,2},{2,3},{3,0},{4,5},{5,6},{6,7},{7,4},{8,9},{9,10},{10,1... | collective-permute-start | bytes 98312 | tf_op jit(solution)/shard_map/ppermute | solution.py:277
  40.9 5.4 %collective-permute-start.9 = (f32[8,1024]{1,0:T(8,128)S(1)}, f32[8,1024]{1,0:T(8,128)S(1)}, u32[]{:S(2)}, u32[]{:S(2)}) collective-permute-start(f32[8,1024]{1,0:T(8,128)S(1)} %get-tuple-element.19), channel_id=1, source_target_pairs={{0,2},{1,3},{2,0},{3,1},{4,6},{5,7},{6,4},{7,5},{8,10},{9,11},{10,... | collective-permute-start | bytes 98312 | tf_op jit(solution)/shard_map/ppermute | solution.py:277
  43.7 3.9 %collective-permute-start.10 = (f32[8,1024]{1,0:T(8,128)S(1)}, f32[8,1024]{1,0:T(8,128)S(1)}, u32[]{:S(2)}, u32[]{:S(2)}) collective-permute-start(f32[8,1024]{1,0:T(8,128)S(1)} %get-tuple-element.20), channel_id=1, source_target_pairs={{0,3},{1,0},{2,1},{3,2},{4,7},{5,4},{6,5},{7,6},{8,11},{9,8},{10,9... | collective-permute-start | bytes 98312 | tf_op jit(solution)/shard_map/ppermute | solution.py:277
